TPU v7x, 32 devices: a whole 2x2x4 slice. The times are simulated.
32 devices in a mesh: dp: 4 (over y, x), seq: 8 (over z, core).
Axes of the slice: x: 2, y: 2, z: 4, core: 2. Of those that a mesh axis runs over, the one named last changes fastest.
Arguments:
- layer_input: bfloat16 [2, 4, 1024, 1024], P(None, 'dp', 'seq'), may hold values from -6 to 6
- first_gain: float32 [1024], replicated, may hold values from 0.5 to 1.5
- query_weight: bfloat16 [1024, 1024], replicated, may hold values from -0.75 to 0.75
- key_weight: bfloat16 [1024, 512], replicated, may hold values from -0.75 to 0.75
- value_weight: bfloat16 [1024, 512], replicated, may hold values from -0.1875 to 0.1875
- output_weight: bfloat16 [1024, 1024], replicated, may hold values from -2 to 2
- second_gain: float32 [1024], replicated, may hold values from 0.5 to 1.5
- gate_weight: bfloat16 [16, 1024, 512], P('seq'), may hold values from -0.1875 to 0.1875
- up_weight: bfloat16 [16, 1024, 512], P('seq'), may hold values from -0.1875 to 0.1875
- down_weight: bfloat16 [16, 512, 1024], P('seq'), may hold values from -3 to 3
- expert_ids: int32 [2, 4, 1024, 8], P(None, 'dp'), may hold values from 0 to 15, all different within a row; in each aligned block of 128 rows (0 to 127, 128 to 255, ..., all dimensions but the last counted through in order) at most 128 rows name the same one
- gate_values: bfloat16 [2, 4, 1024, 8], P(None, 'dp'), may hold values from 0.059814453 to 0.19921875
- positions: int32 [2, 4, 1024], P(None, 'dp', 'seq'), may hold values from 0 to 3069, as said below
- cotangent: bfloat16 [2, 4, 1024, 1024], P(None, 'dp', 'seq'), may hold values from -6 to 6
Outputs:
- layer_output: bfloat16 [2, 4, 1024, 1024], P(None, 'dp', 'seq')
- input_grad: float32 [2, 4, 1024, 1024], P(None, 'dp', 'seq')
- first_gain_grad: float32 [1024], replicated
- query_weight_grad: float32 [1024, 1024], replicated
- key_weight_grad: float32 [1024, 512], replicated
- value_weight_grad: float32 [1024, 512], replicated
- output_weight_grad: float32 [1024, 1024], replicated
- second_gain_grad: float32 [1024], replicated
- gate_weight_grad: float32 [16, 1024, 512], P('seq')
- up_weight_grad: float32 [16, 1024, 512], P('seq')
- down_weight_grad: float32 [16, 512, 1024], P('seq')
Inputs may be any that keep to these rules, and one draw needn't show every extreme that they name: `expert_ids`: each row names 8 different experts. Within each aligned block of 128 rows (the tokens of one device), no expert is named by more than 128 rows, a bound that some block reaches. Within each sequence the positions start at 0 and rise by 1 to 3 from each token to the next; in every draw some sequence rises by 3 at every token.
All inputs are finite; a program needn't handle non-finite values.
Results may differ from a plain program's by a relative error of at most 0.02.
Values may be sent and summed in bfloat16 or wider, within the bound.
No kernel may reach another device: no remote copies, remote signals or barrier semaphores. Data moves between devices by JAX's collectives and lax.ppermute only.
A program may use at most 256 MiB of HBM per device.

v0:
```python
from functools import partial

import jax
import jax.numpy as jnp
from jax import lax
from jax.sharding import PartitionSpec as P

HEAD_DIM = 64
TOP = 8


rope_theta = 10000.0
attention_scale = 0.015625
residual_scale = 0.22
norm_eps = 1e-06
masked_score = -1e30


def rms_scale(values, norm_gain):
    return (
        values * lax.rsqrt(jnp.mean(values * values, axis=-1, keepdims=True) + norm_eps) * norm_gain
    )


def rotate(values, positions):
    half_dim = values.shape[-1] // 2
    exponent = jnp.arange(half_dim, dtype=jnp.float32) * (-2.0 / values.shape[-1])
    angles = positions.astype(jnp.float32)[:, None] * (rope_theta**exponent)[None, :]
    cosine = jnp.cos(angles)[:, None, :]
    sine_part = jnp.sin(angles)[:, None, :]
    first_half = values[..., :half_dim]
    second_half = values[..., half_dim:]
    return jnp.concatenate(
        [
            first_half * cosine - second_half * sine_part,
            second_half * cosine + first_half * sine_part,
        ],
        axis=-1,
    )


def slot_table(route_ids, route_gates, chosen, block_count, capacity):
    rows_all = route_ids.shape[0]
    per_block = rows_all // block_count
    matches = route_ids[:, None, :] == chosen[None, :, None]
    member = jnp.sum(matches.astype(jnp.int32), axis=-1, dtype=jnp.int32)
    weight_of = jnp.sum(jnp.where(matches, route_gates[:, None, :], 0.0), axis=-1)
    member = member.reshape(block_count, per_block, -1)
    rank_in = jnp.cumsum(member, axis=1, dtype=jnp.int32) - member
    slot_of = jnp.where(member > 0, rank_in, capacity)
    one_hot = slot_of[..., None] == jnp.arange(capacity, dtype=jnp.int32)
    row_number = jnp.arange(rows_all, dtype=jnp.int32).reshape(block_count, per_block)
    picked = jnp.sum(jnp.where(one_hot, row_number[:, :, None, None], 0), axis=1, dtype=jnp.int32)
    filled = jnp.any(one_hot, axis=1)
    slot_rows = jnp.where(filled, picked, rows_all)
    slot_gates = jnp.sum(
        jnp.where(one_hot, weight_of.reshape(block_count, per_block, -1)[..., None], 0.0), axis=1
    )
    return (slot_rows, slot_gates)


def swiglu(gate_pre, up_pre):
    return jax.nn.silu(gate_pre) * up_pre


def expert_forward(taken, gate_weight, up_weight, down_weight):
    gate_pre = jnp.einsum("sjmd,jdf->sjmf", taken, gate_weight, preferred_element_type=jnp.float32)
    up_pre = jnp.einsum("sjmd,jdf->sjmf", taken, up_weight, preferred_element_type=jnp.float32)
    hidden = swiglu(gate_pre, up_pre).astype(jnp.bfloat16)
    return jnp.einsum("sjmf,jfd->sjmd", hidden, down_weight, preferred_element_type=jnp.float32)


def expert_backward(taken, slot_grad, gate_weight, up_weight, down_weight):
    gate_pre = jnp.einsum("sjmd,jdf->sjmf", taken, gate_weight, preferred_element_type=jnp.float32)
    up_pre = jnp.einsum("sjmd,jdf->sjmf", taken, up_weight, preferred_element_type=jnp.float32)
    active, swiglu_back = jax.vjp(swiglu, gate_pre, up_pre)
    hidden = active.astype(jnp.bfloat16)
    hidden_grad = jnp.einsum(
        "sjmd,jfd->sjmf", slot_grad, down_weight, preferred_element_type=jnp.float32
    )
    down_term = jnp.einsum("sjmf,sjmd->jfd", hidden, slot_grad, preferred_element_type=jnp.float32)
    gate_pre_grad, up_pre_grad = swiglu_back(hidden_grad)
    gate_low = gate_pre_grad.astype(jnp.bfloat16)
    up_low = up_pre_grad.astype(jnp.bfloat16)
    gate_term = jnp.einsum("sjmd,sjmf->jdf", taken, gate_low, preferred_element_type=jnp.float32)
    up_term = jnp.einsum("sjmd,sjmf->jdf", taken, up_low, preferred_element_type=jnp.float32)
    taken_grad = jnp.einsum(
        "sjmf,jdf->sjmd", gate_low, gate_weight, preferred_element_type=jnp.float32
    )
    taken_grad = taken_grad + jnp.einsum(
        "sjmf,jdf->sjmd", up_low, up_weight, preferred_element_type=jnp.float32
    )
    return (taken_grad, gate_term, up_term, down_term)


def to_groups(token_heads, kv_heads, group_size):
    row_count = token_heads.shape[0]
    shaped = token_heads.reshape(row_count, kv_heads, group_size, -1)
    return jnp.transpose(shaped, (1, 2, 0, 3)).reshape(kv_heads, group_size * row_count, -1)


def from_groups(grouped, row_count):
    kv_heads = grouped.shape[0]
    shaped = grouped.reshape(kv_heads, -1, row_count, grouped.shape[-1])
    return jnp.transpose(shaped, (2, 0, 1, 3)).reshape(row_count, -1)


def masked_scores(query_groups, key_piece, query_index):
    scores = (
        jnp.einsum("kqd,skd->kqs", query_groups, key_piece, preferred_element_type=jnp.float32)
        * attention_scale
    )
    key_index = jnp.arange(key_piece.shape[0], dtype=jnp.int32)
    allowed = key_index[None, None, :] <= query_index[None, :, None]
    return jnp.where(allowed, scores, masked_score)


def attend_forward(state_now, shard_piece, offset, query_groups, query_index, last_row, kv_heads):
    key_piece = shard_piece[0].reshape(shard_piece[0].shape[0], kv_heads, -1)
    value_piece = shard_piece[1].reshape(shard_piece[1].shape[0], kv_heads, -1)

    def update(state_in):
        running_max, row_total, accum = state_in
        scores = masked_scores(query_groups, key_piece, query_index)
        new_max = jnp.maximum(running_max, jnp.max(scores, axis=-1))
        weights = jnp.exp(scores - new_max[..., None])
        row_total = jnp.sum(weights, axis=-1)
        accum = jnp.einsum(
            "kqs,skd->kqd",
            weights.astype(jnp.bfloat16),
            value_piece,
            preferred_element_type=jnp.float32,
        )
        return (new_max, row_total, accum)

    return lax.cond(offset <= last_row, update, lambda state_in: state_in, state_now)


def attend_backward(
    state_now,
    shard_piece,
    offset,
    query_groups,
    grad_groups,
    log_total,
    delta,
    query_index,
    last_row,
    kv_heads,
):
    key_piece = shard_piece[0].reshape(shard_piece[0].shape[0], kv_heads, -1)
    value_piece = shard_piece[1].reshape(shard_piece[1].shape[0], kv_heads, -1)
    key_count = key_piece.shape[0]

    def update(state_in):
        scores = masked_scores(query_groups, key_piece, query_index)
        probability = jnp.exp(scores - log_total[..., None])
        prob_grad = jnp.einsum(
            "kqd,skd->kqs", grad_groups, value_piece, preferred_element_type=jnp.float32
        )
        score_grad = (probability * (prob_grad - delta[..., None])).astype(jnp.bfloat16)
        query_grad = (
            jnp.einsum("kqs,skd->kqd", score_grad, key_piece, preferred_element_type=jnp.float32)
            * attention_scale
        )
        key_term = (
            jnp.einsum("kqs,kqd->skd", score_grad, query_groups, preferred_element_type=jnp.float32)
            * attention_scale
        )
        value_term = jnp.einsum(
            "kqs,kqd->skd",
            probability.astype(jnp.bfloat16),
            grad_groups,
            preferred_element_type=jnp.float32,
        )
        key_grad = key_term.reshape(key_count, -1)
        value_grad = value_term.reshape(key_count, -1)
        return (query_grad, key_grad, value_grad)

    return lax.cond(offset <= last_row, update, lambda state_in: state_in, state_now)


def body(
    layer_input,
    first_gain,
    query_weight,
    key_weight,
    value_weight,
    output_weight,
    second_gain,
    gate_weight,
    up_weight,
    down_weight,
    expert_ids,
    gate_values,
    positions,
    cotangent,
):
    micro_count = layer_input.shape[0]
    per_device = layer_input.shape[2]
    features = layer_input.shape[3]
    devices = lax.axis_size("seq")
    seq_place = lax.axis_index("seq")
    seq_length = per_device * devices
    local_experts = gate_weight.shape[0]
    capacity = 2 * per_device * TOP // (local_experts * devices)
    kv_heads = key_weight.shape[1] // HEAD_DIM
    query_heads = query_weight.shape[1] // HEAD_DIM
    group_size = query_heads // kv_heads
    query_index = seq_place * per_device + jnp.tile(
        jnp.arange(per_device, dtype=jnp.int32), group_size
    )
    last_row = seq_place * per_device + per_device - 1
    sums = [
        jnp.zeros(first_gain.shape, jnp.float32),
        jnp.zeros(query_weight.shape, jnp.float32),
        jnp.zeros(key_weight.shape, jnp.float32),
        jnp.zeros(value_weight.shape, jnp.float32),
        jnp.zeros(output_weight.shape, jnp.float32),
        jnp.zeros(second_gain.shape, jnp.float32),
        jnp.zeros(gate_weight.shape, jnp.float32),
        jnp.zeros(up_weight.shape, jnp.float32),
        jnp.zeros(down_weight.shape, jnp.float32),
    ]
    outputs_list = []
    grads_list = []
    for micro_step in range(micro_count):
        inputs_now = layer_input[micro_step, 0].astype(jnp.float32)
        cot_now = cotangent[micro_step, 0]
        pos_now = positions[micro_step, 0]
        ids_now = expert_ids[micro_step, 0]
        gates_now = gate_values[micro_step, 0].astype(jnp.float32)
        normed, first_norm_back = jax.vjp(rms_scale, inputs_now, first_gain)
        first_low = normed.astype(jnp.bfloat16)
        query_raw = jnp.dot(first_low, query_weight, preferred_element_type=jnp.float32).reshape(
            per_device, query_heads, HEAD_DIM
        )
        query_rot, query_rope_back = jax.vjp(lambda values: rotate(values, pos_now), query_raw)
        key_raw = jnp.dot(first_low, key_weight, preferred_element_type=jnp.float32).reshape(
            per_device, kv_heads, HEAD_DIM
        )
        key_rot, key_rope_back = jax.vjp(lambda values: rotate(values, pos_now), key_raw)
        key_low = key_rot.reshape(per_device, -1).astype(jnp.bfloat16)
        value_low = jnp.dot(first_low, value_weight, preferred_element_type=jnp.float32).astype(
            jnp.bfloat16
        )
        query_groups = to_groups(
            query_rot.reshape(per_device, -1).astype(jnp.bfloat16), kv_heads, group_size
        )
        initial = (
            jnp.full((kv_heads, group_size * per_device), masked_score, jnp.float32),
            jnp.zeros((kv_heads, group_size * per_device), jnp.float32),
            jnp.zeros(query_groups.shape, jnp.float32),
        )
        forward_piece = partial(
            attend_forward,
            query_groups=query_groups,
            query_index=query_index,
            last_row=last_row,
            kv_heads=kv_heads,
        )
        running_max, row_total, accum = forward_piece(
            initial,
            (
                lax.all_gather(key_low, "seq", axis=0, tiled=True),
                lax.all_gather(value_low, "seq", axis=0, tiled=True),
            ),
            jnp.int32(0),
        )
        attention_out = accum / row_total[..., None]
        log_total = running_max + jnp.log(row_total)
        mixed_low = from_groups(attention_out, per_device).astype(jnp.bfloat16)
        middle = inputs_now + residual_scale * jnp.dot(
            mixed_low, output_weight, preferred_element_type=jnp.float32
        )
        normed_two, second_norm_back = jax.vjp(rms_scale, middle, second_gain)
        second_low = normed_two.astype(jnp.bfloat16)
        gathered = lax.all_gather(second_low, "seq", axis=0, tiled=True)
        mine = seq_place * local_experts + jnp.arange(local_experts, dtype=jnp.int32)
        slot_rows, slot_gates = slot_table(ids_now, gates_now, mine, devices, capacity)
        kept_rows = jnp.take(gathered, slot_rows, axis=0, mode="fill", fill_value=0)
        produced = expert_forward(kept_rows, gate_weight, up_weight, down_weight)
        spread = (
            jnp.zeros((seq_length, features), jnp.float32)
            .at[slot_rows.reshape(-1)]
            .add((slot_gates[..., None] * produced).reshape(-1, features), mode="drop")
        )
        moe = lax.psum_scatter(
            spread.astype(jnp.bfloat16), "seq", scatter_dimension=0, tiled=True
        ).astype(jnp.float32)
        cot_all = lax.all_gather(cot_now, "seq", axis=0, tiled=True)
        picked = residual_scale * jnp.take(
            cot_all, slot_rows, axis=0, mode="fill", fill_value=0
        ).astype(jnp.float32)
        slot_grad = (slot_gates[..., None] * picked).astype(jnp.bfloat16)
        taken_grad, gate_term, up_term, down_term = expert_backward(
            kept_rows, slot_grad, gate_weight, up_weight, down_weight
        )
        spread_grad = (
            jnp.zeros((seq_length, features), jnp.float32)
            .at[slot_rows.reshape(-1)]
            .add(taken_grad.reshape(-1, features), mode="drop")
        )
        second_grad = lax.psum_scatter(
            spread_grad.astype(jnp.bfloat16), "seq", scatter_dimension=0, tiled=True
        ).astype(jnp.float32)
        outputs_list.append((middle + residual_scale * moe).astype(jnp.bfloat16))
        sums[6] = sums[6] + gate_term
        sums[7] = sums[7] + up_term
        sums[8] = sums[8] + down_term
        middle_part, second_gain_part = second_norm_back(second_grad)
        sums[5] = sums[5] + second_gain_part
        middle_grad = cot_now.astype(jnp.float32) + middle_part
        proj_low = (residual_scale * middle_grad).astype(jnp.bfloat16)
        sums[4] = sums[4] + jnp.einsum(
            "td,te->de", mixed_low, proj_low, preferred_element_type=jnp.float32
        )
        mixed_grad = jnp.einsum(
            "te,de->td", proj_low, output_weight, preferred_element_type=jnp.float32
        ).astype(jnp.bfloat16)
        grad_groups = to_groups(mixed_grad, kv_heads, group_size)
        delta = jnp.sum(grad_groups.astype(jnp.float32) * attention_out, axis=-1)
        initial_back = (
            jnp.zeros(query_groups.shape, jnp.float32),
            jnp.zeros((seq_length, key_low.shape[1]), jnp.float32),
            jnp.zeros((seq_length, value_low.shape[1]), jnp.float32),
        )
        backward_piece = partial(
            attend_backward,
            query_groups=query_groups,
            grad_groups=grad_groups,
            log_total=log_total,
            delta=delta,
            query_index=query_index,
            last_row=last_row,
            kv_heads=kv_heads,
        )
        back_state = backward_piece(
            initial_back,
            (
                lax.all_gather(key_low, "seq", axis=0, tiled=True),
                lax.all_gather(value_low, "seq", axis=0, tiled=True),
            ),
            jnp.int32(0),
        )
        query_grad, key_all_grad, value_all_grad = back_state
        key_grad, value_grad = (
            lax.psum_scatter(
                key_all_grad.astype(jnp.bfloat16), "seq", scatter_dimension=0, tiled=True
            ).astype(jnp.float32),
            lax.psum_scatter(
                value_all_grad.astype(jnp.bfloat16), "seq", scatter_dimension=0, tiled=True
            ).astype(jnp.float32),
        )
        (query_raw_grad,) = query_rope_back(
            from_groups(query_grad, per_device).reshape(per_device, query_heads, HEAD_DIM)
        )
        (key_raw_grad,) = key_rope_back(key_grad.reshape(per_device, kv_heads, HEAD_DIM))
        query_low_grad = query_raw_grad.reshape(per_device, -1).astype(jnp.bfloat16)
        key_low_grad = key_raw_grad.reshape(per_device, -1).astype(jnp.bfloat16)
        value_low_grad = value_grad.astype(jnp.bfloat16)
        sums[1] = sums[1] + jnp.einsum(
            "td,te->de", first_low, query_low_grad, preferred_element_type=jnp.float32
        )
        sums[2] = sums[2] + jnp.einsum(
            "td,te->de", first_low, key_low_grad, preferred_element_type=jnp.float32
        )
        sums[3] = sums[3] + jnp.einsum(
            "td,te->de", first_low, value_low_grad, preferred_element_type=jnp.float32
        )
        first_grad = jnp.einsum(
            "te,de->td", query_low_grad, query_weight, preferred_element_type=jnp.float32
        )
        first_grad = first_grad + jnp.einsum(
            "te,de->td", key_low_grad, key_weight, preferred_element_type=jnp.float32
        )
        first_grad = first_grad + jnp.einsum(
            "te,de->td", value_low_grad, value_weight, preferred_element_type=jnp.float32
        )
        input_part, first_gain_part = first_norm_back(first_grad)
        sums[0] = sums[0] + first_gain_part
        grads_list.append(middle_grad + input_part)
    dense = lax.psum((sums[0], sums[1], sums[2], sums[3], sums[4], sums[5]), ("dp", "seq"))
    expert = (
        lax.psum(sums[6].astype(jnp.bfloat16), "dp").astype(jnp.float32),
        lax.psum(sums[7].astype(jnp.bfloat16), "dp").astype(jnp.float32),
        lax.psum(sums[8].astype(jnp.bfloat16), "dp").astype(jnp.float32),
    )
    return (
        jnp.stack(outputs_list)[:, None],
        jnp.stack(grads_list)[:, None],
        dense[0],
        dense[1],
        dense[2],
        dense[3],
        dense[4],
        dense[5],
        expert[0],
        expert[1],
        expert[2],
    )


def solution(mesh):
    return jax.shard_map(
        body,
        mesh=mesh,
        in_specs=(
            P(None, "dp", "seq", None),
            P(),
            P(),
            P(),
            P(),
            P(),
            P(),
            P("seq", None, None),
            P("seq", None, None),
            P("seq", None, None),
            P(None, "dp", None, None),
            P(None, "dp", None, None),
            P(None, "dp", "seq"),
            P(None, "dp", "seq", None),
        ),
        out_specs=(
            P(None, "dp", "seq", None),
            P(None, "dp", "seq", None),
            P(),
            P(),
            P(),
            P(),
            P(),
            P(),
            P("seq", None, None),
            P("seq", None, None),
            P("seq", None, None),
        ),
        check_vma=False,
    )
```

profile of v0, /device:TPU:0, one launch (start us, length us, event | category | flops | bytes accessed | tf_op | source)
XLA Modules:
  0.0 1015.5 jit_solution(13612978447822827913)
XLA Ops:
  17.1 3.9 copy.245
  24.4 11.6 %all-gather.13.cloned.1.call-done = bf16[1024,512]{1,0:T(8,128)(2,1)} async-done(((bf16[128,512]{1,0:T(8,128)(2,1)}), bf16[1024,512]{1,0:T(8,128)(2,1)}) %all-gather.13.cloned.1.call-update) | async-done | bytes 1048592 | tf_op jit(solution)/shard_map/all_gather | solution.py:266
  38.3 23.5 %all-gather.11.cloned.1.call-done = bf16[1024,512]{0,1:T(8,128)(2,1)} async-done(((bf16[128,512]{0,1:T(8,128)(2,1)}), bf16[1024,512]{0,1:T(8,128)(2,1)}) %all-gather.11.cloned.1.call-update) | async-done | bytes 1048592 | tf_op jit(solution)/shard_map/all_gather | solution.py:265
  61.8 10.6 %conditional.4 = (f32[8,256]{1,0:T(8,128)}, f32[8,256]{1,0:T(8,128)}, f32[8,256,64]{1,2,0:T(8,128)S(1)}, f32[8,256]{1,0:T(8,128)S(1)}) conditional(s32[]{:T(128)} %convert_element_type.332, () %tuple.54, (s32[256]{0:T(256)S(1)}, bf16[8,256,64]{1,2,0:T(8,128)(2,1)}, bf16[1024,8,64]{0,2,1:T(8,128)(2,1)}, bf16[1024,8,64]{0,2,1:T(8,128)(2,1)}) %tuple.186), branch_computations={%region_1.0_spmd, %region_2.5_spmd} | conditional | flops 560199680 | bytes 33358908 | solution.py:136
  95.6 12.8 %gather_fusion.2 = bf16[2048,1024]{1,0:T(8,128)(2,1)} fusion(bf16[1024,1024]{1,0:T(8,128)(2,1)} %bitcast.469, s32[2048]{0:T(1024)S(1)} %broadcast_clamp_fusion.1), kind=kCustom, calls=%fused_computation.2.clone | custom fusion | bytes 8396800 | tf_op jit(solution)/shard_map/jit(_take)/gather | solution.py:292
  108.4 14.0 %all-gather.15.cloned.1.call-done = bf16[1024,1024]{1,0:T(8,128)(2,1)} async-done(((bf16[128,1024]{1,0:T(8,128)(2,1)}), bf16[1024,1024]{1,0:T(8,128)(2,1)}) %all-gather.15.cloned.1.call-update) | async-done | bytes 2097168 | tf_op jit(solution)/shard_map/all_gather | solution.py:278
  122.4 12.8 %gather_fusion = bf16[2048,1024]{1,0:T(8,128)(2,1)} fusion(bf16[1024,1024]{1,0:T(8,128)(2,1)} %all-gather.15.cloned.1.call-done, s32[2048]{0:T(1024)S(1)} %broadcast_clamp_fusion.1), kind=kCustom, calls=%fused_computation.clone | custom fusion | bytes 8396800 | tf_op jit(solution)/shard_map/jit(_take)/gather | solution.py:281
  135.2 6.2 copy.257
  141.4 5.4 fusion.57
  149.2 5.9 fusion.46
  160.6 4.2 copy.278
  164.7 21.2 %scatter_custom_fusion.2 = f32[1024,1024]{1,0:T(8,128)} fusion(s32[2048]{0:T(1024)S(1)} %bitcast.529, f32[2048,1024]{1,0:T(8,128)} %bitcast.483, f32[]{:T(128)} %constant.88.clone.1), kind=kCustom, calls=%fused_computation.148 | custom fusion | flops 2097152 | bytes 4194816 | tf_op jit(solution)/shard_map/scatter-add | solution.py:302
  195.9 10.6 %conditional.5 = (f32[8,256]{1,0:T(8,128)}, f32[8,256]{1,0:T(8,128)}, f32[8,256,64]{1,2,0:T(8,128)S(1)}, f32[8,256]{1,0:T(8,128)S(1)}) conditional(s32[]{:T(128)} %convert_element_type.332, () %tuple.56, (s32[256]{0:T(256)S(1)}, bf16[8,256,64]{1,2,0:T(8,128)(2,1)S(1)}, bf16[1024,8,64]{0,2,1:T(8,128)(2,1)}, bf16[1024,8,64]{0,2,1:T(8,128)(2,1)}) %tuple.188), branch_computations={%region_15.17_spmd, %region_16.20_spmd} | conditional | flops 560199680 | bytes 33358908 | solution.py:136
  213.9 11.4 %reduce-scatter.21.cloned.1.call-done = bf16[128,1024]{1,0:T(8,128)(2,1)} async-done(((bf16[1024,1024]{1,0:T(8,128)(2,1)}), bf16[128,1024]{1,0:T(8,128)(2,1)}) %reduce-scatter.21.cloned.1.call-update) | async-done | bytes 262160 | tf_op jit(solution)/shard_map/reduce_scatter | solution.py:304
  229.0 26.3 %all-gather.25.cloned.1.call-done = bf16[1,1,1024,1024]{3,2,1,0:T(8,128)(2,1)} async-done(((bf16[1,1,128,1024]{3,2,1,0:T(8,128)(2,1)}), bf16[1,1,1024,1024]{3,2,1,0:T(8,128)(2,1)}) %all-gather.25.cloned.1.call-update) | async-done | bytes 2097168 | tf_op jit(solution)/shard_map/all_gather | solution.py:291
  255.3 12.8 %gather_fusion.3 = bf16[2048,1024]{1,0:T(8,128)(2,1)} fusion(bf16[1024,1024]{1,0:T(8,128)(2,1)} %bitcast.470, s32[2048]{0:T(1024)S(1)} %broadcast_clamp_fusion), kind=kCustom, calls=%fused_computation.3.clone | custom fusion | bytes 8396800 | tf_op jit(solution)/shard_map/jit(_take)/gather | solution.py:292
  268.1 18.0 %all-gather.21.cloned.1.call-done = bf16[1024,1024]{1,0:T(8,128)(2,1)} async-done(((bf16[128,1024]{1,0:T(8,128)(2,1)}), bf16[1024,1024]{1,0:T(8,128)(2,1)}) %all-gather.21.cloned.1.call-update) | async-done | bytes 2097168 | tf_op jit(solution)/shard_map/all_gather | solution.py:278
  286.1 12.8 %gather_fusion.1 = bf16[2048,1024]{1,0:T(8,128)(2,1)} fusion(bf16[1024,1024]{1,0:T(8,128)(2,1)} %all-gather.21.cloned.1.call-done, s32[2048]{0:T(1024)S(1)} %broadcast_clamp_fusion), kind=kCustom, calls=%fused_computation.1.clone | custom fusion | bytes 8396800 | tf_op jit(solution)/shard_map/jit(_take)/gather | solution.py:281
  298.9 6.2 copy.271
  305.1 5.4 fusion.61
  312.9 5.7 fusion.45
  324.1 4.2 copy.285
  328.2 21.2 %scatter_custom_fusion.3 = f32[1024,1024]{1,0:T(8,128)} fusion(s32[2048]{0:T(1024)S(1)} %bitcast.531, f32[2048,1024]{1,0:T(8,128)} %bitcast.484, f32[]{:T(128)} %constant.88.clone.1), kind=kCustom, calls=%fused_computation.146 | custom fusion | flops 2097152 | bytes 4194816 | tf_op jit(solution)/shard_map/scatter-add | solution.py:302
  349.4 3.9 convert_element_type.397
  353.4 3.9 bitcast_multiply_fusion.1
  357.3 4.2 copy.260
  361.5 21.6 %scatter_custom_fusion = f32[1024,1024]{1,0:T(8,128)} fusion(s32[2048]{0:T(1024)S(1)} %bitcast.530, f32[2048,1024]{1,0:T(8,128)} %bitcast.482, f32[]{:T(128)} %constant.88.clone.1), kind=kCustom, calls=%fused_computation.152 | custom fusion | flops 2097152 | bytes 4194816 | tf_op jit(solution)/shard_map/scatter-add | solution.py:286
  383.1 3.9 convert_element_type.351
  387.0 4.0 bitcast_multiply_fusion
  391.0 4.2 copy.274
  395.2 21.2 %scatter_custom_fusion.1 = f32[1024,1024]{1,0:T(8,128)} fusion(s32[2048]{0:T(1024)S(1)} %bitcast.532, f32[2048,1024]{1,0:T(8,128)} %bitcast.481, f32[]{:T(128)} %constant.88.clone.1), kind=kCustom, calls=%fused_computation.150 | custom fusion | flops 2097152 | bytes 4194816 | tf_op jit(solution)/shard_map/scatter-add | solution.py:286
  416.4 3.9 convert_element_type.374
  425.5 36.6 %reduce-scatter.19.cloned.1.call-done = bf16[128,1024]{1,0:T(8,128)(2,1)} async-done(((bf16[1024,1024]{1,0:T(8,128)(2,1)}), bf16[128,1024]{1,0:T(8,128)(2,1)}) %reduce-scatter.19.cloned.1.call-update) | async-done | bytes 262160 | tf_op jit(solution)/shard_map/reduce_scatter | solution.py:288
  469.3 14.4 %conditional.7 = (f32[8,256,64]{1,2,0:T(8,128)}, bf16[1024,512]{0,1:T(8,128)(2,1)}, bf16[1024,512]{0,1:T(8,128)(2,1)}) conditional(s32[]{:T(128)} %convert_element_type.332, () %tuple.60, (s32[256]{0:T(256)S(1)}, bf16[8,256,64]{1,2,0:T(8,128)(2,1)S(1)}, bf16[1024,8,64]{0,2,1:T(8,128)(2,1)S(1)}, f32[8,256]{1,0:T(8,128)}, f32[8,256]{1,0:T(8,128)S(1)}, ...), branch_computations={%region_40.42_spmd, %region_41.44_spmd} | conditional | flops 1364983808 | bytes 51438672 | solution.py:180
  490.7 16.1 %conditional.6 = (f32[8,256,64]{1,2,0:T(8,128)}, bf16[1024,512]{0,1:T(8,128)(2,1)}, bf16[1024,512]{0,1:T(8,128)(2,1)}) conditional(s32[]{:T(128)} %convert_element_type.332, () %tuple.58, (s32[256]{0:T(256)S(1)}, bf16[8,256,64]{1,2,0:T(8,128)(2,1)}, bf16[1024,8,64]{0,2,1:T(8,128)(2,1)S(1)}, f32[8,256]{1,0:T(8,128)}, f32[8,256]{1,0:T(8,128)S(1)}, ...), branch_computations={%region_31.33_spmd, %region_32.35_spmd} | conditional | flops 1364983808 | bytes 50390068 | solution.py:180
  511.6 7.3 fusion.55
  519.0 3.8 fusion.56
  522.8 4.3 fusion.63
  529.8 7.9 fusion.44
  542.6 3.9 fusion.42
  563.6 19.3 %reduce-scatter.27.cloned.1.call-done = bf16[128,512]{1,0:T(8,128)(2,1)} async-done(((bf16[1024,512]{1,0:T(8,128)(2,1)}), bf16[128,512]{1,0:T(8,128)(2,1)}) %reduce-scatter.27.cloned.1.call-update) | async-done | bytes 131088
  589.1 26.4 %reduce-scatter.31.cloned.1.call-done = bf16[128,512]{1,0:T(8,128)(2,1)} async-done(((bf16[1024,512]{1,0:T(8,128)(2,1)}), bf16[128,512]{1,0:T(8,128)(2,1)}) %reduce-scatter.31.cloned.1.call-update) | async-done | bytes 131088
  622.9 4.0 fusion.203
  628.5 128.8 %all-reduce.16.cloned.1.call-done = (bf16[2,1024,512]{2,1,0:T(8,128)(2,1)}, bf16[2,1024,512]{2,1,0:T(8,128)(2,1)}, bf16[2,512,1024]{2,1,0:T(8,128)(2,1)}) async-done(((bf16[2,1024,512]{2,1,0:T(8,128)(2,1)}, bf16[2,1024,512]{2,1,0:T(8,128)(2,1)}, bf16[2,512,1024]{2,1,0:T(8,128)(2,1)}), (bf16[2,1024,512]{2,1,0:T(8,128)(2,1)}, bf16[2,1024,512]{2,1,0:T(8,128)(2,1)}, ...) | async-done | bytes 6291472 | tf_op jit(solution)/shard_map/psum | solution.py:385
  757.3 4.3 convert_element_type.408
  770.6 40.9 %all-reduce.8 = (f32[1024]{0:T(1024)}, f32[1024]{0:T(1024)}) all-reduce(f32[1024]{0:T(1024)S(1)} %add.297, f32[1024]{0:T(1024)S(1)} %copy-done.76), channel_id=1, replica_groups=mesh['dp'=4,'seq'=8] {'dp','seq'}, use_global_device_ids=true, to_apply=%region_48.50 | all-reduce | flops 2048 | bytes 16384 | tf_op jit(solution)/shard_map/psum | solution.py:383
  814.3 183.3 %all-reduce.14.cloned.1.call-done = (f32[1024,1024]{1,0:T(8,128)}, f32[1024,512]{1,0:T(8,128)}, f32[1024,512]{1,0:T(8,128)}, f32[1024,1024]{1,0:T(8,128)}) async-done(((f32[1024,1024]{1,0:T(8,128)}, f32[1024,512]{1,0:T(8,128)}, f32[1024,512]{1,0:T(8,128)}, f32[1024,1024]{1,0:T(8,128)}), (f32[1024,1024]{1,0:T(8,128)}, f32[1024,512]{1,0:T(8,128)}, f32[1024,512]{1,0:T(8,128)}, ...) | async-done | bytes 12582928 | tf_op jit(solution)/shard_map/psum | solution.py:383
  997.6 4.9 copy.407
  (379 shorter events, 207.1 us)
Async XLA Ops:
  7.2 142.0 %copy-start = (bf16[2,512,1024]{2,1,0:T(8,128)(2,1)S(1)}, bf16[2,512,1024]{2,1,0:T(8,128)(2,1)}, u32[]{:S(2)}) copy-start(bf16[2,512,1024]{2,1,0:T(8,128)(2,1)} %param.33) | copy-start | bytes 6291460
  7.2 6.5 copy-start.1
  7.2 6.5 copy-start.54
  7.2 6.2 copy-start.81
  7.2 9.0 copy-start.37
  7.2 28.8 %all-gather.13.cloned.1.call-start = ((), (), s32[]{:S(2)}) async-start(), calls=%async_computation.9 | async-start | bytes 1179648 | tf_op jit(solution)/shard_map/all_gather | solution.py:266
  8.7 70.0 %copy-start.84 = (f32[128]{0:T(128)}, f32[128]{0:T(128)S(1)}, u32[]{:S(2)}) copy-start(f32[128]{0:T(128)S(1)} %get-tuple-element.345) | copy-start | bytes 1540
  8.7 12.4 %copy-start.73 = (f32[128]{0:T(128)}, f32[128]{0:T(128)S(1)}, u32[]{:S(2)}) copy-start(f32[128]{0:T(128)S(1)} %fusion.169) | copy-start | bytes 1540
  11.1 50.7 %all-gather.11.cloned.1.call-start = ((), (), s32[]{:S(2)}) async-start(), calls=%async_computation.8 | async-start | bytes 1179648 | tf_op jit(solution)/shard_map/all_gather | solution.py:265
  13.6 9.9 copy-start.58
  13.6 9.9 copy-start.60
  13.6 179.3 %copy-start.62 = (f32[128,32]{0,1:T(8,128)}, f32[128,32]{0,1:T(8,128)S(1)}, u32[]{:S(2)}) copy-start(f32[128,32]{0,1:T(8,128)S(1)} %get-tuple-element.418) | copy-start | bytes 49156
  13.6 179.3 %copy-start.64 = (f32[128,32]{0,1:T(8,128)}, f32[128,32]{0,1:T(8,128)S(1)}, u32[]{:S(2)}) copy-start(f32[128,32]{0,1:T(8,128)S(1)} %get-tuple-element.419) | copy-start | bytes 49156
  16.2 79.4 %all-gather.23.cloned.1.call-start = ((), (), s32[]{:S(2)}) async-start(), calls=%async_computation.18 | async-start | bytes 2359296 | tf_op jit(solution)/shard_map/all_gather | solution.py:291
  17.1 105.3 %all-gather.15.cloned.1.call-start = ((), (), s32[]{:S(2)}) async-start(), calls=%async_computation.10 | async-start | bytes 2359296 | tf_op jit(solution)/shard_map/all_gather | solution.py:278
  74.8 9.0 copy-start.67
  75.5 8.5 copy-start.68
  77.7 12.1 %copy-start.86 = (f32[128]{0:T(128)}, f32[128]{0:T(128)S(1)}, u32[]{:S(2)}) copy-start(f32[128]{0:T(128)S(1)} %get-tuple-element.420) | copy-start | bytes 1540
  77.7 147.6 %copy-start.10 = (f32[128,1024]{1,0:T(8,128)}, f32[128,1024]{1,0:T(8,128)S(1)}, u32[]{:S(2)}) copy-start(f32[128,1024]{1,0:T(8,128)S(1)} %get-tuple-element.421) | copy-start | bytes 1572868
  78.6 114.6 %all-gather.19.cloned.1.call-start = ((), (), s32[]{:S(2)}) async-start(), calls=%async_computation.13 | async-start | bytes 1179648 | tf_op jit(solution)/shard_map/all_gather | solution.py:266
  78.7 111.9 %copy-start.71 = (f32[128]{0:T(128)}, f32[128]{0:T(128)S(1)}, u32[]{:S(2)}) copy-start(f32[128]{0:T(128)S(1)} %fusion.171) | copy-start | bytes 1540
  81.0 114.9 %all-gather.17.cloned.1.call-start = ((), (), s32[]{:S(2)}) async-start(), calls=%async_computation.12 | async-start | bytes 1179648 | tf_op jit(solution)/shard_map/all_gather | solution.py:265
  83.5 141.8 %reduce-scatter.21.cloned.1.call-start = ((), (), s32[]{:S(2)}) async-start(), calls=%async_computation.16 | async-start | bytes 2359296 | tf_op jit(solution)/shard_map/reduce_scatter | solution.py:304
  95.5 53.7 %copy-start.79 = (pred[8,2,128]{2,0,1:T(8,128)(4,1)}, pred[8,2,128]{2,0,1:T(8,128)(4,1)S(1)}, u32[]{:S(2)}) copy-start(pred[8,2,128]{2,0,1:T(8,128)(4,1)S(1)} %copy.256) | copy-start | bytes 6148
  95.6 53.6 %copy-start.77 = (f32[8,2,128]{2,0,1:T(8,128)}, f32[8,2,128]{2,0,1:T(8,128)S(1)}, u32[]{:S(2)}) copy-start(f32[8,2,128]{2,0,1:T(8,128)S(1)} %get-tuple-element.407) | copy-start | bytes 24580
  189.8 65.5 %all-gather.25.cloned.1.call-start = ((), (), s32[]{:S(2)}) async-start(), calls=%async_computation.19 | async-start | bytes 2359296 | tf_op jit(solution)/shard_map/all_gather | solution.py:291
  190.5 95.6 %all-gather.21.cloned.1.call-start = ((), (), s32[]{:S(2)}) async-start(), calls=%async_computation.14 | async-start | bytes 2359296 | tf_op jit(solution)/shard_map/all_gather | solution.py:278
  227.9 192.7 %reduce-scatter.23.cloned.1.call-start = ((), (), s32[]{:S(2)}) async-start(), calls=%async_computation.17 | async-start | bytes 2359296 | tf_op jit(solution)/shard_map/reduce_scatter | solution.py:304
  353.3 72.2 %reduce-scatter.17.cloned.1.call-start = ((), (), s32[]{:S(2)}) async-start(), calls=%async_computation.11 | async-start | bytes 2359296 | tf_op jit(solution)/shard_map/reduce_scatter | solution.py:288
  387.0 75.0 %reduce-scatter.19.cloned.1.call-start = ((), (), s32[]{:S(2)}) async-start(), calls=%async_computation.15 | async-start | bytes 2359296 | tf_op jit(solution)/shard_map/reduce_scatter | solution.py:288
  420.3 136.0 %reduce-scatter.29.cloned.1.call-start = ((), (), s32[]{:S(2)}) async-start(), calls=%async_computation.22 | async-start | bytes 1179648
  420.6 48.7 %copy-start.7 = (bf16[1024,512]{0,1:T(8,128)(2,1)S(1)}, bf16[1024,512]{0,1:T(8,128)(2,1)}, u32[]{:S(2)}) copy-start(bf16[1024,512]{0,1:T(8,128)(2,1)} %all-gather.17.cloned.1.call-done) | copy-start | bytes 3145732
  483.6 7.1 copy-start.6
  483.6 7.1 copy-start.70
  486.0 72.1 %reduce-scatter.25.cloned.1.call-start = ((), (), s32[]{:S(2)}) async-start(), calls=%async_computation.20 | async-start | bytes 1179648
  509.2 73.7 %reduce-scatter.27.cloned.1.call-start = ((), (), s32[]{:S(2)}) async-start(), calls=%async_computation.21 | async-start | bytes 1179648
  511.6 104.0 %reduce-scatter.31.cloned.1.call-start = ((), (), s32[]{:S(2)}) async-start(), calls=%async_computation.23 | async-start | bytes 1179648
  511.6 7.4 copy-start.22
  511.6 7.3 copy-start.44
  529.5 227.8 %all-reduce.16.cloned.1.call-start = ((), (), s32[]{:S(2)}) async-start(), calls=%async_computation.25 | async-start | bytes 12582912 | tf_op jit(solution)/shard_map/psum | solution.py:385
  529.8 7.9 copy-start.24
  529.8 7.9 copy-start.34
  529.8 7.9 copy-start.88
  546.5 451.1 %all-reduce.14.cloned.1.call-start = ((), (), s32[]{:S(2)}) async-start(), calls=%async_computation.24 | async-start | bytes 25165824 | tf_op jit(solution)/shard_map/psum | solution.py:383
  619.1 7.8 copy-start.4
  767.3 44.2 %copy-start.85 = (f32[128]{0:T(128)S(1)}, f32[128]{0:T(128)}, u32[]{:S(2)}) copy-start(f32[128]{0:T(128)} %copy-done.84) | copy-start | bytes 1540
  767.4 44.2 %copy-start.83 = (f32[128]{0:T(128)S(1)}, f32[128]{0:T(128)}, u32[]{:S(2)}) copy-start(f32[128]{0:T(128)} %copy-done.82) | copy-start | bytes 1540
  997.6 6.3 copy-start.38
  (60 other events, 179.7 us)
Sparse Core Ops, SparseCore 0:
  11.2 24.7 all-gather.12
  38.2 23.5 all-gather.10
  64.0 27.6 all-gather.22
  93.8 28.5 all-gather.14
  123.8 21.6 all-gather.18
  146.9 23.5 all-gather.16
  189.9 35.3 reduce-scatter.20
  227.5 27.7 all-gather.24
  257.5 28.5 all-gather.20
  353.4 35.3 reduce-scatter.22
  391.1 34.3 reduce-scatter.16
  427.6 34.3 reduce-scatter.18
  486.1 31.1 reduce-scatter.28
  519.4 30.5 reduce-scatter.24
  552.1 30.7 reduce-scatter.26
  585.0 30.4 reduce-scatter.30
  619.7 137.6 all-reduce.15
  764.2 233.3 all-reduce.13
where the time goes:
time: 1020 us
  waiting for transfers between devices  503 us (49%)
  matrix products  163 us (16%)
  other arithmetic  154 us (15%)
  local copies, waits for them, and re-layouts  136 us (13%)
  blocking collectives  40.9 us (4%)
  between operations  16.2 us (2%)
    psum x1, waiting for transfers between devices, body(): lax.psum((sums[0], sums[1], sums[2], sums[3], sums[4], sums[5]), ('dp', '...  183 us
    psum x1, waiting for transfers between devices, body(): lax.psum(sums[6].astype(jnp.bfloat16), 'dp').astype(jnp.float32)  129 us
    unnamed x22, waiting for transfers between devices  46.7 us
    scatter-add x2, other arithmetic, body(): spread = jnp.zeros((seq_length, features), jnp.float32).at[slot_rows.resh...  42.8 us
    scatter-add x2, other arithmetic, body(): spread_grad = jnp.zeros((seq_length, features), jnp.float32).at[slot_rows...  42.4 us
    psum x1, blocking collectives, body(): lax.psum((sums[0], sums[1], sums[2], sums[3], sums[4], sums[5]), ('dp', '...  40.9 us
    reduce_scatter x2, waiting for transfers between devices, body(): lax.psum_scatter(spread.astype(jnp.bfloat16), 'seq', scatter_dimension=0,...  39.4 us
    gather x4, local copies, waits for them, and re-layouts, body(): kept_rows = jnp.take(gathered, slot_rows, axis=0, mode='fill', fill_value=0)  38 us
  transfers between devices with their start and end apart: 18, of which 12 were waited for; matrix products, arithmetic and copies ran while one was open for 34% of the time, Pallas kernels for 0%

commit v1 on v0

v1 whole, which is shorter than its diff:
```python
from functools import partial

import jax
import jax.numpy as jnp
from jax import lax
from jax.experimental import pallas as pl
from jax.experimental.pallas import tpu as pltpu
from jax.sharding import PartitionSpec as P

HEAD_DIM = 64

rope_theta = 10000.0
attention_scale = 0.015625
residual_scale = 0.22
norm_eps = 1e-06
masked_score = -1e30

f32 = jnp.float32
bf16 = jnp.bfloat16
NT = (((1,), (1,)), ((), ()))
TN = (((0,), (0,)), ((), ()))


def dot(a, b):
    return jnp.dot(a, b, preferred_element_type=f32)


def dot_nt(a, b):
    return lax.dot_general(a, b, NT, preferred_element_type=f32)


def params(mib, *semantics):
    return pltpu.CompilerParams(
        vmem_limit_bytes=mib * 1024 * 1024, dimension_semantics=semantics or None
    )


def cost(flops, nbytes, trans=0):
    return pl.CostEstimate(
        flops=int(flops), bytes_accessed=int(nbytes), transcendentals=int(trans)
    )


def whole(shape):
    return pl.BlockSpec(shape, lambda *_: (0,) * len(shape))


def rope_tables(positions, width):
    half = HEAD_DIM // 2
    exponent = jnp.arange(half, dtype=f32) * (-2.0 / HEAD_DIM)
    angles = positions.astype(f32)[:, None] * (rope_theta**exponent)[None, :]
    cosine, sine = jnp.cos(angles), jnp.sin(angles)
    copies = width // HEAD_DIM
    cos_row = jnp.concatenate([cosine, cosine] * copies, axis=1)
    sin_row = jnp.concatenate([-sine, sine] * copies, axis=1)
    return cos_row, sin_row


def partner(values):
    width = values.shape[1]
    half = HEAD_DIM // 2
    lane = lax.broadcasted_iota(jnp.int32, values.shape, 1)
    ahead = pltpu.roll(values, width - half, 1)
    behind = pltpu.roll(values, half, 1)
    return jnp.where(lane % HEAD_DIM < half, ahead, behind)


def pre_kernel(x_ref, gain_ref, cos_ref, sin_ref, wq_ref, wk_ref, wv_ref, send_ref, low_ref, kv_ref):
    group = pl.program_id(0)
    pair = 2 * HEAD_DIM

    @pl.when(group == 0)
    def _():
        x = x_ref[...].astype(f32)
        scale = lax.rsqrt(jnp.mean(x * x, axis=-1, keepdims=True) + norm_eps)
        low = (x * scale * gain_ref[...]).astype(bf16)
        low_ref[...] = low
        keys = dot(low, wk_ref[...])
        vals = dot(low, wv_ref[...])
        for at in range(keys.shape[1] // pair):
            k = keys[:, at * pair : (at + 1) * pair]
            v = vals[:, at * pair : (at + 1) * pair]
            k = k * cos_ref[...] + partner(k) * sin_ref[...]
            lane = lax.broadcasted_iota(jnp.int32, k.shape, 1)
            first = lane < HEAD_DIM
            kv_ref[2 * at] = jnp.where(first, k, pltpu.roll(v, HEAD_DIM, 1)).astype(bf16)
            kv_ref[2 * at + 1] = jnp.where(first, pltpu.roll(k, HEAD_DIM, 1), v).astype(bf16)

    q = dot(low_ref[...], wq_ref[...])
    q = (q * cos_ref[...] + partner(q) * sin_ref[...]) * attention_scale
    send_ref[0, :, :pair] = q.astype(bf16)
    send_ref[0, :, pair:] = kv_ref[group]


def pre_call(x, gain, cos_row, sin_row, wq, wk, wv):
    rows, features = x.shape
    groups = wk.shape[1] // HEAD_DIM
    pair = wq.shape[1] // groups
    return pl.pallas_call(
        pre_kernel,
        grid=(groups,),
        in_specs=[
            whole((rows, features)),
            whole((1, features)),
            whole((rows, pair)),
            whole((rows, pair)),
            pl.BlockSpec((features, pair), lambda g: (0, g)),
            whole(wk.shape),
            whole(wv.shape),
        ],
        out_specs=[
            pl.BlockSpec((1, rows, 2 * pair), lambda g: (g, 0, 0)),
            whole((rows, features)),
        ],
        out_shape=[
            jax.ShapeDtypeStruct((groups, rows, 2 * pair), bf16),
            jax.ShapeDtypeStruct((rows, features), bf16),
        ],
        scratch_shapes=[pltpu.VMEM((groups, rows, pair), bf16)],
        compiler_params=params(40, "arbitrary"),
        cost_estimate=cost(4 * rows * features * features, 6e6),
        name="norm_qkv_rope",
    )(x, gain, cos_row, sin_row, wq, wk, wv)


def split_heads(block, first):
    wide = block.astype(f32)
    lane = lax.broadcasted_iota(jnp.int32, wide.shape, 1)
    turned = pltpu.roll(wide, HEAD_DIM, 1)
    if first:
        parts = [jnp.where(lane < HEAD_DIM, wide, 0.0), jnp.where(lane < HEAD_DIM, turned, 0.0)]
    else:
        parts = [jnp.where(lane >= HEAD_DIM, turned, 0.0), jnp.where(lane >= HEAD_DIM, wide, 0.0)]
    return jnp.concatenate(parts, axis=0).astype(bf16)


def join_heads(turned):
    rows = turned.shape[1] // 2
    return jnp.transpose(jnp.concatenate([turned[:, :rows], turned[:, rows:]], axis=0))


def scores_of(kv, q2, rows):
    scores = dot_nt(kv, q2)
    count = scores.shape[0]
    own = scores[count - rows :]
    key_at = lax.broadcasted_iota(jnp.int32, own.shape, 0)
    query_at = lax.broadcasted_iota(jnp.int32, own.shape, 1) % rows
    own = jnp.where(key_at <= query_at, own, masked_score)
    if count == rows:
        return own
    return jnp.concatenate([scores[: count - rows], own], axis=0)


def attend_kernel(qkv_ref, out_ref):
    blocks, _, rows, width = qkv_ref.shape
    pair = width // 2
    kv = qkv_ref[:, 0, :, pair:].reshape(blocks * rows, pair)
    kv_t = jnp.transpose(kv)
    for at in range(blocks):
        count = (at + 1) * rows
        q2 = split_heads(qkv_ref[at, 0, :, :pair], True)
        scores = scores_of(kv[:count], q2, rows)
        top = jnp.max(scores, axis=0, keepdims=True)
        weights = jnp.exp(scores - top)
        total = jnp.sum(weights, axis=0, keepdims=True)
        out_t = dot(kv_t[:, :count], weights.astype(bf16))
        out_ref[at, 0] = join_heads(out_t[HEAD_DIM:] / total).astype(bf16)


def attend_call(qkv):
    blocks, micro, rows, width = qkv.shape
    pair = width // 2
    length = blocks * rows
    return pl.pallas_call(
        attend_kernel,
        grid=(micro,),
        in_specs=[pl.BlockSpec((blocks, 1, rows, width), lambda m: (0, m, 0, 0))],
        out_specs=pl.BlockSpec((blocks, 1, rows, pair), lambda m: (0, m, 0, 0)),
        out_shape=jax.ShapeDtypeStruct((blocks, micro, rows, pair), bf16),
        compiler_params=params(48, "arbitrary"),
        cost_estimate=cost(
            micro * length * length * 512, 3 * qkv.size, micro * length * length
        ),
        name="attention_forward",
    )(qkv)


def attend_back_kernel(qkv_ref, grad_ref, cos_ref, sin_ref, out_ref, dkv_ref):
    blocks, _, rows, width = qkv_ref.shape
    pair = width // 2
    kv = qkv_ref[:, 0, :, pair:].reshape(blocks * rows, pair)
    kv_t = jnp.transpose(kv)
    dkv_ref[...] = jnp.zeros_like(dkv_ref)
    for at in range(blocks):
        count = (at + 1) * rows
        q2 = split_heads(qkv_ref[at, 0, :, :pair], True)
        g2 = split_heads(grad_ref[at, 0], False)
        scores = scores_of(kv[:count], q2, rows)
        top = jnp.max(scores, axis=0, keepdims=True)
        weights = jnp.exp(scores - top)
        total = jnp.sum(weights, axis=0, keepdims=True)
        prob = weights * (1.0 / total)
        prob_grad = dot_nt(kv[:count], g2)
        delta = jnp.sum(prob * prob_grad, axis=0, keepdims=True)
        score_grad = (prob * (prob_grad - delta)).astype(bf16)
        dkv_ref[:count] += dot(score_grad, q2) + dot(prob.astype(bf16), g2)
        dq_t = dot(kv_t[:, :count], score_grad)
        dq = join_heads(dq_t[:HEAD_DIM] * attention_scale)
        dq = dq * cos_ref[at, 0] - partner(dq) * sin_ref[at, 0]
        out_ref[at, 0, :, :pair] = dq.astype(bf16)
    for at in range(blocks):
        dkv = dkv_ref[at * rows : (at + 1) * rows]
        lane = lax.broadcasted_iota(jnp.int32, dkv.shape, 1)
        turned = dkv * cos_ref[at, 0] - partner(dkv) * sin_ref[at, 0]
        out_ref[at, 0, :, pair:] = jnp.where(lane < HEAD_DIM, turned, dkv).astype(bf16)


def attend_back_call(qkv, grads, cos_all, sin_all):
    blocks, micro, rows, width = qkv.shape
    pair = width // 2
    length = blocks * rows
    spec = lambda lanes: pl.BlockSpec((blocks, 1, rows, lanes), lambda m: (0, m, 0, 0))
    return pl.pallas_call(
        attend_back_kernel,
        grid=(micro,),
        in_specs=[spec(width), spec(pair), spec(pair), spec(pair)],
        out_specs=spec(width),
        out_shape=jax.ShapeDtypeStruct(qkv.shape, bf16),
        scratch_shapes=[pltpu.VMEM((length, pair), f32)],
        compiler_params=params(56, "arbitrary"),
        cost_estimate=cost(
            micro * length * length * 1280, 10 * qkv.size, micro * length * length
        ),
        name="attention_backward",
    )(qkv, grads, cos_all, sin_all)


def post_kernel(mix_ref, wo_ref, x_ref, gain_ref, mixed_ref, middle_ref, low_ref):
    mixed = jnp.concatenate([mix_ref[g] for g in range(mix_ref.shape[0])], axis=1)
    mixed_ref[...] = mixed
    middle = x_ref[...].astype(f32) + residual_scale * dot(mixed, wo_ref[...])
    middle_ref[...] = middle
    scale = lax.rsqrt(jnp.mean(middle * middle, axis=-1, keepdims=True) + norm_eps)
    low_ref[...] = (middle * scale * gain_ref[...]).astype(bf16)


def post_call(mix, wo, x, gain):
    rows, features = x.shape
    return pl.pallas_call(
        post_kernel,
        out_shape=[
            jax.ShapeDtypeStruct((rows, wo.shape[0]), bf16),
            jax.ShapeDtypeStruct((rows, features), f32),
            jax.ShapeDtypeStruct((rows, features), bf16),
        ],
        compiler_params=params(32),
        cost_estimate=cost(2 * rows * wo.size, 5e6),
        name="project_norm",
    )(mix, wo, x, gain)


def expert_kernel(x_ref, cot_ref, w_ref, wg_ref, wu_ref, wd_ref, dx_ref, h_ref, dg_ref, du_ref):
    x = x_ref[0]
    cot = residual_scale * cot_ref[0].astype(f32)
    weight = w_ref[...]
    total = None
    for e in range(wg_ref.shape[0]):
        gate = dot(x, wg_ref[e])
        up = dot(x, wu_ref[e])
        slot_grad = (weight[:, e : e + 1] * cot).astype(bf16)
        hidden_grad = dot_nt(slot_grad, wd_ref[e])
        sig = 1.0 / (1.0 + jnp.exp(-gate))
        silu = gate * sig
        h_ref[e] = (silu * up).astype(bf16)
        gate_grad = (hidden_grad * up * (sig * (1.0 + gate * (1.0 - sig)))).astype(bf16)
        up_grad = (hidden_grad * silu).astype(bf16)
        dg_ref[e] = gate_grad
        du_ref[e] = up_grad
        term = dot_nt(gate_grad, wg_ref[e]) + dot_nt(up_grad, wu_ref[e])
        total = term if total is None else total + term
    dx_ref[...] = total.astype(bf16)


def expert_call(x, cot, weight, wg, wu, wd):
    blocks, rows, features = x.shape
    count, _, hidden = wg.shape
    tokens = blocks * rows
    inner = jax.ShapeDtypeStruct((count, tokens, hidden), bf16)
    inner_spec = pl.BlockSpec((count, rows, hidden), lambda s: (0, s, 0))
    return pl.pallas_call(
        expert_kernel,
        grid=(blocks,),
        in_specs=[
            pl.BlockSpec((1, rows, features), lambda s: (s, 0, 0)),
            pl.BlockSpec((1, rows, features), lambda s: (s, 0, 0)),
            pl.BlockSpec((rows, count), lambda s: (s, 0)),
            whole(wg.shape),
            whole(wu.shape),
            whole(wd.shape),
        ],
        out_specs=[
            pl.BlockSpec((rows, features), lambda s: (s, 0)),
            inner_spec,
            inner_spec,
            inner_spec,
        ],
        out_shape=[jax.ShapeDtypeStruct((tokens, features), bf16), inner, inner, inner],
        compiler_params=params(48, "arbitrary"),
        cost_estimate=cost(10 * tokens * wg.size, 4e7, tokens * hidden * count),
        name="expert_gradients",
    )(x, cot, weight, wg, wu, wd)


def turn_kernel(sg_ref, middle_ref, gain_ref, cot_ref, wo_ref, mg_ref, proj_ref, dmid_ref, dgain_ref):
    grad = sg_ref[...].astype(f32)
    middle = middle_ref[...]
    scale = lax.rsqrt(jnp.mean(middle * middle, axis=-1, keepdims=True) + norm_eps)
    unit = middle * scale
    dgain_ref[...] = jnp.sum(grad * unit, axis=0, keepdims=True)
    w = gain_ref[...] * grad
    dmid = cot_ref[...].astype(f32) + scale * (w - unit * jnp.mean(w * unit, axis=-1, keepdims=True))
    dmid_ref[...] = dmid
    proj = (residual_scale * dmid).astype(bf16)
    proj_ref[...] = proj
    mixed_grad = dot_nt(proj, wo_ref[...]).astype(bf16)
    groups, _, pair = mg_ref.shape
    for g in range(groups):
        mg_ref[g] = mixed_grad[:, g * pair : (g + 1) * pair]


def turn_call(sg, middle, gain, cot, wo, groups):
    rows, features = middle.shape
    pair = wo.shape[0] // groups
    return pl.pallas_call(
        turn_kernel,
        out_shape=[
            jax.ShapeDtypeStruct((groups, rows, pair), bf16),
            jax.ShapeDtypeStruct((rows, features), bf16),
            jax.ShapeDtypeStruct((rows, features), f32),
            jax.ShapeDtypeStruct((1, features), f32),
        ],
        compiler_params=params(32),
        cost_estimate=cost(2 * rows * wo.size, 6e6),
        name="norm_back_project_back",
    )(sg, middle, gain, cot, wo)


def last_kernel(d_ref, wq_ref, wk_ref, wv_ref, x_ref, gain_ref, dmid_ref, out_ref):
    groups, rows, width = d_ref.shape
    pair = width // 2
    dq = jnp.concatenate([d_ref[g, :, :pair] for g in range(groups)], axis=1)
    grad = dot_nt(dq, wq_ref[...])
    keys, vals = [], []
    for at in range(groups // 2):
        a = d_ref[2 * at, :, pair:].astype(f32)
        b = d_ref[2 * at + 1, :, pair:].astype(f32)
        lane = lax.broadcasted_iota(jnp.int32, a.shape, 1)
        keys.append(jnp.where(lane < HEAD_DIM, a, pltpu.roll(b, HEAD_DIM, 1)).astype(bf16))
        vals.append(jnp.where(lane < HEAD_DIM, pltpu.roll(a, HEAD_DIM, 1), b).astype(bf16))
    grad = grad + dot_nt(jnp.concatenate(keys, axis=1), wk_ref[...])
    grad = grad + dot_nt(jnp.concatenate(vals, axis=1), wv_ref[...])
    x = x_ref[...].astype(f32)
    scale = lax.rsqrt(jnp.mean(x * x, axis=-1, keepdims=True) + norm_eps)
    unit = x * scale
    w = gain_ref[...] * grad
    out_ref[...] = dmid_ref[...] + scale * (w - unit * jnp.mean(w * unit, axis=-1, keepdims=True))


def last_call(d, wq, wk, wv, x, gain, dmid):
    rows, features = x.shape
    return pl.pallas_call(
        last_kernel,
        out_shape=jax.ShapeDtypeStruct((rows, features), f32),
        compiler_params=params(40),
        cost_estimate=cost(4 * rows * features * features, 8e6),
        name="input_gradient",
    )(d, wq, wk, wv, x, gain, dmid)


def body(
    layer_input,
    first_gain,
    query_weight,
    key_weight,
    value_weight,
    output_weight,
    second_gain,
    gate_weight,
    up_weight,
    down_weight,
    expert_ids,
    gate_values,
    positions,
    cotangent,
):
    micro, _, per_device, features = layer_input.shape
    devices = lax.axis_size("seq")
    replicas = lax.axis_size("dp")
    seq_place = lax.axis_index("seq")
    rows = micro * per_device
    local_experts = gate_weight.shape[0]
    groups = key_weight.shape[1] // HEAD_DIM
    pair = query_weight.shape[1] // groups
    copies = devices // groups

    def spread(blocks):
        if copies > 1:
            blocks = jnp.repeat(blocks, copies, axis=0)
        return lax.all_to_all(blocks, "seq", 0, 0, tiled=True)

    def unspread(blocks):
        return lax.all_to_all(blocks, "seq", 0, 0, tiled=True)[::copies]

    x = layer_input.reshape(rows, features)
    cot = cotangent.reshape(rows, features)
    gain_one = first_gain.reshape(1, features)
    gain_two = second_gain.reshape(1, features)
    pos = positions.reshape(rows)
    pos_all = lax.all_to_all(
        jnp.broadcast_to(pos[None, :], (devices, rows)), "seq", 0, 0, tiled=True
    )
    cos_row, sin_row = rope_tables(pos, pair)

    send, first_low = pre_call(
        x, gain_one, cos_row, sin_row, query_weight, key_weight, value_weight
    )
    qkv = spread(send)
    cot_all = lax.all_gather(cot, "seq", axis=0)
    qkv = qkv.reshape(devices, micro, per_device, 2 * pair)
    mix = attend_call(qkv)
    mix = unspread(mix.reshape(devices, rows, pair))
    mixed, middle, second_low = post_call(mix, output_weight, x, gain_two)
    second_all = lax.all_gather(second_low, "seq", axis=0)

    mine = seq_place * local_experts + jnp.arange(local_experts, dtype=jnp.int32)
    ids = expert_ids[:, 0]
    gates = gate_values[:, 0].astype(f32)
    routed = jnp.sum(
        jnp.where(ids[..., None] == mine, gates[..., None], 0.0), axis=2
    )
    routed = routed.reshape(micro, devices, per_device, local_experts)
    routed = jnp.transpose(routed, (1, 0, 2, 3)).reshape(devices * rows, local_experts)

    dx, hidden, gate_low, up_low = expert_call(
        second_all, cot_all, routed, gate_weight, up_weight, down_weight
    )
    second_grad = lax.psum_scatter(dx, "seq", scatter_dimension=0, tiled=True)

    tokens = second_all.reshape(devices * rows, features)
    cot_tokens = cot_all.reshape(devices * rows, features)
    slot_grad = (routed.T[..., None] * (residual_scale * cot_tokens.astype(f32))[None]).astype(bf16)
    gate_term = jnp.einsum("td,etf->edf", tokens, gate_low, preferred_element_type=f32)
    up_term = jnp.einsum("td,etf->edf", tokens, up_low, preferred_element_type=f32)
    down_term = jnp.einsum("etf,etd->efd", hidden, slot_grad, preferred_element_type=f32)
    expert_sums = lax.psum(
        (gate_term.astype(bf16), up_term.astype(bf16), down_term.astype(bf16)), "dp"
    )
    produced = jnp.einsum("etf,efd->etd", hidden, down_weight, preferred_element_type=f32)
    moe_all = jnp.sum(routed.T[..., None] * produced, axis=0).astype(bf16)
    moe = lax.psum_scatter(moe_all, "seq", scatter_dimension=0, tiled=True)
    layer_output = (middle + residual_scale * moe.astype(f32)).astype(bf16)

    mg_send, proj, middle_grad, gain_two_part = turn_call(
        second_grad, middle, gain_two, cot, output_weight, groups
    )
    mg = spread(mg_send)
    output_part = lax.dot_general(mixed, proj, TN, preferred_element_type=f32).astype(bf16)
    dense = jnp.concatenate(
        [output_part, jnp.broadcast_to(gain_two_part.astype(bf16), (16, features))], axis=0
    )
    dense = lax.psum(dense, ("dp", "seq"))
    output_weight_grad = dense[: output_part.shape[0]].astype(f32)
    second_gain_grad = dense[output_part.shape[0]].astype(f32)

    cos_all, sin_all = rope_tables(pos_all.reshape(-1), pair)
    table_shape = (devices, micro, per_device, pair)
    dqkv = attend_back_call(
        qkv,
        mg.reshape(devices, micro, per_device, pair),
        cos_all.reshape(table_shape),
        sin_all.reshape(table_shape),
    )
    d_all = dqkv.reshape(devices * rows, 2 * pair)
    first_all = lax.all_gather(first_low, "seq", axis=0).reshape(devices * rows, features)
    part = lax.dot_general(first_all, d_all, TN, preferred_element_type=f32).astype(bf16)
    part = part.reshape(replicas, features // replicas, 2 * pair)
    part = lax.all_to_all(part, "dp", 0, 0, tiled=True)
    part = jnp.sum(part.astype(f32), axis=0).astype(bf16)
    wide = lax.all_gather(part, ("dp", "seq"), axis=0)
    wide = wide.reshape(replicas, devices, features // replicas, 2 * pair)[:, ::copies].astype(f32)
    wide = jnp.transpose(wide, (0, 2, 1, 3)).reshape(features, groups, 2 * pair)
    query_weight_grad = wide[..., :pair].reshape(query_weight.shape)
    key_weight_grad = wide[..., pair : pair + HEAD_DIM].reshape(key_weight.shape)
    value_weight_grad = wide[..., pair + HEAD_DIM :].reshape(value_weight.shape)
    first_gain_grad = (
        jnp.sum(query_weight_grad * query_weight.astype(f32), axis=1)
        + jnp.sum(key_weight_grad * key_weight.astype(f32), axis=1)
        + jnp.sum(value_weight_grad * value_weight.astype(f32), axis=1)
    ) / first_gain

    back = unspread(dqkv.reshape(devices, rows, 2 * pair))
    input_grad = last_call(
        back, query_weight, key_weight, value_weight, x, gain_one, middle_grad
    )
    return (
        layer_output.reshape(layer_input.shape),
        input_grad.reshape(layer_input.shape),
        first_gain_grad,
        query_weight_grad,
        key_weight_grad,
        value_weight_grad,
        output_weight_grad,
        second_gain_grad,
        expert_sums[0].astype(f32),
        expert_sums[1].astype(f32),
        expert_sums[2].astype(f32),
    )


def solution(mesh):
    return jax.shard_map(
        body,
        mesh=mesh,
        in_specs=(
            P(None, "dp", "seq", None),
            P(),
            P(),
            P(),
            P(),
            P(),
            P(),
            P("seq", None, None),
            P("seq", None, None),
            P("seq", None, None),
            P(None, "dp", None, None),
            P(None, "dp", None, None),
            P(None, "dp", "seq"),
            P(None, "dp", "seq", None),
        ),
        out_specs=(
            P(None, "dp", "seq", None),
            P(None, "dp", "seq", None),
            P(),
            P(),
            P(),
            P(),
            P(),
            P(),
            P("seq", None, None),
            P("seq", None, None),
            P("seq", None, None),
        ),
        check_vma=False,
    )
```

time: 1020 us -> 743 us (0.73)
  matrix products: 163 us -> 37.5 us
  other arithmetic: 154 us -> 39.2 us
  waiting for transfers between devices: 503 us -> 413 us
  local copies, waits for them, and re-layouts: 136 us -> 58.9 us
  Pallas kernels: 0 us -> 60.9 us
  blocking collectives: 40.9 us -> 101 us
    dot_general x56 -> x6, matrix products: 163 us -> 37.5 us  [the longest x1 10.9 us: body(): jnp.einsum('etf,efd->etd', hidden, down_weight, preferred_element_type=f32)]
    all_to_all x0 -> x4, blocking collectives: none -> 101 us  [the longest x1 58.1 us: spread(): return lax.all_to_all(blocks, 'seq', 0, 0, tiled=True)]
    scatter-add x4 -> x0, other arithmetic: 85.2 us -> none  [the longest x2 42.8 us: body(): spread = jnp.zeros((seq_length, features), jnp.float32).at[slot_rows.resh...]
    gather x6 -> x0, local copies, waits for them, and re-layouts: 63.5 us -> none  [the longest x4 38 us: body(): kept_rows = jnp.take(gathered, slot_rows, axis=0, mode='fill', fill_value=0)]
    pallas_call x0 -> x7, Pallas kernels: none -> 60.9 us  [the longest x1 28.5 us: expert_call(): pl.pallas_call(expert_kernel, grid=(blocks,), in_specs=[pl.BlockSpec((1,...]
    psum x2, waiting for transfers between devices: 312 us -> 252 us  [the longest x1 136 us: body(): dense = lax.psum(dense, ('dp', 'seq'))]
    unnamed x22 -> x8, waiting for transfers between devices: 46.7 us -> 1.3 us
    psum x1 -> x0, blocking collectives: 40.9 us -> none  [body(): lax.psum((sums[0], sums[1], sums[2], sums[3], sums[4], sums[5]), ('dp', '...]
  transfers between devices with their start and end apart: 18 -> 10, of which waited for: 12 -> 7; matrix products, arithmetic and copies ran while one was open for 34% -> 11% of each run, Pallas kernels for 0% -> 4%
where the time goes in v1:
time: 743 us; the launch traced here: 735 us
  waiting for transfers between devices  413 us (56%)
  blocking collectives  101 us (14%)
  Pallas kernels  60.9 us (8%)
  local copies, waits for them, and re-layouts  58.9 us (8%)
  other arithmetic  39.2 us (5%)
  matrix products  37.5 us (5%)
  between operations  15.1 us (2%)
  starting transfers between devices  9.52 us (1%)
    psum x1, waiting for transfers between devices, body(): dense = lax.psum(dense, ('dp', 'seq'))  136 us
    psum x1, waiting for transfers between devices, body(): lax.psum((gate_term.astype(bf16), up_term.astype(bf16), down_term.astype(...  116 us
    all_to_all x1, blocking collectives, spread(): return lax.all_to_all(blocks, 'seq', 0, 0, tiled=True)  58.1 us
    all_gather x1, waiting for transfers between devices, body(): wide = lax.all_gather(part, ('dp', 'seq'), axis=0)  52.6 us
    all_gather x1, waiting for transfers between devices, body(): second_all = lax.all_gather(second_low, 'seq', axis=0)  44.7 us
    reduce_scatter x1, waiting for transfers between devices, body(): moe = lax.psum_scatter(moe_all, 'seq', scatter_dimension=0, tiled=True)  41.5 us
    unnamed x90, local copies, waits for them, and re-layouts  36.2 us
    pallas_call x1, Pallas kernels, expert_call(): pl.pallas_call(expert_kernel, grid=(blocks,), in_specs=[pl.BlockSpec((1,...  28.5 us
  transfers between devices with their start and end apart: 10, of which 7 were waited for; matrix products, arithmetic and copies ran while one was open for 11% of the time, Pallas kernels for 4%

profile of v1, /device:TPU:0, one launch (start us, length us, event | category | flops | bytes accessed | tf_op | source)
XLA Modules:
  0.0 735.4 jit_solution(18143931937072107893)
XLA Ops:
  9.5 1.6 copy-done
  15.2 4.5 norm_qkv_rope.1
  19.8 58.1 %all_to_all.31 = bf16[8,256,256]{2,1,0:T(8,128)(2,1)S(1)} all-to-all(bf16[8,256,256]{2,1,0:T(8,128)(2,1)S(1)} %get-tuple-element.24), channel_id=1, replica_groups=mesh['dp'=4,'seq'=8] {'seq'}, dimensions={0} | all-to-all | bytes 2097152 | tf_op jit(solution)/shard_map/all_to_all | solution.py:409
  78.0 7.8 %attention_forward.1 = bf16[8,2,128,128]{3,2,1,0:T(8,128)(2,1)S(1)} custom-call(bf16[8,2,128,256]{3,2,1,0:T(8,128)(2,1)S(1)} %bitcast.74), custom_call_target="tpu_custom_call" | custom-call | flops 1073741824 | bytes 1572864 | tf_op jit(solution)/shard_map/attention_forward/pallas_call | solution.py:174
  85.8 17.8 %all_to_all.32.mix_ref = bf16[8,256,128]{2,1,0:T(8,128)(2,1)S(1)} all-to-all(bf16[8,256,128]{2,1,0:T(8,128)(2,1)S(1)} %bitcast.76), channel_id=1, replica_groups=mesh['dp'=4,'seq'=8] {'seq'}, dimensions={0} | all-to-all | bytes 1048576 | tf_op jit(solution)/shard_map/all_to_all | solution.py:412
  106.3 1.3 copy.105
  107.6 44.7 %all-gather.10.cloned.1.call-done = bf16[2048,1024]{1,0:T(8,128)(2,1)} async-done(((bf16[256,1024]{1,0:T(8,128)(2,1)}), bf16[2048,1024]{1,0:T(8,128)(2,1)}) %all-gather.10.cloned.1.call-update) | async-done | bytes 4194320 | tf_op jit(solution)/shard_map/all_gather | solution.py:433
  153.6 1.6 copy-done.28
  155.2 1.6 copy-done.29
  156.7 28.5 %expert_gradients.1 = (bf16[2048,1024]{1,0:T(8,128)(2,1)}, bf16[2,2048,512]{2,1,0:T(8,128)(2,1)}, bf16[2,2048,512]{2,1,0:T(8,128)(2,1)}, bf16[2,2048,512]{2,1,0:T(8,128)(2,1)}) custom-call(bf16[8,256,1024]{2,1,0:T(8,128)(2,1)} %bitcast.100, bf16[8,256,1024]{2,1,0:T(8,128)(2,1)} %all-gather.8.cloned.1.call-done.cot_ref, f32[2048,2]{1,0:T(8,128)S(1)} %bitcast.71, ...), custom_call_target="tpu_custom_call" | custom-call | flops 21474836480 | bytes 40000000 | tf_op jit(solution)/shard_map/expert_gradients/pallas_call | solution.py:290
  186.4 1.6 copy.106
  187.9 7.1 convert_multiply_fusion
  195.1 5.7 convert_bitcast_fusion.1
  200.8 5.7 convert_bitcast_fusion.2
  206.5 10.7 %fusion.11 = bf16[2,512,1024]{2,1,0:T(8,128)(2,1)} fusion(bf16[2,2048,512]{2,1,0:T(8,128)(2,1)} %get-tuple-element.27, f32[2048,1024]{1,0:T(8,128)} %bitcast.86, f32[2,2048]{1,0:T(2,128)S(1)} %copy.106), kind=kOutput, calls=%fused_computation.19 | convolution fusion | flops 4304404480 | bytes 14696448 | tf_op jit(solution)/shard_map/etf,etd->efd/dot_general | solution.py:454
  217.5 10.9 %multiply_reduce_fusion = bf16[2048,1024]{1,0:T(8,128)(2,1)} fusion(f32[2,2048]{1,0:T(2,128)S(1)} %copy.106, bf16[2,2048,512]{2,1,0:T(8,128)(2,1)} %get-tuple-element.27, bf16[2,512,1024]{2,1,0:T(8,128)(2,1)} %wd_ref.1), kind=kOutput, calls=%fused_computation.1 | convolution fusion | flops 4301258752 | bytes 10502144 | tf_op jit(solution)/shard_map/etf,efd->etd/dot_general | solution.py:458
  229.0 8.0 %all_to_all.33 = s32[8,1,256]{2,1,0:T(1,128)S(1)} all-to-all(s32[8,1,256]{2,1,0:T(1,128)S(1)} %broadcast_in_dim.20), channel_id=1, replica_groups=mesh['dp'=4,'seq'=8] {'seq'}, dimensions={0} | all-to-all | bytes 16384 | tf_op jit(solution)/shard_map/all_to_all | solution.py:419
  242.9 3.5 all-to-all-start.2
  246.7 3.7 fusion.12
  250.4 3.0 pad_maximum_fusion.1
  254.2 1.5 pad_maximum_fusion
  256.1 20.1 %all-to-all-done.2 = bf16[8,256,128]{2,1,0:T(8,128)(2,1)S(1)} async-done(((bf16[8,256,128]{2,1,0:T(8,128)(2,1)}), bf16[8,256,128]{2,1,0:T(8,128)(2,1)S(1)}, u32[]{:S(2)}, u32[]{:S(2)}) %all-to-all-start.2) | async-done | bytes 524320 | tf_op jit(solution)/shard_map/all_to_all | solution.py:409
  277.0 14.4 %attention_backward.1 = bf16[8,2,128,256]{3,2,1,0:T(8,128)(2,1)} custom-call(bf16[8,2,128,256]{3,2,1,0:T(8,128)(2,1)} %bitcast.75, bf16[8,2,128,128]{3,2,1,0:T(8,128)(2,1)} %bitcast.91, f32[8,2,128,128]{3,2,1,0:T(8,128)} %get-tuple-element.118.cos_ref, f32[8,2,128,128]{3,2,1,0:T(8,128)} %get-tuple-element.119.sin_ref), custom_call_target="tpu_custom_call" | custom-call | flops 2684354560 | bytes 5242880 | tf_op jit(solution)/shard_map/attention_backward/pallas_call | solution.py:223
  292.0 3.8 convolution_convert_fusion.1
  295.8 17.6 %all_to_all.34 = bf16[4,256,256]{2,1,0:T(8,128)(2,1)S(1)} all-to-all(bf16[4,256,256]{2,1,0:T(8,128)(2,1)S(1)} %bitcast.92), channel_id=1, replica_groups=mesh['dp'=4,'seq'=8] {'dp'}, dimensions={0} | all-to-all | bytes 1048576 | tf_op jit(solution)/shard_map/all_to_all | solution.py:487
  314.2 4.5 all-to-all-start.4
  318.7 1.4 copy.109
  320.1 1.3 copy.111
  321.4 115.9 %all-reduce.6.cloned.1.call-done = (bf16[2,1024,512]{1,2,0:T(8,128)(2,1)}, bf16[2,1024,512]{1,2,0:T(8,128)(2,1)}, bf16[2,512,1024]{2,1,0:T(8,128)(2,1)}) async-done(((bf16[2,1024,512]{1,2,0:T(8,128)(2,1)}, bf16[2,1024,512]{1,2,0:T(8,128)(2,1)}, bf16[2,512,1024]{2,1,0:T(8,128)(2,1)}), (bf16[2,1024,512]{1,2,0:T(8,128)(2,1)}, bf16[2,1024,512]{1,2,0:T(8,128)(2,1)}, ...) | async-done | bytes 6291472 | tf_op jit(solution)/shard_map/psum | solution.py:455
  437.3 4.1 convert_element_type.131
  441.4 4.3 copy.119
  445.6 3.0 copy.120
  448.6 41.5 %reduce-scatter.3.cloned.1.call-done = bf16[256,1024]{1,0:T(8,128)(2,1)} async-done(((bf16[2048,1024]{1,0:T(8,128)(2,1)}), bf16[256,1024]{1,0:T(8,128)(2,1)}) %reduce-scatter.3.cloned.1.call-update) | async-done | bytes 524304 | tf_op jit(solution)/shard_map/reduce_scatter | solution.py:460
  490.1 2.3 add_convert_fusion
  492.4 136.1 %all-reduce.4.cloned.1.call-done = bf16[1040,1024]{1,0:T(8,128)(2,1)} async-done(((bf16[1040,1024]{1,0:T(8,128)(2,1)}), bf16[1040,1024]{1,0:T(8,128)(2,1)}) %all-reduce.4.cloned.1.call-update) | async-done | bytes 2129936 | tf_op jit(solution)/shard_map/psum | solution.py:471
  628.5 1.3 slice_convert_fusion.1
  629.8 4.1 slice_convert_fusion
  637.4 3.7 input_gradient.1
  641.1 52.6 %all-gather.14.cloned.1.call-done = bf16[8192,256]{1,0:T(8,128)(2,1)} async-done(((bf16[256,256]{1,0:T(8,128)(2,1)}), bf16[8192,256]{1,0:T(8,128)(2,1)}) %all-gather.14.cloned.1.call-update) | async-done | bytes 4194320 | tf_op jit(solution)/shard_map/all_gather | solution.py:489
  693.7 3.2 convert_bitcast_fusion
  696.9 4.9 copy.107
  701.8 4.7 fusion.14
  706.5 2.3 slice.20
  708.8 3.8 copy.108
  712.6 4.1 copy.110
  716.7 5.2 multiply_reduce_fusion.1
  722.3 3.0 copy.117
  725.6 1.8 copy.118
  (120 shorter events, 26.6 us)
Async XLA Ops:
  7.2 100.5 %all-gather.8.cloned.1.call-start = ((), (), s32[]{:S(2)}) async-start(), calls=%async_computation.8 | async-start | bytes 4718592 | tf_op jit(solution)/shard_map/all_gather | solution.py:428
  7.9 144.4 %all-gather.10.cloned.1.call-start = ((), (), s32[]{:S(2)}) async-start(), calls=%async_computation.12 | async-start | bytes 4718592 | tf_op jit(solution)/shard_map/all_gather | solution.py:433
  9.5 1.6 copy-start
  11.1 1.2 copy-start.2
  12.3 1.2 copy-start.4
  13.5 1.0 copy-start.8
  19.8 58.2 %copy-start.18 = (bf16[256,1024]{1,0:T(8,128)(2,1)}, bf16[256,1024]{1,0:T(8,128)(2,1)S(1)}, u32[]{:S(2)}) copy-start(bf16[256,1024]{1,0:T(8,128)(2,1)S(1)} %get-tuple-element.31) | copy-start | bytes 1572868
  19.8 83.8 %copy-start.7 = (bf16[1024,1024]{1,0:T(8,128)(2,1)S(1)}, bf16[1024,1024]{1,0:T(8,128)(2,1)}, u32[]{:S(2)}) copy-start(bf16[1024,1024]{1,0:T(8,128)(2,1)} %wo_ref.3) | copy-start | bytes 6291460
  19.8 83.8 %copy-start.9 = (bf16[2,1,128,1024]{3,2,1,0:T(8,128)(2,1)S(1)}, bf16[2,1,128,1024]{3,2,1,0:T(8,128)(2,1)}, u32[]{:S(2)}) copy-start(bf16[2,1,128,1024]{3,2,1,0:T(8,128)(2,1)} %param.14) | copy-start | bytes 1572868
  19.8 83.7 %copy-start.27 = (f32[1024]{0:T(1024)S(1)}, f32[1024]{0:T(1024)}, u32[]{:S(2)}) copy-start(f32[1024]{0:T(1024)} %param.20) | copy-start | bytes 12292
  77.9 7.8 %copy-start.16 = (bf16[8,256,256]{2,1,0:T(8,128)(2,1)}, bf16[8,256,256]{2,1,0:T(8,128)(2,1)S(1)}, u32[]{:S(2)}) copy-start(bf16[8,256,256]{2,1,0:T(8,128)(2,1)S(1)} %all_to_all.31) | copy-start | bytes 3145732
  78.0 28.2 %copy-start.37 = (bf16[2,1,1024,8]{2,3,1,0:T(8,128)(2,1)S(1)}, bf16[2,1,1024,8]{2,3,1,0:T(8,128)(2,1)}, u32[]{:S(2)}) copy-start(bf16[2,1,1024,8]{2,3,1,0:T(8,128)(2,1)} %param.25) | copy-start | bytes 98308
  78.0 28.2 %copy-start.36 = (s32[2,1,1024,8]{2,3,1,0:T(8,128)S(1)}, s32[2,1,1024,8]{2,3,1,0:T(8,128)}, u32[]{:S(2)}) copy-start(s32[2,1,1024,8]{2,3,1,0:T(8,128)} %param.24) | copy-start | bytes 196612
  104.4 0.8 copy-start.20
  106.0 131.0 %copy-start.11 = (f32[256,1024]{1,0:T(8,128)}, f32[256,1024]{1,0:T(8,128)S(1)}, u32[]{:S(2)}) copy-start(f32[256,1024]{1,0:T(8,128)S(1)} %get-tuple-element.25.middle_ref) | copy-start | bytes 3145732
  106.0 131.0 %reduce-scatter.5.cloned.1.call-start = ((), (), s32[]{:S(2)}) async-start(), calls=%async_computation.10 | async-start | bytes 4718592 | tf_op jit(solution)/shard_map/reduce_scatter | solution.py:447
  152.3 1.2 copy-start.12
  153.6 1.6 copy-start.28
  155.2 1.6 copy-start.29
  185.2 106.8 %all-gather.12.cloned.1.call-start = ((), (), s32[]{:S(2)}) async-start(), calls=%async_computation.13 | async-start | bytes 4718592 | tf_op jit(solution)/shard_map/all_gather | solution.py:484
  185.8 251.5 %all-reduce.6.cloned.1.call-start = ((), (), s32[]{:S(2)}) async-start(), calls=%async_computation.15 | async-start | bytes 12582912 | tf_op jit(solution)/shard_map/psum | solution.py:455
  187.9 7.1 copy-start.39
  187.9 7.1 copy-start.41
  195.1 5.7 copy-start.40
  217.2 272.8 %reduce-scatter.3.cloned.1.call-start = ((), (), s32[]{:S(2)}) async-start(), calls=%async_computation.9 | async-start | bytes 4718592 | tf_op jit(solution)/shard_map/reduce_scatter | solution.py:460
  237.0 1.0 copy-start.13
  238.1 1.0 copy-start.17
  240.3 1.0 copy-start.14
  242.1 0.8 copy-start.23
  242.9 33.3 %all-to-all-start.2 = ((bf16[8,256,128]{2,1,0:T(8,128)(2,1)}), bf16[8,256,128]{2,1,0:T(8,128)(2,1)S(1)}, u32[]{:S(2)}, u32[]{:S(2)}) async-start(bf16[8,256,128]{2,1,0:T(8,128)(2,1)} %copy-done.19), calls=%async_computation.4 | async-start | bytes 1048576 | tf_op jit(solution)/shard_map/all_to_all | solution.py:409
  246.4 382.1 %all-reduce.4.cloned.1.call-start = ((), (), s32[]{:S(2)}) async-start(), calls=%async_computation.11 | async-start | bytes 4259840 | tf_op jit(solution)/shard_map/psum | solution.py:471
  246.7 6.8 copy-start.22
  246.7 6.8 copy-start.24
  255.8 437.9 %all-gather.14.cloned.1.call-start = ((), (), s32[]{:S(2)}) async-start(), calls=%async_computation.14 | async-start | bytes 4325376 | tf_op jit(solution)/shard_map/all_gather | solution.py:489
  276.2 0.8 copy-start.35
  295.8 22.9 %copy-start.3 = (bf16[1024,512]{1,0:T(8,128)(2,1)S(1)}, bf16[1024,512]{1,0:T(8,128)(2,1)}, u32[]{:S(2)}) copy-start(bf16[1024,512]{1,0:T(8,128)(2,1)} %wk_ref.3) | copy-start | bytes 3145732
  295.8 24.3 %copy-start.5 = (bf16[1024,512]{1,0:T(8,128)(2,1)S(1)}, bf16[1024,512]{1,0:T(8,128)(2,1)}, u32[]{:S(2)}) copy-start(bf16[1024,512]{1,0:T(8,128)(2,1)} %wv_ref.3) | copy-start | bytes 3145732
  314.2 319.7 %all-to-all-start.4 = ((bf16[8,256,256]{2,1,0:T(8,128)(2,1)}), bf16[8,256,256]{2,1,0:T(8,128)(2,1)}, u32[]{:S(2)}, u32[]{:S(2)}) async-start(bf16[8,256,256]{2,1,0:T(8,128)(2,1)} %bitcast.90), calls=%async_computation.6 | async-start | bytes 2097152 | tf_op jit(solution)/shard_map/all_to_all | solution.py:412
  441.4 4.3 copy-start.34
  448.6 185.3 %copy-start.1 = (bf16[1024,1024]{1,0:T(8,128)(2,1)S(1)}, bf16[1024,1024]{1,0:T(8,128)(2,1)}, u32[]{:S(2)}) copy-start(bf16[1024,1024]{1,0:T(8,128)(2,1)} %wq_ref.3) | copy-start | bytes 6291460
  448.6 185.3 %copy-start.26 = (f32[1024]{0:T(1024)S(1)}, f32[1024]{0:T(1024)}, u32[]{:S(2)}) copy-start(f32[1024]{0:T(1024)} %param.15) | copy-start | bytes 12292
  633.9 1.2 copy-start.6
  635.1 1.0 copy-start.10
  636.2 1.2 copy-start.15
  716.7 5.2 copy-start.31
  716.7 5.2 copy-start.33
  722.0 3.3 copy-start.30
  722.0 3.3 copy-start.32
  (4 other events, 3.0 us)
Sparse Core Ops, SparseCore 0:
  9.6 72.0 all-gather.7
  106.2 46.1 all-gather.9
  185.3 48.7 reduce-scatter.4
  235.6 56.4 all-gather.11
  296.7 140.5 all-reduce.5
  440.0 50.0 reduce-scatter.2
  496.2 132.2 all-reduce.3
  632.0 61.6 all-gather.13

commit v2 on v1

--- a/solution.py
+++ b/solution.py
@@ -65,62 +65,56 @@
     return jnp.where(lane % HEAD_DIM < half, ahead, behind)
 
 
-def pre_kernel(x_ref, gain_ref, cos_ref, sin_ref, wq_ref, wk_ref, wv_ref, send_ref, low_ref, kv_ref):
-    group = pl.program_id(0)
+def qkv_kernel(place_ref, x_ref, gain_ref, cos_ref, sin_ref, wq_ref, wk_ref, wv_ref, qkv_ref, low_ref):
     pair = 2 * HEAD_DIM
-
-    @pl.when(group == 0)
-    def _():
-        x = x_ref[...].astype(f32)
-        scale = lax.rsqrt(jnp.mean(x * x, axis=-1, keepdims=True) + norm_eps)
-        low = (x * scale * gain_ref[...]).astype(bf16)
-        low_ref[...] = low
-        keys = dot(low, wk_ref[...])
-        vals = dot(low, wv_ref[...])
-        for at in range(keys.shape[1] // pair):
-            k = keys[:, at * pair : (at + 1) * pair]
-            v = vals[:, at * pair : (at + 1) * pair]
-            k = k * cos_ref[...] + partner(k) * sin_ref[...]
-            lane = lax.broadcasted_iota(jnp.int32, k.shape, 1)
-            first = lane < HEAD_DIM
-            kv_ref[2 * at] = jnp.where(first, k, pltpu.roll(v, HEAD_DIM, 1)).astype(bf16)
-            kv_ref[2 * at + 1] = jnp.where(first, pltpu.roll(k, HEAD_DIM, 1), v).astype(bf16)
-
-    q = dot(low_ref[...], wq_ref[...])
-    q = (q * cos_ref[...] + partner(q) * sin_ref[...]) * attention_scale
-    send_ref[0, :, :pair] = q.astype(bf16)
-    send_ref[0, :, pair:] = kv_ref[group]
-
-
-def pre_call(x, gain, cos_row, sin_row, wq, wk, wv):
-    rows, features = x.shape
-    groups = wk.shape[1] // HEAD_DIM
-    pair = wq.shape[1] // groups
-    return pl.pallas_call(
-        pre_kernel,
-        grid=(groups,),
-        in_specs=[
-            whole((rows, features)),
-            whole((1, features)),
-            whole((rows, pair)),
-            whole((rows, pair)),
-            pl.BlockSpec((features, pair), lambda g: (0, g)),
-            whole(wk.shape),
-            whole(wv.shape),
-        ],
-        out_specs=[
-            pl.BlockSpec((1, rows, 2 * pair), lambda g: (g, 0, 0)),
-            whole((rows, features)),
-        ],
+    x = x_ref[0].astype(f32)
+    scale = lax.rsqrt(jnp.mean(x * x, axis=-1, keepdims=True) + norm_eps)
+    low = (x * scale * gain_ref[...]).astype(bf16)
+    low_ref[0] = low
+    cosine, sine = cos_ref[...], sin_ref[...]
+    q = dot(low, wq_ref[...])
+    q = (q * cosine + partner(q) * sine) * attention_scale
+    qkv_ref[0, :, :pair] = q.astype(bf16)
+    k = dot(low, wk_ref[...])
+    v = dot(low, wv_ref[...])
+    second = place_ref[0] % 2
+    k = k * cosine + partner(k) * sine
+    k = jnp.where(second == 0, k, pltpu.roll(k, HEAD_DIM, 1))
+    v = jnp.where(second == 0, pltpu.roll(v, HEAD_DIM, 1), v)
+    lane = lax.broadcasted_iota(jnp.int32, k.shape, 1)
+    qkv_ref[0, :, pair:] = jnp.where(lane < HEAD_DIM, k, v).astype(bf16)
+
+
+def qkv_call(group, x_all, gain, cos_all, sin_all, wq, wk, wv):
+    blocks, rows, features = x_all.shape
+    pair = 2 * HEAD_DIM
+    return pl.pallas_call(
+        qkv_kernel,
+        grid_spec=pltpu.PrefetchScalarGridSpec(
+            num_scalar_prefetch=1,
+            grid=(blocks,),
+            in_specs=[
+                pl.BlockSpec((1, rows, features), lambda s, place: (s, 0, 0)),
+                pl.BlockSpec((1, features), lambda s, place: (0, 0)),
+                pl.BlockSpec((rows, pair), lambda s, place: (s, 0)),
+                pl.BlockSpec((rows, pair), lambda s, place: (s, 0)),
+                pl.BlockSpec((features, pair), lambda s, place: (0, place[0])),
+                pl.BlockSpec((features, pair), lambda s, place: (0, place[0] // 2)),
+                pl.BlockSpec((features, pair), lambda s, place: (0, place[0] // 2)),
+            ],
+            out_specs=[
+                pl.BlockSpec((1, rows, 2 * pair), lambda s, place: (s, 0, 0)),
+                pl.BlockSpec((1, rows, features), lambda s, place: (s, 0, 0)),
+            ],
+        ),
         out_shape=[
-            jax.ShapeDtypeStruct((groups, rows, 2 * pair), bf16),
-            jax.ShapeDtypeStruct((rows, features), bf16),
-        ],
-        scratch_shapes=[pltpu.VMEM((groups, rows, pair), bf16)],
-        compiler_params=params(40, "arbitrary"),
-        cost_estimate=cost(4 * rows * features * features, 6e6),
+            jax.ShapeDtypeStruct((blocks, rows, 2 * pair), bf16),
+            jax.ShapeDtypeStruct((blocks, rows, features), bf16),
+        ],
+        compiler_params=params(32, "arbitrary"),
+        cost_estimate=cost(6 * blocks * rows * features * pair, 14e6),
         name="norm_qkv_rope",
-    )(x, gain, cos_row, sin_row, wq, wk, wv)
+    )(group, x_all, gain, cos_all, sin_all, wq, wk, wv)
 
 
 def split_heads(block, first):
@@ -259,7 +253,9 @@
     )(mix, wo, x, gain)
 
 
-def expert_kernel(x_ref, cot_ref, w_ref, wg_ref, wu_ref, wd_ref, dx_ref, h_ref, dg_ref, du_ref):
+def expert_kernel(
+    x_ref, cot_ref, w_ref, wg_ref, wu_ref, wd_ref, dx_ref, h_ref, dg_ref, du_ref, sg_ref
+):
     x = x_ref[0]
     cot = residual_scale * cot_ref[0].astype(f32)
     weight = w_ref[...]
@@ -268,6 +264,7 @@
         gate = dot(x, wg_ref[e])
         up = dot(x, wu_ref[e])
         slot_grad = (weight[:, e : e + 1] * cot).astype(bf16)
+        sg_ref[e] = slot_grad
         hidden_grad = dot_nt(slot_grad, wd_ref[e])
         sig = 1.0 / (1.0 + jnp.exp(-gate))
         silu = gate * sig
@@ -303,12 +300,48 @@
             inner_spec,
             inner_spec,
             inner_spec,
-        ],
-        out_shape=[jax.ShapeDtypeStruct((tokens, features), bf16), inner, inner, inner],
+            pl.BlockSpec((count, rows, features), lambda s: (0, s, 0)),
+        ],
+        out_shape=[
+            jax.ShapeDtypeStruct((tokens, features), bf16),
+            inner,
+            inner,
+            inner,
+            jax.ShapeDtypeStruct((count, tokens, features), bf16),
+        ],
         compiler_params=params(48, "arbitrary"),
         cost_estimate=cost(10 * tokens * wg.size, 4e7, tokens * hidden * count),
         name="expert_gradients",
     )(x, cot, weight, wg, wu, wd)
+
+
+def moe_kernel(h_ref, w_ref, wd_ref, out_ref):
+    weight = w_ref[...]
+    total = None
+    for e in range(wd_ref.shape[0]):
+        term = weight[:, e : e + 1] * dot(h_ref[e], wd_ref[e])
+        total = term if total is None else total + term
+    out_ref[...] = total.astype(bf16)
+
+
+def moe_call(hidden, weight, wd):
+    count, tokens, inner = hidden.shape
+    features = wd.shape[2]
+    rows = 256
+    return pl.pallas_call(
+        moe_kernel,
+        grid=(tokens // rows,),
+        in_specs=[
+            pl.BlockSpec((count, rows, inner), lambda s: (0, s, 0)),
+            pl.BlockSpec((rows, count), lambda s: (s, 0)),
+            whole(wd.shape),
+        ],
+        out_specs=pl.BlockSpec((rows, features), lambda s: (s, 0)),
+        out_shape=jax.ShapeDtypeStruct((tokens, features), bf16),
+        compiler_params=params(32, "arbitrary"),
+        cost_estimate=cost(2 * tokens * wd.size, 1.1e7),
+        name="expert_outputs",
+    )(hidden, weight, wd)
 
 
 def turn_kernel(sg_ref, middle_ref, gain_ref, cot_ref, wo_ref, mg_ref, proj_ref, dmid_ref, dgain_ref):
@@ -343,6 +376,92 @@
         cost_estimate=cost(2 * rows * wo.size, 6e6),
         name="norm_back_project_back",
     )(sg, middle, gain, cot, wo)
+
+
+def output_weight_kernel(mixed_ref, proj_ref, dgain_ref, out_ref):
+    held, each, features = out_ref.shape
+    rows = mixed_ref.shape[1] // held
+    part = lax.dot_general(mixed_ref[...], proj_ref[...], TN, preferred_element_type=f32)
+    extra = jnp.broadcast_to(dgain_ref[...], (each - rows, features)).astype(bf16)
+    for at in range(held):
+        out_ref[at, :rows] = part[at * rows : (at + 1) * rows].astype(bf16)
+        out_ref[at, rows:] = extra
+
+
+def output_weight_call(mixed, proj, dgain, parts):
+    rows, width = mixed.shape
+    features = proj.shape[1]
+    each = width // parts
+    lanes = max(each, 2 * HEAD_DIM)
+    held = lanes // each
+    return pl.pallas_call(
+        output_weight_kernel,
+        grid=(parts // held,),
+        in_specs=[
+            pl.BlockSpec((rows, lanes), lambda s: (0, s)),
+            whole((rows, features)),
+            whole((1, features)),
+        ],
+        out_specs=pl.BlockSpec((held, each + 16, features), lambda s: (s, 0, 0)),
+        out_shape=jax.ShapeDtypeStruct((parts, each + 16, features), bf16),
+        compiler_params=params(32, "arbitrary"),
+        cost_estimate=cost(2 * rows * width * features, 4e6),
+        name="output_weight_part",
+    )(mixed, proj, dgain)
+
+
+def weights_out_kernel(wide_ref, wq_ref, wk_ref, wv_ref, gain_ref, dq_ref, dk_ref, dv_ref, dg_ref):
+    groups, rows, width = wide_ref.shape
+    pair = width // 2
+    total = jnp.zeros((rows, pair), f32)
+    for g in range(groups):
+        part = wide_ref[g, :, :pair].astype(f32)
+        at = slice(g * pair, (g + 1) * pair)
+        dq_ref[:, at] = part
+        total += part * wq_ref[:, at].astype(f32)
+    for g in range(groups // 2):
+        a = wide_ref[2 * g, :, pair:].astype(f32)
+        b = wide_ref[2 * g + 1, :, pair:].astype(f32)
+        lane = lax.broadcasted_iota(jnp.int32, a.shape, 1)
+        at = slice(g * pair, (g + 1) * pair)
+        k = jnp.where(lane < HEAD_DIM, a, pltpu.roll(b, HEAD_DIM, 1))
+        v = jnp.where(lane < HEAD_DIM, pltpu.roll(a, HEAD_DIM, 1), b)
+        dk_ref[:, at] = k
+        dv_ref[:, at] = v
+        total += k * wk_ref[:, at].astype(f32) + v * wv_ref[:, at].astype(f32)
+    dg_ref[...] = jnp.sum(jnp.transpose(total), axis=0, keepdims=True) / gain_ref[...]
+
+
+def weights_out_call(wide, wq, wk, wv, gain):
+    chunks, groups, rows, width = wide.shape
+    features = chunks * rows
+    by_rows = lambda w: pl.BlockSpec((rows, w.shape[1]), lambda c: (c, 0))
+    return pl.pallas_call(
+        weights_out_kernel,
+        grid=(chunks,),
+        in_specs=[
+            pl.BlockSpec((None, groups, rows, width), lambda c: (c, 0, 0, 0)),
+            by_rows(wq),
+            by_rows(wk),
+            by_rows(wv),
+            pl.BlockSpec((1, rows), lambda c: (0, c)),
+        ],
+        out_specs=[
+            by_rows(wq),
+            by_rows(wk),
+            by_rows(wv),
+            pl.BlockSpec((1, rows), lambda c: (0, c)),
+        ],
+        out_shape=[
+            jax.ShapeDtypeStruct(wq.shape, f32),
+            jax.ShapeDtypeStruct(wk.shape, f32),
+            jax.ShapeDtypeStruct(wv.shape, f32),
+            jax.ShapeDtypeStruct((1, features), f32),
+        ],
+        compiler_params=params(32, "arbitrary"),
+        cost_estimate=cost(2 * wq.size, 1.6e7),
+        name="attention_weights_out",
+    )(wide, wq, wk, wv, gain)
 
 
 def last_kernel(d_ref, wq_ref, wk_ref, wv_ref, x_ref, gain_ref, dmid_ref, out_ref):
@@ -375,6 +494,36 @@
         cost_estimate=cost(4 * rows * features * features, 8e6),
         name="input_gradient",
     )(d, wq, wk, wv, x, gain, dmid)
+
+
+def swap(values, axis, bit):
+    return lax.ppermute(values, axis, [(i, i ^ bit) for i in range(lax.axis_size(axis))])
+
+
+def half_sum(values, axis, bit):
+    half = values.shape[0] // 2
+    upper = (lax.axis_index(axis) & bit) > 0
+    low, high = values[:half], values[half:]
+    came = swap(jnp.where(upper, low, high), axis, bit)
+    return (jnp.where(upper, high, low).astype(f32) + came.astype(f32)).astype(bf16)
+
+
+def join_halves(values, axis, bit):
+    came = swap(values, axis, bit)
+    upper = (lax.axis_index(axis) & bit) > 0
+    return jnp.concatenate(
+        [jnp.where(upper, came, values), jnp.where(upper, values, came)], axis=0
+    )
+
+
+def sum_over(values, axis, bits):
+    shape = values.shape
+    values = values.reshape(-1, shape[-1])
+    for bit in bits:
+        values = half_sum(values, axis, bit)
+    for bit in bits[::-1]:
+        values = join_halves(values, axis, bit)
+    return values.reshape(shape)
 
 
 def body(
@@ -403,6 +552,8 @@
     pair = query_weight.shape[1] // groups
     copies = devices // groups
 
+    dp_bits = [1 << i for i in range(replicas.bit_length() - 1)]
+
     def spread(blocks):
         if copies > 1:
             blocks = jnp.repeat(blocks, copies, axis=0)
@@ -415,17 +566,18 @@
     cot = cotangent.reshape(rows, features)
     gain_one = first_gain.reshape(1, features)
     gain_two = second_gain.reshape(1, features)
-    pos = positions.reshape(rows)
+    x_all = lax.all_gather(x, "seq", axis=0)
     pos_all = lax.all_to_all(
-        jnp.broadcast_to(pos[None, :], (devices, rows)), "seq", 0, 0, tiled=True
-    )
-    cos_row, sin_row = rope_tables(pos, pair)
-
-    send, first_low = pre_call(
-        x, gain_one, cos_row, sin_row, query_weight, key_weight, value_weight
-    )
-    qkv = spread(send)
-    cot_all = lax.all_gather(cot, "seq", axis=0)
+        jnp.broadcast_to(positions.reshape(1, rows), (devices, rows)), "seq", 0, 0, tiled=True
+    )
+    cos_all, sin_all = rope_tables(pos_all.reshape(-1), pair)
+    x_all, cot_then = lax.optimization_barrier((x_all, cot))
+    cot_all = lax.all_gather(cot_then, "seq", axis=0)
+
+    group = (seq_place // copies).astype(jnp.int32).reshape(1)
+    qkv, first_all = qkv_call(
+        group, x_all, gain_one, cos_all, sin_all, query_weight, key_weight, value_weight
+    )
     qkv = qkv.reshape(devices, micro, per_device, 2 * pair)
     mix = attend_call(qkv)
     mix = unspread(mix.reshape(devices, rows, pair))
@@ -441,38 +593,44 @@
     routed = routed.reshape(micro, devices, per_device, local_experts)
     routed = jnp.transpose(routed, (1, 0, 2, 3)).reshape(devices * rows, local_experts)
 
-    dx, hidden, gate_low, up_low = expert_call(
+    dx, hidden, gate_low, up_low, slot_grad = expert_call(
         second_all, cot_all, routed, gate_weight, up_weight, down_weight
     )
     second_grad = lax.psum_scatter(dx, "seq", scatter_dimension=0, tiled=True)
 
     tokens = second_all.reshape(devices * rows, features)
-    cot_tokens = cot_all.reshape(devices * rows, features)
-    slot_grad = (routed.T[..., None] * (residual_scale * cot_tokens.astype(f32))[None]).astype(bf16)
     gate_term = jnp.einsum("td,etf->edf", tokens, gate_low, preferred_element_type=f32)
     up_term = jnp.einsum("td,etf->edf", tokens, up_low, preferred_element_type=f32)
     down_term = jnp.einsum("etf,etd->efd", hidden, slot_grad, preferred_element_type=f32)
-    expert_sums = lax.psum(
-        (gate_term.astype(bf16), up_term.astype(bf16), down_term.astype(bf16)), "dp"
-    )
-    produced = jnp.einsum("etf,efd->etd", hidden, down_weight, preferred_element_type=f32)
-    moe_all = jnp.sum(routed.T[..., None] * produced, axis=0).astype(bf16)
+    moe_all = moe_call(hidden, routed, down_weight)
+    gate_sum = sum_over(gate_term.astype(bf16), "dp", dp_bits)
+    up_sum = sum_over(up_term.astype(bf16), "dp", dp_bits[::-1])
+    down_low = down_term.astype(bf16)
+    cut = local_experts // 2
+    down_sum = jnp.concatenate(
+        [
+            sum_over(down_low[:cut], "dp", dp_bits),
+            sum_over(down_low[cut:], "dp", dp_bits[::-1]),
+        ],
+        axis=0,
+    )
+
+    mg_send, proj, middle_grad, gain_two_part = turn_call(
+        second_grad, middle, gain_two, cot, output_weight, groups
+    )
+    mg = spread(mg_send)
+    dense = output_weight_call(mixed, proj, gain_two_part, devices)
+    mg, dense, moe_all = lax.optimization_barrier((mg, dense, moe_all))
+    dense = lax.psum_scatter(dense, "seq", scatter_dimension=0)
     moe = lax.psum_scatter(moe_all, "seq", scatter_dimension=0, tiled=True)
     layer_output = (middle + residual_scale * moe.astype(f32)).astype(bf16)
-
-    mg_send, proj, middle_grad, gain_two_part = turn_call(
-        second_grad, middle, gain_two, cot, output_weight, groups
-    )
-    mg = spread(mg_send)
-    output_part = lax.dot_general(mixed, proj, TN, preferred_element_type=f32).astype(bf16)
-    dense = jnp.concatenate(
-        [output_part, jnp.broadcast_to(gain_two_part.astype(bf16), (16, features))], axis=0
-    )
-    dense = lax.psum(dense, ("dp", "seq"))
-    output_weight_grad = dense[: output_part.shape[0]].astype(f32)
-    second_gain_grad = dense[output_part.shape[0]].astype(f32)
-
-    cos_all, sin_all = rope_tables(pos_all.reshape(-1), pair)
+    for bit in dp_bits:
+        dense = (dense.astype(f32) + swap(dense, "dp", bit).astype(f32)).astype(bf16)
+    dense = lax.all_gather(dense, "seq", axis=0).astype(f32)
+    each = output_weight.shape[0] // devices
+    output_weight_grad = dense[:, :each].reshape(output_weight.shape)
+    second_gain_grad = dense[0, each]
+
     table_shape = (devices, micro, per_device, pair)
     dqkv = attend_back_call(
         qkv,
@@ -481,22 +639,15 @@
         sin_all.reshape(table_shape),
     )
     d_all = dqkv.reshape(devices * rows, 2 * pair)
-    first_all = lax.all_gather(first_low, "seq", axis=0).reshape(devices * rows, features)
-    part = lax.dot_general(first_all, d_all, TN, preferred_element_type=f32).astype(bf16)
-    part = part.reshape(replicas, features // replicas, 2 * pair)
-    part = lax.all_to_all(part, "dp", 0, 0, tiled=True)
-    part = jnp.sum(part.astype(f32), axis=0).astype(bf16)
+    first_tokens = first_all.reshape(devices * rows, features)
+    part = lax.dot_general(first_tokens, d_all, TN, preferred_element_type=f32).astype(bf16)
+    for bit in dp_bits[::-1]:
+        part = half_sum(part, "dp", bit)
     wide = lax.all_gather(part, ("dp", "seq"), axis=0)
-    wide = wide.reshape(replicas, devices, features // replicas, 2 * pair)[:, ::copies].astype(f32)
-    wide = jnp.transpose(wide, (0, 2, 1, 3)).reshape(features, groups, 2 * pair)
-    query_weight_grad = wide[..., :pair].reshape(query_weight.shape)
-    key_weight_grad = wide[..., pair : pair + HEAD_DIM].reshape(key_weight.shape)
-    value_weight_grad = wide[..., pair + HEAD_DIM :].reshape(value_weight.shape)
-    first_gain_grad = (
-        jnp.sum(query_weight_grad * query_weight.astype(f32), axis=1)
-        + jnp.sum(key_weight_grad * key_weight.astype(f32), axis=1)
-        + jnp.sum(value_weight_grad * value_weight.astype(f32), axis=1)
-    ) / first_gain
+    wide = wide.reshape(replicas, devices, features // replicas, 2 * pair)[:, ::copies]
+    query_weight_grad, key_weight_grad, value_weight_grad, first_gain_grad = weights_out_call(
+        wide, query_weight, key_weight, value_weight, gain_one
+    )
 
     back = unspread(dqkv.reshape(devices, rows, 2 * pair))
     input_grad = last_call(
@@ -505,15 +656,15 @@
     return (
         layer_output.reshape(layer_input.shape),
         input_grad.reshape(layer_input.shape),
-        first_gain_grad,
+        first_gain_grad.reshape(features),
         query_weight_grad,
         key_weight_grad,
         value_weight_grad,
         output_weight_grad,
         second_gain_grad,
-        expert_sums[0].astype(f32),
-        expert_sums[1].astype(f32),
-        expert_sums[2].astype(f32),
+        gate_sum.astype(f32),
+        up_sum.astype(f32),
+        down_sum.astype(f32),
     )
 
 

time: 743 us -> 572 us (0.77)
  waiting for transfers between devices: 413 us -> 284 us
  blocking collectives: 101 us -> 24.8 us
  starting transfers between devices: 9.52 us -> 33.9 us
  matrix products: 37.5 us -> 21.9 us
  Pallas kernels: 60.9 us -> 76.3 us
  other arithmetic: 39.2 us -> 52 us
    psum x2 -> x0, waiting for transfers between devices: 252 us -> none  [the longest x1 136 us: body(): dense = lax.psum(dense, ('dp', 'seq'))]
    ppermute x0 -> x20, waiting for transfers between devices: none -> 132 us  [swap(): lax.ppermute(values, axis, [(i, i ^ bit) for i in range(lax.axis_size(axi...]
    all_to_all x3 -> x0, blocking collectives: 83.7 us -> none  [the longest x1 58.1 us: spread(): return lax.all_to_all(blocks, 'seq', 0, 0, tiled=True)]
    all_gather x1, waiting for transfers between devices: 52.6 us -> 0.01 us  [body(): wide = lax.all_gather(part, ('dp', 'seq'), axis=0)]
    all_gather x2 -> x3, waiting for transfers between devices: 0.65 us -> 51.5 us  [the longest x1 51.5 us: body(): x_all = lax.all_gather(x, 'seq', axis=0)]
    reduce_scatter x1, waiting for transfers between devices: 0.02 us -> 48.9 us  [body(): second_grad = lax.psum_scatter(dx, 'seq', scatter_dimension=0, tiled=True)]
    reduce_scatter x1, waiting for transfers between devices: 41.5 us -> 0.01 us  [body(): moe = lax.psum_scatter(moe_all, 'seq', scatter_dimension=0, tiled=True)]
    ppermute x0 -> x20, starting transfers between devices: none -> 21.1 us  [swap(): lax.ppermute(values, axis, [(i, i ^ bit) for i in range(lax.axis_size(axi...]
  transfers between devices with their start and end apart: 10 -> 31, of which waited for: 7 -> 18; matrix products, arithmetic and copies ran while one was open for 11% -> 16% of each run, Pallas kernels for 4% -> 8%
where the time goes in v2:
time: 572 us; the launch traced here: 563 us
  waiting for transfers between devices  284 us (50%)
  Pallas kernels  76.3 us (13%)
  local copies, waits for them, and re-layouts  54.9 us (10%)
  other arithmetic  52 us (9%)
  starting transfers between devices  33.9 us (6%)
  blocking collectives  24.8 us (4%)
  matrix products  21.9 us (4%)
  between operations  15.3 us (3%)
    ppermute x20, waiting for transfers between devices, swap(): lax.ppermute(values, axis, [(i, i ^ bit) for i in range(lax.axis_size(axi...  132 us
    all_gather x1, waiting for transfers between devices, body(): x_all = lax.all_gather(x, 'seq', axis=0)  51.5 us
    reduce_scatter x1, waiting for transfers between devices, body(): second_grad = lax.psum_scatter(dx, 'seq', scatter_dimension=0, tiled=True)  48.9 us
    unnamed x120, local copies, waits for them, and re-layouts  46.9 us
    all_gather x1, waiting for transfers between devices, body(): second_all = lax.all_gather(second_low, 'seq', axis=0)  43.9 us
    pallas_call x1, Pallas kernels, expert_call(): pl.pallas_call(expert_kernel, grid=(blocks,), in_specs=[pl.BlockSpec((1,...  29.3 us
    all_to_all x1, blocking collectives, unspread(): return lax.all_to_all(blocks, 'seq', 0, 0, tiled=True)[::copies]  24.8 us
    ppermute x20, starting transfers between devices, swap(): lax.ppermute(values, axis, [(i, i ^ bit) for i in range(lax.axis_size(axi...  21.1 us
  transfers between devices with their start and end apart: 31, of which 18 were waited for; matrix products, arithmetic and copies ran while one was open for 16% of the time, Pallas kernels for 8%

profile of v2, /device:TPU:0, one launch (start us, length us, event | category | flops | bytes accessed | tf_op | source)
XLA Modules:
  0.0 562.6 jit_solution(4331820354526201526)
XLA Ops:
  8.0 51.5 %all-gather.10.cloned.1.call-done.x_ref = bf16[8,256,1024]{2,1,0:T(8,128)(2,1)} async-done(((bf16[1,256,1024]{2,1,0:T(8,128)(2,1)}), bf16[8,256,1024]{2,1,0:T(8,128)(2,1)}) %all-gather.10.cloned.1.call-update) | async-done | bytes 4194320 | tf_op jit(solution)/shard_map/all_gather | solution.py:569
  60.8 3.3 all-to-all-start
  64.2 5.5 all-to-all-done
  69.7 3.7 fusion.12
  75.6 6.3 %norm_qkv_rope.1 = (bf16[8,256,256]{2,1,0:T(8,128)(2,1)S(1)}, bf16[8,256,1024]{2,1,0:T(8,128)(2,1)S(1)}) custom-call(s32[1]{0:T(128)} %bitcast.place_ref, bf16[8,256,1024]{2,1,0:T(8,128)(2,1)S(1)} %copy-done.13, f32[1,1024]{1,0:T(1,128)S(1)} %bitcast.93, f32[2048,128]{1,0:T(8,128)S(1)} %get-tuple-element.138.cos_ref, ...), custom_call_target="tpu_custom_call" | custom-call | flops 1610612736 | bytes 14000000 | tf_op jit(solution)/shard_map/norm_qkv_rope/pallas_call | solution.py:91
  84.0 7.8 %attention_forward.1 = bf16[8,2,128,128]{3,2,1,0:T(8,128)(2,1)S(1)} custom-call(bf16[8,2,128,256]{3,2,1,0:T(8,128)(2,1)S(1)} %bitcast.99), custom_call_target="tpu_custom_call" | custom-call | flops 1073741824 | bytes 1572864 | tf_op jit(solution)/shard_map/attention_forward/pallas_call | solution.py:168
  91.8 24.8 %all_to_all.21.mix_ref = bf16[8,256,128]{2,1,0:T(8,128)(2,1)S(1)} all-to-all(bf16[8,256,128]{2,1,0:T(8,128)(2,1)S(1)} %bitcast.92), channel_id=1, replica_groups=mesh['dp'=4,'seq'=8] {'seq'}, dimensions={0} | all-to-all | bytes 1048576 | tf_op jit(solution)/shard_map/all_to_all | solution.py:563
  122.2 43.9 %all-gather.12.cloned.1.call-done = bf16[2048,1024]{1,0:T(8,128)(2,1)} async-done(((bf16[256,1024]{1,0:T(8,128)(2,1)}), bf16[2048,1024]{1,0:T(8,128)(2,1)}) %all-gather.12.cloned.1.call-update) | async-done | bytes 4194320 | tf_op jit(solution)/shard_map/all_gather | solution.py:585
  170.5 29.3 %expert_gradients.1 = (bf16[2048,1024]{1,0:T(8,128)(2,1)}, bf16[2,2048,512]{2,1,0:T(8,128)(2,1)}, bf16[2,2048,512]{2,1,0:T(8,128)(2,1)}, bf16[2,2048,512]{2,1,0:T(8,128)(2,1)}, bf16[2,2048,1024]{2,1,0:T(8,128)(2,1)}) custom-call(bf16[8,256,1024]{2,1,0:T(8,128)(2,1)} %bitcast.117, bf16[8,256,1024]{2,1,0:T(8,128)(2,1)} %bitcast.118, f32[2048,2]{1,0:T(8,128)S(1)} %bitcast.90, ...), custom_call_target="tpu_custom_call" | custom-call | flops 21474836480 | bytes 40000000 | tf_op jit(solution)/shard_map/expert_gradients/pallas_call | solution.py:287
  199.8 48.9 %reduce-scatter.4.cloned.1.call-done.sg_ref = bf16[256,1024]{1,0:T(8,128)(2,1)} async-done(((bf16[2048,1024]{1,0:T(8,128)(2,1)}), bf16[256,1024]{1,0:T(8,128)(2,1)}) %reduce-scatter.4.cloned.1.call-update) | async-done | bytes 524304 | tf_op jit(solution)/shard_map/reduce_scatter | solution.py:599
  257.4 4.2 all-to-all-start.2
  264.5 2.2 copy-done.35
  266.7 6.1 %expert_outputs.1 = bf16[2048,1024]{1,0:T(8,128)(2,1)S(1)} custom-call(bf16[2,2048,512]{2,1,0:T(8,128)(2,1)S(1)} %copy-done.35, f32[2048,2]{1,0:T(8,128)S(1)} %bitcast.91, bf16[2,512,1024]{2,1,0:T(8,128)(2,1)S(1)} %copy-done.33), custom_call_target="tpu_custom_call" | custom-call | flops 4294967296 | bytes 11000000 | tf_op jit(solution)/shard_map/expert_outputs/pallas_call | solution.py:331
  276.9 2.2 output_weight_part.1
  281.2 3.7 fusion.13
  284.9 3.0 pad_maximum_fusion.2
  287.9 14.6 %attention_backward.1 = bf16[8,2,128,256]{3,2,1,0:T(8,128)(2,1)} custom-call(bf16[8,2,128,256]{3,2,1,0:T(8,128)(2,1)} %bitcast.100, bf16[8,2,128,128]{3,2,1,0:T(8,128)(2,1)} %bitcast.18.grad_ref, f32[8,2,128,128]{3,2,1,0:T(8,128)} %get-tuple-element.140.cos_ref, f32[8,2,128,128]{3,2,1,0:T(8,128)} %get-tuple-element.141.sin_ref), custom_call_target="tpu_custom_call" | custom-call | flops 2684354560 | bytes 5242880 | tf_op jit(solution)/shard_map/attention_backward/pallas_call | solution.py:217
  302.5 2.5 convolution_convert_fusion.1
  308.1 7.3 %collective-permute-done = bf16[512,256]{1,0:T(8,128)(2,1)S(1)} collective-permute-done((bf16[512,256]{1,0:T(8,128)(2,1)}, bf16[512,256]{1,0:T(8,128)(2,1)S(1)}, u32[]{:S(2)}, u32[]{:S(2)}) %collective-permute-start) | collective-permute-done | bytes 262176 | tf_op jit(solution)/shard_map/ppermute | solution.py:500
  318.1 3.6 collective-permute-done.1
  322.5 9.7 %convolution_convert_fusion = bf16[2,512,1024]{2,1,0:T(8,128)(2,1)S(1)} fusion(bf16[2,2048,512]{2,1,0:T(8,128)(2,1)} %get-tuple-element.44.h_ref, bf16[2,2048,1024]{2,1,0:T(8,128)(2,1)} %get-tuple-element.56), kind=kOutput, calls=%fused_computation.13 | convolution fusion | flops 4296015872 | bytes 14680064 | tf_op jit(solution)/shard_map/etf,etd->efd/dot_general | solution.py:604
  335.3 4.9 convert_bitcast_fusion
  340.9 3.6 collective-permute-done.12
  344.5 4.1 collective-permute-done.16
  350.9 4.7 convert_bitcast_fusion.1
  356.3 17.2 %collective-permute-done.13 = bf16[128,1024]{1,0:T(8,128)(2,1)S(1)} collective-permute-done((bf16[128,1024]{1,0:T(8,128)(2,1)S(1)}, bf16[128,1024]{1,0:T(8,128)(2,1)S(1)}, u32[]{:S(2)}, u32[]{:S(2)}) %collective-permute-start.13) | collective-permute-done | bytes 262176 | tf_op jit(solution)/shard_map/ppermute | solution.py:500
  386.4 21.2 %collective-permute-done.4 = bf16[1024,512]{0,1:T(8,128)(2,1)} collective-permute-done((bf16[1024,512]{0,1:T(8,128)(2,1)}, bf16[1024,512]{0,1:T(8,128)(2,1)}, u32[]{:S(2)}, u32[]{:S(2)}) %collective-permute-start.4) | collective-permute-done | bytes 1048608 | tf_op jit(solution)/shard_map/ppermute | solution.py:500
  407.6 2.5 fusion.5
  410.1 35.2 %collective-permute-done.2 = bf16[144,1024]{1,0:T(8,128)(2,1)S(1)} collective-permute-done((bf16[144,1024]{1,0:T(8,128)(2,1)}, bf16[144,1024]{1,0:T(8,128)(2,1)S(1)}, u32[]{:S(2)}, u32[]{:S(2)}) %collective-permute-start.2) | collective-permute-done | bytes 294944 | tf_op jit(solution)/shard_map/ppermute | solution.py:500
  450.2 5.2 collective-permute-done.3
  460.2 6.6 %collective-permute-done.5 = bf16[512,512]{0,1:T(8,128)(2,1)} collective-permute-done((bf16[512,512]{0,1:T(8,128)(2,1)}, bf16[512,512]{0,1:T(8,128)(2,1)}, u32[]{:S(2)}, u32[]{:S(2)}) %collective-permute-start.5) | collective-permute-done | bytes 524320 | tf_op jit(solution)/shard_map/ppermute | solution.py:500
  468.3 2.3 broadcast_select_fusion.7
  473.6 4.3 collective-permute-done.19
  479.1 10.0 %collective-permute-done.6 = bf16[512,512]{0,1:T(8,128)(2,1)S(1)} collective-permute-done((bf16[512,512]{0,1:T(8,128)(2,1)S(1)}, bf16[512,512]{0,1:T(8,128)(2,1)S(1)}, u32[]{:S(2)}, u32[]{:S(2)}) %collective-permute-start.6) | collective-permute-done | bytes 524320 | tf_op jit(solution)/shard_map/ppermute | solution.py:500
  490.1 4.5 all-to-all-start.3
  494.7 2.4 pad_maximum_fusion.4
  497.6 2.3 maximum_convert_fusion.2
  499.9 6.8 %collective-permute-done.11 = bf16[1024,512]{0,1:T(8,128)(2,1)} collective-permute-done((bf16[1024,512]{0,1:T(8,128)(2,1)}, bf16[1024,512]{0,1:T(8,128)(2,1)}, u32[]{:S(2)}, u32[]{:S(2)}) %collective-permute-start.11) | collective-permute-done | bytes 1048608 | tf_op jit(solution)/shard_map/ppermute | solution.py:500
  508.4 2.6 maximum_convert_fusion.1
  511.0 5.3 copy.75
  516.3 6.6 %collective-permute-done.7 = bf16[1024,512]{0,1:T(8,128)(2,1)} collective-permute-done((bf16[1024,512]{0,1:T(8,128)(2,1)}, bf16[1024,512]{0,1:T(8,128)(2,1)}, u32[]{:S(2)}, u32[]{:S(2)}) %collective-permute-start.7) | collective-permute-done | bytes 1048608 | tf_op jit(solution)/shard_map/ppermute | solution.py:500
  525.0 2.6 maximum_convert_fusion
  527.5 5.3 copy.74
  536.4 3.7 input_gradient.1
  540.1 2.3 add_convert_fusion.2
  543.6 2.2 copy-done.14
  545.8 4.1 attention_weights_out.1
  549.9 4.1 slice.106
  (209 shorter events, 86.5 us)
Async XLA Ops:
  7.2 52.3 %all-gather.10.cloned.1.call-start = ((), (), s32[]{:S(2)}) async-start(), calls=%async_computation.7 | async-start | bytes 4718592 | tf_op jit(solution)/shard_map/all_gather | solution.py:569
  7.9 114.2 %all-gather.14.cloned.1.call-start = ((), (), s32[]{:S(2)}) async-start(), calls=%async_computation.12 | async-start | bytes 4718592 | tf_op jit(solution)/shard_map/all_gather | solution.py:575
  60.8 8.9 %all-to-all-start = ((s32[8,1,256]{2,1,0:T(1,128)}), s32[8,1,256]{2,1,0:T(1,128)S(1)}, u32[]{:S(2)}, u32[]{:S(2)}) async-start(s32[8,1,256]{2,1,0:T(1,128)} %broadcast_in_dim.24), calls=%async_computation | async-start | bytes 16384 | tf_op jit(solution)/shard_map/all_to_all | solution.py:570
  64.1 101.9 %all-gather.12.cloned.1.call-start = ((), (), s32[]{:S(2)}) async-start(), calls=%async_computation.11 | async-start | bytes 4718592 | tf_op jit(solution)/shard_map/all_gather | solution.py:585
  84.0 32.6 %copy-start.34 = (bf16[8,256,256]{2,1,0:T(8,128)(2,1)}, bf16[8,256,256]{2,1,0:T(8,128)(2,1)S(1)}, u32[]{:S(2)}) copy-start(bf16[8,256,256]{2,1,0:T(8,128)(2,1)S(1)} %get-tuple-element.35) | copy-start | bytes 3145732
  84.0 32.6 %copy-start.6 = (bf16[1024,1024]{1,0:T(8,128)(2,1)S(1)}, bf16[1024,1024]{1,0:T(8,128)(2,1)}, u32[]{:S(2)}) copy-start(bf16[1024,1024]{1,0:T(8,128)(2,1)} %wo_ref.3) | copy-start | bytes 6291460
  84.0 32.6 %copy-start.8 = (bf16[2,1,128,1024]{3,2,1,0:T(8,128)(2,1)S(1)}, bf16[2,1,128,1024]{3,2,1,0:T(8,128)(2,1)}, u32[]{:S(2)}) copy-start(bf16[2,1,128,1024]{3,2,1,0:T(8,128)(2,1)} %param.14) | copy-start | bytes 1572868
  84.0 32.6 %copy-start.28 = (f32[1024]{0:T(1024)S(1)}, f32[1024]{0:T(1024)}, u32[]{:S(2)}) copy-start(f32[1024]{0:T(1024)} %param.20) | copy-start | bytes 12292
  91.8 28.8 %copy-start.55 = (bf16[2,1,1024,8]{2,3,1,0:T(8,128)(2,1)S(1)}, bf16[2,1,1024,8]{2,3,1,0:T(8,128)(2,1)}, u32[]{:S(2)}) copy-start(bf16[2,1,1024,8]{2,3,1,0:T(8,128)(2,1)} %param.25) | copy-start | bytes 98308
  91.8 28.8 %copy-start.54 = (s32[2,1,1024,8]{2,3,1,0:T(8,128)S(1)}, s32[2,1,1024,8]{2,3,1,0:T(8,128)}, u32[]{:S(2)}) copy-start(s32[2,1,1024,8]{2,3,1,0:T(8,128)} %param.24) | copy-start | bytes 196612
  120.1 128.6 %reduce-scatter.4.cloned.1.call-start = ((), (), s32[]{:S(2)}) async-start(), calls=%async_computation.8 | async-start | bytes 4718592 | tf_op jit(solution)/shard_map/reduce_scatter | solution.py:599
  257.4 23.1 %all-to-all-start.2 = ((bf16[8,256,128]{2,1,0:T(8,128)(2,1)}), bf16[8,256,128]{2,1,0:T(8,128)(2,1)}, u32[]{:S(2)}, u32[]{:S(2)}) async-start(bf16[8,256,128]{2,1,0:T(8,128)(2,1)} %copy-done.22), calls=%async_computation.3 | async-start | bytes 1048576 | tf_op jit(solution)/shard_map/all_to_all | solution.py:560
  261.6 123.9 %reduce-scatter.8.cloned.1.call-start = ((), (), s32[]{:S(2)}) async-start(), calls=%async_computation.10 | async-start | bytes 2654208 | tf_op jit(solution)/shard_map/reduce_scatter | solution.py:624
  280.5 259.5 %reduce-scatter.6.cloned.1.call-start = ((), (), s32[]{:S(2)}) async-start(), calls=%async_computation.9 | async-start | bytes 4718592 | tf_op jit(solution)/shard_map/reduce_scatter | solution.py:625
  281.1 261.3 %all-gather.16.cloned.1.call-start = ((), (), s32[]{:S(2)}) async-start(), calls=%async_computation.13 | async-start | bytes 4325376 | tf_op jit(solution)/shard_map/all_gather | solution.py:646
  287.9 14.6 %copy-start.30 = (bf16[8,256,1024]{2,1,0:T(8,128)(2,1)S(1)}, bf16[8,256,1024]{2,1,0:T(8,128)(2,1)}, u32[]{:S(2)}) copy-start(bf16[8,256,1024]{2,1,0:T(8,128)(2,1)} %copy-done.29) | copy-start | bytes 12582916
  306.6 8.8 %collective-permute-start = (bf16[512,256]{1,0:T(8,128)(2,1)}, bf16[512,256]{1,0:T(8,128)(2,1)S(1)}, u32[]{:S(2)}, u32[]{:S(2)}) collective-permute-start(bf16[512,256]{1,0:T(8,128)(2,1)} %broadcast_select_fusion.20), channel_id=1, source_target_pairs={{0,16},{8,24},{16,0},{24,8},{1,17},{9,25},{17,1},{25,9},{2,18},{10... | collective-permute-start | bytes 786440 | tf_op jit(solution)/shard_map/ppermute | solution.py:500
  316.5 5.1 collective-permute-start.1
  322.4 227.6 %all-gather.18.cloned.1.call-start = ((), (), s32[]{:S(2)}) async-start(), calls=%async_computation.14 | async-start | bytes 2654208 | tf_op jit(solution)/shard_map/all_gather | solution.py:629
  322.4 12.8 %copy-start.56 = (bf16[2048,1024]{1,0:T(8,128)(2,1)S(1)}, bf16[2048,1024]{1,0:T(8,128)(2,1)}, u32[]{:S(2)}) copy-start(bf16[2048,1024]{1,0:T(8,128)(2,1)} %all-gather.12.cloned.1.call-done) | copy-start | bytes 12582916
  322.4 12.8 %copy-start.58 = (bf16[2,2048,512]{2,1,0:T(8,128)(2,1)S(1)}, bf16[2,2048,512]{2,1,0:T(8,128)(2,1)}, u32[]{:S(2)}) copy-start(bf16[2,2048,512]{2,1,0:T(8,128)(2,1)} %get-tuple-element.55) | copy-start | bytes 12582916
  332.3 12.2 %collective-permute-start.12 = (bf16[256,1024]{1,0:T(8,128)(2,1)S(1)}, bf16[256,1024]{1,0:T(8,128)(2,1)S(1)}, u32[]{:S(2)}, u32[]{:S(2)}) collective-permute-start(bf16[256,1024]{1,0:T(8,128)(2,1)S(1)} %get-tuple-element.114), channel_id=1, source_target_pairs={{0,8},{8,0},{16,24},{24,16},{1,9},{9,1},{17,25},{25,17},{2,10},{10... | collective-permute-start | bytes 1572872 | tf_op jit(solution)/shard_map/ppermute | solution.py:500
  333.8 14.9 %collective-permute-start.16 = (bf16[256,1024]{1,0:T(8,128)(2,1)S(1)}, bf16[256,1024]{1,0:T(8,128)(2,1)S(1)}, u32[]{:S(2)}, u32[]{:S(2)}) collective-permute-start(bf16[256,1024]{1,0:T(8,128)(2,1)S(1)} %get-tuple-element.115), channel_id=1, source_target_pairs={{0,16},{8,24},{16,0},{24,8},{1,17},{9,25},{17,1},{25,9},{2,18},{10... | collective-permute-start | bytes 1572872 | tf_op jit(solution)/shard_map/ppermute | solution.py:500
  340.3 10.6 %copy-start.57 = (bf16[2,2048,512]{2,1,0:T(8,128)(2,1)S(1)}, bf16[2,2048,512]{2,1,0:T(8,128)(2,1)}, u32[]{:S(2)}) copy-start(bf16[2,2048,512]{2,1,0:T(8,128)(2,1)} %get-tuple-element.54) | copy-start | bytes 12582916
  340.3 41.5 %collective-permute-start.8 = (bf16[1024,512]{0,1:T(8,128)(2,1)S(1)}, bf16[1024,512]{0,1:T(8,128)(2,1)S(1)}, u32[]{:S(2)}, u32[]{:S(2)}) collective-permute-start(bf16[1024,512]{0,1:T(8,128)(2,1)S(1)} %select_bitcast_fusion), channel_id=1, source_target_pairs={{0,16},{8,24},{16,0},{24,8},{1,17},{9,25},{17,1},{25,9},{2,18},{10... | collective-permute-start | bytes 3145736 | tf_op jit(solution)/shard_map/ppermute | solution.py:500
  349.3 24.2 %collective-permute-start.13 = (bf16[128,1024]{1,0:T(8,128)(2,1)S(1)}, bf16[128,1024]{1,0:T(8,128)(2,1)S(1)}, u32[]{:S(2)}, u32[]{:S(2)}) collective-permute-start(bf16[128,1024]{1,0:T(8,128)(2,1)S(1)} %broadcast_select_fusion.19), channel_id=1, source_target_pairs={{0,16},{8,24},{16,0},{24,8},{1,17},{9,25},{17,1},{25,9},{2,18},{10... | collective-permute-start | bytes 786440 | tf_op jit(solution)/shard_map/ppermute | solution.py:500
  355.6 20.9 %copy-start.39 = (bf16[2,1024,512]{1,2,0:T(8,128)(2,1)}, bf16[2,1024,512]{1,2,0:T(8,128)(2,1)S(1)}, u32[]{:S(2)}) copy-start(bf16[2,1024,512]{1,2,0:T(8,128)(2,1)S(1)} %convert_bitcast_fusion.1) | copy-start | bytes 6291460
  355.7 21.4 %collective-permute-start.17 = (bf16[128,1024]{1,0:T(8,128)(2,1)S(1)}, bf16[128,1024]{1,0:T(8,128)(2,1)S(1)}, u32[]{:S(2)}, u32[]{:S(2)}) collective-permute-start(bf16[128,1024]{1,0:T(8,128)(2,1)S(1)} %broadcast_select_fusion.16), channel_id=1, source_target_pairs={{0,8},{8,0},{16,24},{24,16},{1,9},{9,1},{17,25},{25,17},{2,10},{10... | collective-permute-start | bytes 786440 | tf_op jit(solution)/shard_map/ppermute | solution.py:500
  373.7 6.4 %collective-permute-start.14 = (bf16[128,1024]{1,0:T(8,128)(2,1)S(1)}, bf16[128,1024]{1,0:T(8,128)(2,1)S(1)}, u32[]{:S(2)}, u32[]{:S(2)}) collective-permute-start(bf16[128,1024]{1,0:T(8,128)(2,1)S(1)} %add_convert_fusion.6), channel_id=1, source_target_pairs={{0,16},{8,24},{16,0},{24,8},{1,17},{9,25},{17,1},{25,9},{2,18},{10... | collective-permute-start | bytes 786440 | tf_op jit(solution)/shard_map/ppermute | solution.py:500
  376.5 31.0 %collective-permute-start.4 = (bf16[1024,512]{0,1:T(8,128)(2,1)}, bf16[1024,512]{0,1:T(8,128)(2,1)}, u32[]{:S(2)}, u32[]{:S(2)}) collective-permute-start(bf16[1024,512]{0,1:T(8,128)(2,1)} %select_bitcast_fusion.1), channel_id=1, source_target_pairs={{0,8},{8,0},{16,24},{24,16},{1,9},{9,1},{17,25},{25,17},{2,10},{10... | collective-permute-start | bytes 3145736 | tf_op jit(solution)/shard_map/ppermute | solution.py:500
  377.9 70.4 %collective-permute-start.18 = (bf16[128,1024]{1,0:T(8,128)(2,1)}, bf16[128,1024]{1,0:T(8,128)(2,1)}, u32[]{:S(2)}, u32[]{:S(2)}) collective-permute-start(bf16[128,1024]{1,0:T(8,128)(2,1)} %add_convert_fusion.5), channel_id=1, source_target_pairs={{0,8},{8,0},{16,24},{24,16},{1,9},{9,1},{17,25},{25,17},{2,10},{10... | collective-permute-start | bytes 786440 | tf_op jit(solution)/shard_map/ppermute | solution.py:500
  381.0 87.3 %collective-permute-start.15 = (bf16[256,1024]{1,0:T(8,128)(2,1)}, bf16[256,1024]{1,0:T(8,128)(2,1)}, u32[]{:S(2)}, u32[]{:S(2)}) collective-permute-start(bf16[256,1024]{1,0:T(8,128)(2,1)} %pad_maximum_fusion.6), channel_id=1, source_target_pairs={{0,8},{8,0},{16,24},{24,16},{1,9},{9,1},{17,25},{25,17},{2,10},{10... | collective-permute-start | bytes 1572872 | tf_op jit(solution)/shard_map/ppermute | solution.py:500
  384.3 73.4 %collective-permute-start.9 = (bf16[512,512]{0,1:T(8,128)(2,1)}, bf16[512,512]{0,1:T(8,128)(2,1)}, u32[]{:S(2)}, u32[]{:S(2)}) collective-permute-start(bf16[512,512]{0,1:T(8,128)(2,1)} %broadcast_select_fusion.10), channel_id=1, source_target_pairs={{0,8},{8,0},{16,24},{24,16},{1,9},{9,1},{17,25},{25,17},{2,10},{10... | collective-permute-start | bytes 1572872 | tf_op jit(solution)/shard_map/ppermute | solution.py:500
  385.5 59.8 %copy-start.53 = (bf16[1,144,1024]{2,1,0:T(8,128)(2,1)S(1)}, bf16[1,144,1024]{2,1,0:T(8,128)(2,1)}, u32[]{:S(2)}) copy-start(bf16[1,144,1024]{2,1,0:T(8,128)(2,1)} %reduce-scatter.8.cloned.1.call-done) | copy-start | bytes 884740
  385.5 59.8 %collective-permute-start.2 = (bf16[144,1024]{1,0:T(8,128)(2,1)}, bf16[144,1024]{1,0:T(8,128)(2,1)S(1)}, u32[]{:S(2)}, u32[]{:S(2)}) collective-permute-start(bf16[144,1024]{1,0:T(8,128)(2,1)} %bitcast.110), channel_id=1, source_target_pairs={{0,8},{8,0},{16,24},{24,16},{1,9},{9,1},{17,25},{25,17},{2,10},{10... | collective-permute-start | bytes 884744 | tf_op jit(solution)/shard_map/ppermute | solution.py:500
  410.1 35.7 %copy-start.37 = (bf16[1024,512]{0,1:T(8,128)(2,1)}, bf16[1024,512]{0,1:T(8,128)(2,1)S(1)}, u32[]{:S(2)}) copy-start(bf16[1024,512]{0,1:T(8,128)(2,1)S(1)} %fusion.5) | copy-start | bytes 3145732
  445.4 10.0 %collective-permute-start.3 = (bf16[144,1024]{1,0:T(8,128)(2,1)S(1)}, bf16[144,1024]{1,0:T(8,128)(2,1)S(1)}, u32[]{:S(2)}, u32[]{:S(2)}) collective-permute-start(bf16[144,1024]{1,0:T(8,128)(2,1)S(1)} %add_convert_fusion.4), channel_id=1, source_target_pairs={{0,16},{8,24},{16,0},{24,8},{1,17},{9,25},{17,1},{25,9},{2,18},{10... | collective-permute-start | bytes 884744 | tf_op jit(solution)/shard_map/ppermute | solution.py:500
  446.6 20.1 %collective-permute-start.5 = (bf16[512,512]{0,1:T(8,128)(2,1)}, bf16[512,512]{0,1:T(8,128)(2,1)}, u32[]{:S(2)}, u32[]{:S(2)}) collective-permute-start(bf16[512,512]{0,1:T(8,128)(2,1)} %broadcast_select_fusion.13), channel_id=1, source_target_pairs={{0,16},{8,24},{16,0},{24,8},{1,17},{9,25},{17,1},{25,9},{2,18},{10... | collective-permute-start | bytes 1572872 | tf_op jit(solution)/shard_map/ppermute | solution.py:500
  456.2 10.5 %copy-start.38 = (bf16[1024,512]{0,1:T(8,128)(2,1)S(1)}, bf16[1024,512]{0,1:T(8,128)(2,1)}, u32[]{:S(2)}) copy-start(bf16[1024,512]{0,1:T(8,128)(2,1)} %copy-done.37) | copy-start | bytes 3145732
  457.4 11.0 %copy-start.45 = (bf16[128,1024]{1,0:T(8,128)(2,1)S(1)}, bf16[128,1024]{1,0:T(8,128)(2,1)}, u32[]{:S(2)}) copy-start(bf16[128,1024]{1,0:T(8,128)(2,1)} %copy-done.44) | copy-start | bytes 786436
  457.4 20.5 %collective-permute-start.19 = (bf16[256,1024]{1,0:T(8,128)(2,1)S(1)}, bf16[256,1024]{1,0:T(8,128)(2,1)S(1)}, u32[]{:S(2)}, u32[]{:S(2)}) collective-permute-start(bf16[256,1024]{1,0:T(8,128)(2,1)S(1)} %pad_maximum_fusion.7), channel_id=1, source_target_pairs={{0,16},{8,24},{16,0},{24,8},{1,17},{9,25},{17,1},{25,9},{2,18},{10... | collective-permute-start | bytes 1572872 | tf_op jit(solution)/shard_map/ppermute | solution.py:500
  459.3 11.3 %collective-permute-start.10 = (bf16[512,512]{0,1:T(8,128)(2,1)S(1)}, bf16[512,512]{0,1:T(8,128)(2,1)S(1)}, u32[]{:S(2)}, u32[]{:S(2)}) collective-permute-start(bf16[512,512]{0,1:T(8,128)(2,1)S(1)} %add_convert_fusion), channel_id=1, source_target_pairs={{0,8},{8,0},{16,24},{24,16},{1,9},{9,1},{17,25},{25,17},{2,10},{10... | collective-permute-start | bytes 1572872 | tf_op jit(solution)/shard_map/ppermute | solution.py:500
  468.0 21.1 %collective-permute-start.6 = (bf16[512,512]{0,1:T(8,128)(2,1)S(1)}, bf16[512,512]{0,1:T(8,128)(2,1)S(1)}, u32[]{:S(2)}, u32[]{:S(2)}) collective-permute-start(bf16[512,512]{0,1:T(8,128)(2,1)S(1)} %add_convert_fusion.1), channel_id=1, source_target_pairs={{0,16},{8,24},{16,0},{24,8},{1,17},{9,25},{17,1},{25,9},{2,18},{10... | collective-permute-start | bytes 1572872 | tf_op jit(solution)/shard_map/ppermute | solution.py:500
  470.7 19.4 %copy-start.40 = (bf16[512,512]{0,1:T(8,128)(2,1)}, bf16[512,512]{0,1:T(8,128)(2,1)S(1)}, u32[]{:S(2)}) copy-start(bf16[512,512]{0,1:T(8,128)(2,1)S(1)} %get-tuple-element.124) | copy-start | bytes 1572868
  470.7 19.4 %copy-start.42 = (bf16[512,512]{0,1:T(8,128)(2,1)}, bf16[512,512]{0,1:T(8,128)(2,1)S(1)}, u32[]{:S(2)}) copy-start(bf16[512,512]{0,1:T(8,128)(2,1)S(1)} %get-tuple-element.125) | copy-start | bytes 1572868
  471.8 34.9 %collective-permute-start.11 = (bf16[1024,512]{0,1:T(8,128)(2,1)}, bf16[1024,512]{0,1:T(8,128)(2,1)}, u32[]{:S(2)}, u32[]{:S(2)}) collective-permute-start(bf16[1024,512]{0,1:T(8,128)(2,1)} %pad_maximum_fusion.5), channel_id=1, source_target_pairs={{0,16},{8,24},{16,0},{24,8},{1,17},{9,25},{17,1},{25,9},{2,18},{10... | collective-permute-start | bytes 3145736 | tf_op jit(solution)/shard_map/ppermute | solution.py:500
  490.1 42.7 %all-to-all-start.3 = ((bf16[8,256,256]{2,1,0:T(8,128)(2,1)}), bf16[8,256,256]{2,1,0:T(8,128)(2,1)}, u32[]{:S(2)}, u32[]{:S(2)}) async-start(bf16[8,256,256]{2,1,0:T(8,128)(2,1)} %bitcast.108), calls=%async_computation.5 | async-start | bytes 2097152 | tf_op jit(solution)/shard_map/all_to_all | solution.py:563
  497.1 25.8 %collective-permute-start.7 = (bf16[1024,512]{0,1:T(8,128)(2,1)}, bf16[1024,512]{0,1:T(8,128)(2,1)}, u32[]{:S(2)}, u32[]{:S(2)}) collective-permute-start(bf16[1024,512]{0,1:T(8,128)(2,1)} %pad_maximum_fusion.4), channel_id=1, source_target_pairs={{0,8},{8,0},{16,24},{24,16},{1,9},{9,1},{17,25},{25,17},{2,10},{10... | collective-permute-start | bytes 3145736 | tf_op jit(solution)/shard_map/ppermute | solution.py:500
  (42 other events, 95.3 us)
Sparse Core Ops, SparseCore 0:
  9.6 49.8 all-gather.9
  61.1 55.3 all-gather.13
  120.2 45.8 all-gather.11
  200.0 48.7 reduce-scatter.3
  280.7 37.5 reduce-scatter.7
  321.0 49.1 reduce-scatter.5
  373.2 70.3 all-gather.15
  456.3 29.6 all-gather.17

commit v3 on v2

--- a/solution.py
+++ b/solution.py
@@ -253,13 +253,22 @@
     )(mix, wo, x, gain)
 
 
-def expert_kernel(
-    x_ref, cot_ref, w_ref, wg_ref, wu_ref, wd_ref, dx_ref, h_ref, dg_ref, du_ref, sg_ref
-):
-    x = x_ref[0]
+def expert_kernel(place_ref, a_ref, b_ref, cot_ref, w_ref, wg_ref, wu_ref, wd_ref, *refs):
+    dx_ref, moe_ref, x_ref, h_ref, dg_ref, du_ref, sg_ref = refs[-7:]
+    step = pl.program_id(0)
+
+    @pl.when(step == 0)
+    def _():
+        x_ref[...] = a_ref[...]
+
+    @pl.when(step == 1)
+    def _():
+        x_ref[...] = b_ref[...]
+
+    x = x_ref[...]
     cot = residual_scale * cot_ref[0].astype(f32)
     weight = w_ref[...]
-    total = None
+    total, made = None, None
     for e in range(wg_ref.shape[0]):
         gate = dot(x, wg_ref[e])
         up = dot(x, wu_ref[e])
@@ -268,80 +277,68 @@
         hidden_grad = dot_nt(slot_grad, wd_ref[e])
         sig = 1.0 / (1.0 + jnp.exp(-gate))
         silu = gate * sig
-        h_ref[e] = (silu * up).astype(bf16)
+        hidden = (silu * up).astype(bf16)
+        h_ref[e] = hidden
         gate_grad = (hidden_grad * up * (sig * (1.0 + gate * (1.0 - sig)))).astype(bf16)
         up_grad = (hidden_grad * silu).astype(bf16)
         dg_ref[e] = gate_grad
         du_ref[e] = up_grad
         term = dot_nt(gate_grad, wg_ref[e]) + dot_nt(up_grad, wu_ref[e])
+        out = weight[:, e : e + 1] * dot(hidden, wd_ref[e])
         total = term if total is None else total + term
-    dx_ref[...] = total.astype(bf16)
-
-
-def expert_call(x, cot, weight, wg, wu, wd):
-    blocks, rows, features = x.shape
+        made = out if made is None else made + out
+    dx_ref[0] = total.astype(bf16)
+    moe_ref[0] = made.astype(bf16)
+
+
+def expert_call(at, place, own, other, cot_all, weight, wg, wu, wd, kept):
+    blocks, rows, features = cot_all.shape
     count, _, hidden = wg.shape
     tokens = blocks * rows
     inner = jax.ShapeDtypeStruct((count, tokens, hidden), bf16)
-    inner_spec = pl.BlockSpec((count, rows, hidden), lambda s: (0, s, 0))
+    inner_spec = pl.BlockSpec((count, rows, hidden), lambda s, place: (0, 2 * at + s, 0))
+    fixed = lambda shape: pl.BlockSpec(shape, lambda s, place: (0,) * len(shape))
+    any_spec = pl.BlockSpec(memory_space=pl.ANY)
+    first = 8
     return pl.pallas_call(
         expert_kernel,
-        grid=(blocks,),
-        in_specs=[
-            pl.BlockSpec((1, rows, features), lambda s: (s, 0, 0)),
-            pl.BlockSpec((1, rows, features), lambda s: (s, 0, 0)),
-            pl.BlockSpec((rows, count), lambda s: (s, 0)),
-            whole(wg.shape),
-            whole(wu.shape),
-            whole(wd.shape),
-        ],
-        out_specs=[
-            pl.BlockSpec((rows, features), lambda s: (s, 0)),
-            inner_spec,
-            inner_spec,
-            inner_spec,
-            pl.BlockSpec((count, rows, features), lambda s: (0, s, 0)),
-        ],
+        grid_spec=pltpu.PrefetchScalarGridSpec(
+            num_scalar_prefetch=1,
+            grid=(2,),
+            in_specs=[
+                fixed((rows, features)),
+                fixed((rows, features)),
+                pl.BlockSpec((1, rows, features), lambda s, place: (place[s], 0, 0)),
+                pl.BlockSpec((rows, count), lambda s, place: (place[s], 0)),
+                fixed(wg.shape),
+                fixed(wu.shape),
+                fixed(wd.shape),
+            ]
+            + [any_spec] * len(kept),
+            out_specs=[
+                pl.BlockSpec((1, rows, features), lambda s, place: (s, 0, 0)),
+                pl.BlockSpec((1, rows, features), lambda s, place: (place[s], 0, 0)),
+                pl.BlockSpec((rows, features), lambda s, place: (2 * at + s, 0)),
+                inner_spec,
+                inner_spec,
+                inner_spec,
+                pl.BlockSpec((count, rows, features), lambda s, place: (0, 2 * at + s, 0)),
+            ],
+        ),
         out_shape=[
+            jax.ShapeDtypeStruct((2, rows, features), bf16),
+            jax.ShapeDtypeStruct((blocks, rows, features), bf16),
             jax.ShapeDtypeStruct((tokens, features), bf16),
             inner,
             inner,
             inner,
             jax.ShapeDtypeStruct((count, tokens, features), bf16),
         ],
+        input_output_aliases={first + i: 1 + i for i in range(len(kept))},
         compiler_params=params(48, "arbitrary"),
-        cost_estimate=cost(10 * tokens * wg.size, 4e7, tokens * hidden * count),
-        name="expert_gradients",
-    )(x, cot, weight, wg, wu, wd)
-
-
-def moe_kernel(h_ref, w_ref, wd_ref, out_ref):
-    weight = w_ref[...]
-    total = None
-    for e in range(wd_ref.shape[0]):
-        term = weight[:, e : e + 1] * dot(h_ref[e], wd_ref[e])
-        total = term if total is None else total + term
-    out_ref[...] = total.astype(bf16)
-
-
-def moe_call(hidden, weight, wd):
-    count, tokens, inner = hidden.shape
-    features = wd.shape[2]
-    rows = 256
-    return pl.pallas_call(
-        moe_kernel,
-        grid=(tokens // rows,),
-        in_specs=[
-            pl.BlockSpec((count, rows, inner), lambda s: (0, s, 0)),
-            pl.BlockSpec((rows, count), lambda s: (s, 0)),
-            whole(wd.shape),
-        ],
-        out_specs=pl.BlockSpec((rows, features), lambda s: (s, 0)),
-        out_shape=jax.ShapeDtypeStruct((tokens, features), bf16),
-        compiler_params=params(32, "arbitrary"),
-        cost_estimate=cost(2 * tokens * wd.size, 1.1e7),
-        name="expert_outputs",
-    )(hidden, weight, wd)
+        cost_estimate=cost(24 * rows * wg.size, 2e7, 2 * rows * hidden * count),
+        name="experts",
+    )(place, own, other, cot_all, weight, wg, wu, wd, *kept)
 
 
 def turn_kernel(sg_ref, middle_ref, gain_ref, cot_ref, wo_ref, mg_ref, proj_ref, dmid_ref, dgain_ref):
@@ -516,16 +513,6 @@
     )
 
 
-def sum_over(values, axis, bits):
-    shape = values.shape
-    values = values.reshape(-1, shape[-1])
-    for bit in bits:
-        values = half_sum(values, axis, bit)
-    for bit in bits[::-1]:
-        values = join_halves(values, axis, bit)
-    return values.reshape(shape)
-
-
 def body(
     layer_input,
     first_gain,
@@ -566,24 +553,12 @@
     cot = cotangent.reshape(rows, features)
     gain_one = first_gain.reshape(1, features)
     gain_two = second_gain.reshape(1, features)
-    x_all = lax.all_gather(x, "seq", axis=0)
     pos_all = lax.all_to_all(
         jnp.broadcast_to(positions.reshape(1, rows), (devices, rows)), "seq", 0, 0, tiled=True
     )
+    x_then, pos_all = lax.optimization_barrier((x, pos_all))
+    x_all = lax.all_gather(x_then, "seq", axis=0)
     cos_all, sin_all = rope_tables(pos_all.reshape(-1), pair)
-    x_all, cot_then = lax.optimization_barrier((x_all, cot))
-    cot_all = lax.all_gather(cot_then, "seq", axis=0)
-
-    group = (seq_place // copies).astype(jnp.int32).reshape(1)
-    qkv, first_all = qkv_call(
-        group, x_all, gain_one, cos_all, sin_all, query_weight, key_weight, value_weight
-    )
-    qkv = qkv.reshape(devices, micro, per_device, 2 * pair)
-    mix = attend_call(qkv)
-    mix = unspread(mix.reshape(devices, rows, pair))
-    mixed, middle, second_low = post_call(mix, output_weight, x, gain_two)
-    second_all = lax.all_gather(second_low, "seq", axis=0)
-
     mine = seq_place * local_experts + jnp.arange(local_experts, dtype=jnp.int32)
     ids = expert_ids[:, 0]
     gates = gate_values[:, 0].astype(f32)
@@ -592,37 +567,74 @@
     )
     routed = routed.reshape(micro, devices, per_device, local_experts)
     routed = jnp.transpose(routed, (1, 0, 2, 3)).reshape(devices * rows, local_experts)
-
-    dx, hidden, gate_low, up_low, slot_grad = expert_call(
-        second_all, cot_all, routed, gate_weight, up_weight, down_weight
-    )
-    second_grad = lax.psum_scatter(dx, "seq", scatter_dimension=0, tiled=True)
-
-    tokens = second_all.reshape(devices * rows, features)
+    cos_all, sin_all, routed = lax.optimization_barrier((cos_all, sin_all, routed))
+    x_all, cot_then, cos_all, sin_all, routed = lax.optimization_barrier(
+        (x_all, cot, cos_all, sin_all, routed)
+    )
+    cot_all = lax.all_gather(cot_then, "seq", axis=0)
+
+    group = (seq_place // copies).astype(jnp.int32).reshape(1)
+    qkv, first_all = qkv_call(
+        group, x_all, gain_one, cos_all, sin_all, query_weight, key_weight, value_weight
+    )
+    qkv = qkv.reshape(devices, micro, per_device, 2 * pair)
+    mix = attend_call(qkv)
+    mix = unspread(mix.reshape(devices, rows, pair))
+    mixed, middle, second_low = post_call(mix, output_weight, x, gain_two)
+
+    chips = devices // 2
+    chip, core = seq_place // 2, seq_place % 2
+    onward = [(i, (i + 2) % devices) for i in range(devices)]
+    held, kept, running = second_low, (), None
+    for hop in range(chips):
+        following = lax.ppermute(held, "seq", onward) if hop < chips - 1 else None
+        other = swap(held, "seq", 1)
+        source = 2 * ((chip - hop) % chips)
+        place = jnp.stack([source + core, source + 1 - core]).astype(jnp.int32)
+        dx, *kept = expert_call(
+            hop, place, held, other, cot_all, routed, gate_weight, up_weight, down_weight, kept
+        )
+        if following is not None:
+            following, dx = lax.optimization_barrier((following, dx))
+        part = dx[0].astype(f32) + swap(dx[1], "seq", 1).astype(f32)
+        if hop == 0:
+            own_part = part
+        else:
+            if running is not None:
+                part = part + running.astype(f32)
+            part = part.astype(bf16)
+            if following is not None:
+                part, following = lax.optimization_barrier((part, following))
+            running = lax.ppermute(part, "seq", onward)
+        held = following
+    second_grad = (own_part + running.astype(f32)).astype(bf16)
+    moe_all, tokens, hidden, gate_low, up_low, slot_grad = kept
+
     gate_term = jnp.einsum("td,etf->edf", tokens, gate_low, preferred_element_type=f32)
     up_term = jnp.einsum("td,etf->edf", tokens, up_low, preferred_element_type=f32)
     down_term = jnp.einsum("etf,etd->efd", hidden, slot_grad, preferred_element_type=f32)
-    moe_all = moe_call(hidden, routed, down_weight)
-    gate_sum = sum_over(gate_term.astype(bf16), "dp", dp_bits)
-    up_sum = sum_over(up_term.astype(bf16), "dp", dp_bits[::-1])
-    down_low = down_term.astype(bf16)
+    gate_term, up_term, down_low, second_grad = lax.optimization_barrier(
+        (gate_term.astype(bf16), up_term.astype(bf16), down_term.astype(bf16), second_grad)
+    )
     cut = local_experts // 2
-    down_sum = jnp.concatenate(
-        [
-            sum_over(down_low[:cut], "dp", dp_bits),
-            sum_over(down_low[cut:], "dp", dp_bits[::-1]),
-        ],
-        axis=0,
-    )
+    sums = [
+        (gate_term.reshape(-1, gate_term.shape[-1]), dp_bits),
+        (up_term.reshape(-1, up_term.shape[-1]), dp_bits[::-1]),
+        (down_low[:cut].reshape(-1, features), dp_bits),
+        (down_low[cut:].reshape(-1, features), dp_bits[::-1]),
+    ]
+    pieces = [half_sum(values, "dp", bits[0]) for values, bits in sums]
 
     mg_send, proj, middle_grad, gain_two_part = turn_call(
         second_grad, middle, gain_two, cot, output_weight, groups
     )
     mg = spread(mg_send)
     dense = output_weight_call(mixed, proj, gain_two_part, devices)
-    mg, dense, moe_all = lax.optimization_barrier((mg, dense, moe_all))
+    mg, dense, moe_all, *pieces = lax.optimization_barrier((mg, dense, moe_all, *pieces))
+    for at in range(1, len(dp_bits)):
+        pieces = [half_sum(p, "dp", bits[at]) for p, (_, bits) in zip(pieces, sums)]
     dense = lax.psum_scatter(dense, "seq", scatter_dimension=0)
-    moe = lax.psum_scatter(moe_all, "seq", scatter_dimension=0, tiled=True)
+    moe = lax.psum_scatter(moe_all, "seq", scatter_dimension=0)
     layer_output = (middle + residual_scale * moe.astype(f32)).astype(bf16)
     for bit in dp_bits:
         dense = (dense.astype(f32) + swap(dense, "dp", bit).astype(f32)).astype(bf16)
@@ -638,6 +650,11 @@
         cos_all.reshape(table_shape),
         sin_all.reshape(table_shape),
     )
+    dqkv, *pieces = lax.optimization_barrier((dqkv, *pieces))
+    for at in range(len(dp_bits))[::-1]:
+        pieces = [join_halves(p, "dp", bits[at]) for p, (_, bits) in zip(pieces, sums)]
+    gate_sum, up_sum = pieces[0].reshape(gate_term.shape), pieces[1].reshape(up_term.shape)
+    down_sum = jnp.concatenate(pieces[2:], axis=0).reshape(down_low.shape)
     d_all = dqkv.reshape(devices * rows, 2 * pair)
     first_tokens = first_all.reshape(devices * rows, features)
     part = lax.dot_general(first_tokens, d_all, TN, preferred_element_type=f32).astype(bf16)

time: 572 us -> 509 us (0.89)
  waiting for transfers between devices: 284 us -> 208 us
  Pallas kernels: 76.3 us -> 95 us
  blocking collectives: 24.8 us -> 42.9 us
  local copies, waits for them, and re-layouts: 54.9 us -> 39.7 us
  other arithmetic: 52 us -> 40.2 us
    all_gather x2 -> x1, waiting for transfers between devices: 95.5 us -> 36.6 us  [body(): x_all = lax.all_gather(x_then, 'seq', axis=0)]
    ppermute x20 -> x28, waiting for transfers between devices: 132 us -> 75.2 us  [swap(): lax.ppermute(values, axis, [(i, i ^ bit) for i in range(lax.axis_size(axi...]
    reduce_scatter x2 -> x1, waiting for transfers between devices: 48.9 us -> 0.01 us  [body(): moe = lax.psum_scatter(moe_all, 'seq', scatter_dimension=0)]
    all_gather x1, waiting for transfers between devices: 0.01 us -> 45.1 us  [body(): wide = lax.all_gather(part, ('dp', 'seq'), axis=0)]
    ppermute x0 -> x6, waiting for transfers between devices: none -> 26.1 us  [the longest x3 21.5 us: body(): running = lax.ppermute(part, 'seq', onward)]
    all_gather x1, waiting for transfers between devices: 0.01 us -> 24.2 us  [body(): dense = lax.all_gather(dense, 'seq', axis=0).astype(f32)]
    pallas_call x2 -> x4, Pallas kernels: 35.4 us -> 50.6 us  [expert_call(): pl.pallas_call(expert_kernel, grid_spec=pltpu.PrefetchScalarGridSpec(num_...]
    unnamed x120 -> x86, local copies, waits for them, and re-layouts: 46.9 us -> 32.1 us
  transfers between devices with their start and end apart: 31 -> 42, of which waited for: 18 -> 21; matrix products, arithmetic and copies ran while one was open for 16% -> 14% of each run, Pallas kernels for 8% -> 19%
where the time goes in v3:
time: 509 us; the launch traced here: 499 us
  waiting for transfers between devices  208 us (41%)
  Pallas kernels  95 us (19%)
  blocking collectives  42.9 us (8%)
  other arithmetic  40.2 us (8%)
  local copies, waits for them, and re-layouts  39.7 us (8%)
  starting transfers between devices  37.3 us (7%)
  matrix products  21.7 us (4%)
  between operations  15 us (3%)
    ppermute x28, waiting for transfers between devices, swap(): lax.ppermute(values, axis, [(i, i ^ bit) for i in range(lax.axis_size(axi...  75.2 us
    pallas_call x4, Pallas kernels, expert_call(): pl.pallas_call(expert_kernel, grid_spec=pltpu.PrefetchScalarGridSpec(num_...  50.6 us
    all_gather x1, waiting for transfers between devices, body(): wide = lax.all_gather(part, ('dp', 'seq'), axis=0)  45.1 us
    all_gather x1, waiting for transfers between devices, body(): x_all = lax.all_gather(x_then, 'seq', axis=0)  36.6 us
    unnamed x86, local copies, waits for them, and re-layouts  32.1 us
    all_to_all x1, blocking collectives, unspread(): return lax.all_to_all(blocks, 'seq', 0, 0, tiled=True)[::copies]  31.2 us
    ppermute x28, starting transfers between devices, swap(): lax.ppermute(values, axis, [(i, i ^ bit) for i in range(lax.axis_size(axi...  25.5 us
    all_gather x1, waiting for transfers between devices, body(): dense = lax.all_gather(dense, 'seq', axis=0).astype(f32)  24.2 us
  transfers between devices with their start and end apart: 42, of which 21 were waited for; matrix products, arithmetic and copies ran while one was open for 14% of the time, Pallas kernels for 19%

profile of v3, /device:TPU:0, one launch (start us, length us, event | category | flops | bytes accessed | tf_op | source)
XLA Modules:
  0.0 499.3 jit_solution(16605085842946908075)
XLA Ops:
  7.9 11.7 %all_to_all.24 = s32[8,1,256]{2,1,0:T(1,128)S(1)} all-to-all(s32[8,1,256]{2,1,0:T(1,128)S(1)} %broadcast_in_dim.24), channel_id=1, replica_groups=mesh['dp'=4,'seq'=8] {'seq'}, dimensions={0} | all-to-all | bytes 16384 | tf_op jit(solution)/shard_map/all_to_all | solution.py:556
  21.9 3.7 fusion.20
  25.6 3.0 pad_maximum_fusion.1
  28.6 36.6 %all-gather.9.cloned.1.call-done = bf16[2048,1024]{1,0:T(8,128)(2,1)} async-done(((bf16[256,1024]{1,0:T(8,128)(2,1)}), bf16[2048,1024]{1,0:T(8,128)(2,1)}) %all-gather.9.cloned.1.call-update) | async-done | bytes 4194320 | tf_op jit(solution)/shard_map/all_gather | solution.py:560
  70.1 2.3 copy-done.16
  72.4 6.3 %norm_qkv_rope.1 = (bf16[8,256,256]{2,1,0:T(8,128)(2,1)S(1)}, bf16[8,256,1024]{2,1,0:T(8,128)(2,1)S(1)}) custom-call(s32[1]{0:T(128)} %bitcast.place_ref, bf16[8,256,1024]{2,1,0:T(8,128)(2,1)S(1)} %bitcast.128, f32[1,1024]{1,0:T(1,128)S(1)} %bitcast.133, f32[2048,128]{1,0:T(8,128)S(1)} %copy-done.12, f32[2048,128]{1,0:T(8,128)S(1)} %copy-done.13, ...), custom_call_target="tpu_custom_call" | custom-call | flops 1610612736 | bytes 14000000 | tf_op jit(solution)/shard_map/norm_qkv_rope/pallas_call | solution.py:91
  78.8 2.0 copy-done.27
  80.9 7.8 %attention_forward.1 = bf16[8,2,128,128]{3,2,1,0:T(8,128)(2,1)S(1)} custom-call(bf16[8,2,128,256]{3,2,1,0:T(8,128)(2,1)S(1)} %bitcast.139), custom_call_target="tpu_custom_call" | custom-call | flops 1073741824 | bytes 1572864 | tf_op jit(solution)/shard_map/attention_forward/pallas_call | solution.py:168
  88.7 31.2 %all_to_all.25.mix_ref = bf16[8,256,128]{2,1,0:T(8,128)(2,1)S(1)} all-to-all(bf16[8,256,128]{2,1,0:T(8,128)(2,1)S(1)} %bitcast.132), channel_id=1, replica_groups=mesh['dp'=4,'seq'=8] {'seq'}, dimensions={0} | all-to-all | bytes 1048576 | tf_op jit(solution)/shard_map/all_to_all | solution.py:550
  125.6 12.6 %experts.4 = (bf16[2,256,1024]{2,1,0:T(8,128)(2,1)S(1)}, bf16[8,256,1024]{2,1,0:T(8,128)(2,1)}, bf16[2048,1024]{1,0:T(8,128)(2,1)}, bf16[2,2048,512]{2,1,0:T(8,1...) custom-call(s32[2]{0:T(128)S(1)} %pad_add_fusion.1.place_ref, ...), custom_call_target="tpu_custom_call" | custom-call | flops 6442450944 | bytes 20000000 | tf_op jit(solution)/shard_map/experts/pallas_call | solution.py:303
  140.1 2.2 collective-permute-done.3.b_ref
  142.2 12.6 %experts.5 = (bf16[2,256,1024]{2,1,0:T(8,128)(2,1)S(1)}, bf16[8,256,1024]{2,1,0:T(8,128)(2,1)}, bf16[2048,1024]{1,0:T(8,128)(2,1)}, bf16[2,2048,512]{2,1,0:T(8,1...) custom-call(s32[2]{0:T(128)S(1)} %pad_add_fusion.2.place_ref, ...), custom_call_target="tpu_custom_call", output_to_operand_aliasing={{1}: (8, {}), {2}: (9, {}), {3}: (10, {}), {4}: (11, {}), {... | custom-call | flops 6442450944 | bytes 20000000 | tf_op jit(solution)/shard_map/experts/pallas_call | solution.py:303
  159.8 2.0 collective-permute-done.6.b_ref
  161.8 12.7 %experts.6 = (bf16[2,256,1024]{2,1,0:T(8,128)(2,1)S(1)}, bf16[8,256,1024]{2,1,0:T(8,128)(2,1)}, bf16[2048,1024]{1,0:T(8,128)(2,1)}, bf16[2,2048,512]{2,1,0:T(8,1...) custom-call(s32[2]{0:T(128)S(1)} %pad_add_fusion.3.place_ref, ...), custom_call_target="tpu_custom_call", output_to_operand_aliasing={{1}: (8, {}), {2}: (9, {}), {3}: (10, {}), {4}: (11, {}), {... | custom-call | flops 6442450944 | bytes 20000000 | tf_op jit(solution)/shard_map/experts/pallas_call | solution.py:303
  174.4 2.2 collective-permute-done.5.a_ref
  176.7 10.5 %collective-permute-done.8 = bf16[256,1024]{1,0:T(8,128)(2,1)S(1)} collective-permute-done((bf16[256,1024]{1,0:T(8,128)(2,1)}, bf16[256,1024]{1,0:T(8,128)(2,1)S(1)}, u32[]{:S(2)}, u32[]{:S(2)}) %collective-permute-start.8) | collective-permute-done | bytes 524320 | tf_op jit(solution)/shard_map/ppermute | solution.py:608
  190.5 12.7 %experts.7 = (bf16[2,256,1024]{2,1,0:T(8,128)(2,1)S(1)}, bf16[8,256,1024]{2,1,0:T(8,128)(2,1)}, bf16[2048,1024]{1,0:T(8,128)(2,1)}, bf16[2,2048,512]{2,1,0:T(8,1...) custom-call(s32[2]{0:T(128)S(1)} %pad_add_fusion.place_ref, ...), custom_call_target="tpu_custom_call", output_to_operand_aliasing={{1}: (8, {}), {2}: (9, {}), {3}: (10, {}), {4}: (11, {}), {... | custom-call | flops 6442450944 | bytes 20000000 | tf_op jit(solution)/shard_map/experts/pallas_call | solution.py:303
  203.5 9.5 %convert_bitcast_fusion = bf16[2,1024,512]{1,2,0:T(8,128)(2,1)} fusion(bf16[2,2048,512]{2,1,0:T(8,128)(2,1)} %get-tuple-element.132, bf16[2048,1024]{1,0:T(8,128)(2,1)} %get-tuple-element.131), kind=kOutput, calls=%fused_computation.11 | convolution fusion | flops 4296015872 | bytes 10485760 | tf_op jit(solution)/shard_map/td,etf->edf/dot_general | solution.py:614
  212.9 4.7 convert_bitcast_fusion.1
  219.9 4.9 convolution_convert_fusion
  224.9 11.0 %collective-permute-done.13 = bf16[256,1024]{1,0:T(8,128)(2,1)S(1)} collective-permute-done((bf16[256,1024]{1,0:T(8,128)(2,1)S(1)}, bf16[256,1024]{1,0:T(8,128)(2,1)S(1)}, u32[]{:S(2)}, u32[]{:S(2)}) %collective-permute-start.13) | collective-permute-done | bytes 524320 | tf_op jit(solution)/shard_map/ppermute | solution.py:608
  236.2 2.8 select_bitcast_fusion
  245.2 2.1 norm_back_project_back.1
  248.3 4.1 all-to-all-start.2
  252.5 4.3 output_weight_part.1
  256.8 18.3 %collective-permute-done.17 = bf16[256,1024]{1,0:T(8,128)(2,1)} collective-permute-done((bf16[256,1024]{1,0:T(8,128)(2,1)}, bf16[256,1024]{1,0:T(8,128)(2,1)}, u32[]{:S(2)}, u32[]{:S(2)}) %collective-permute-start.17) | collective-permute-done | bytes 524320 | tf_op jit(solution)/shard_map/ppermute | solution.py:497
  275.1 2.6 fusion.10
  286.7 14.3 %attention_backward.1 = bf16[8,2,128,256]{3,2,1,0:T(8,128)(2,1)} custom-call(bf16[8,2,128,256]{3,2,1,0:T(8,128)(2,1)} %bitcast.140, bf16[8,2,128,128]{3,2,1,0:T(8,128)(2,1)} %bitcast.44.grad_ref, f32[8,2,128,128]{3,2,1,0:T(8,128)} %bitcast.126, f32[8,2,128,128]{3,2,1,0:T(8,128)} %bitcast.127), custom_call_target="tpu_custom_call" | custom-call | flops 2684354560 | bytes 5242880 | tf_op jit(solution)/shard_map/attention_backward/pallas_call | solution.py:217
  303.3 2.6 convolution_convert_fusion.1
  307.5 4.8 collective-permute-done.22
  314.1 3.4 collective-permute-done.23
  320.1 5.3 %collective-permute-done.24 = bf16[144,1024]{1,0:T(8,128)(2,1)S(1)} collective-permute-done((bf16[144,1024]{1,0:T(8,128)(2,1)}, bf16[144,1024]{1,0:T(8,128)(2,1)S(1)}, u32[]{:S(2)}, u32[]{:S(2)}) %collective-permute-start.24) | collective-permute-done | bytes 294944 | tf_op jit(solution)/shard_map/ppermute | solution.py:497
  328.5 6.0 %collective-permute-done.25 = bf16[144,1024]{1,0:T(8,128)(2,1)S(1)} collective-permute-done((bf16[144,1024]{1,0:T(8,128)(2,1)S(1)}, bf16[144,1024]{1,0:T(8,128)(2,1)S(1)}, u32[]{:S(2)}, u32[]{:S(2)}) %collective-permute-start.25) | collective-permute-done | bytes 294944 | tf_op jit(solution)/shard_map/ppermute | solution.py:497
  339.0 6.3 %all-to-all-start.3 = ((bf16[8,256,256]{2,1,0:T(8,128)(2,1)}), bf16[8,256,256]{2,1,0:T(8,128)(2,1)}, u32[]{:S(2)}, u32[]{:S(2)}) async-start(bf16[8,256,256]{2,1,0:T(8,128)(2,1)} %bitcast.47), calls=%async_computation.4 | async-start | bytes 2097152 | tf_op jit(solution)/shard_map/all_to_all | solution.py:550
  351.2 9.0 %collective-permute-done.31 = bf16[256,1024]{1,0:T(8,128)(2,1)S(1)} collective-permute-done((bf16[256,1024]{1,0:T(8,128)(2,1)S(1)}, bf16[256,1024]{1,0:T(8,128)(2,1)S(1)}, u32[]{:S(2)}, u32[]{:S(2)}) %collective-permute-start.31) | collective-permute-done | bytes 524320 | tf_op jit(solution)/shard_map/ppermute | solution.py:497
  362.2 2.5 convert.22
  364.7 18.8 %collective-permute-done.29 = bf16[1024,512]{0,1:T(8,128)(2,1)S(1)} collective-permute-done((bf16[1024,512]{0,1:T(8,128)(2,1)S(1)}, bf16[1024,512]{0,1:T(8,128)(2,1)S(1)}, u32[]{:S(2)}, u32[]{:S(2)}) %collective-permute-start.29) | collective-permute-done | bytes 1048608 | tf_op jit(solution)/shard_map/ppermute | solution.py:497
  384.0 2.6 maximum_convert_fusion.1
  386.6 5.3 %copy.83 = f32[2048,512]{1,0:T(8,128)} copy(f32[2048,512]{0,1:T(8,128)} %maximum_convert_fusion.1) | data formatting | bytes 8388608
  392.4 2.6 maximum_convert_fusion
  395.0 5.5 %copy.82 = f32[2048,512]{1,0:T(8,128)} copy(f32[2048,512]{0,1:T(8,128)} %maximum_convert_fusion) | data formatting | bytes 8388608
  404.0 3.8 input_gradient.1
  407.8 2.3 fusion.19
  410.1 45.1 %all-gather.13.cloned.1.call-done = bf16[8192,256]{1,0:T(8,128)(2,1)} async-done(((bf16[256,256]{1,0:T(8,128)(2,1)}), bf16[8192,256]{1,0:T(8,128)(2,1)}) %all-gather.13.cloned.1.call-update) | async-done | bytes 4194320 | tf_op jit(solution)/shard_map/all_gather | solution.py:663
  456.4 2.2 copy-done.17
  458.6 4.1 attention_weights_out.1
  462.7 24.2 %all-gather.15.cloned.1.call-done = bf16[1152,1024]{1,0:T(8,128)(2,1)} async-done(((bf16[144,1024]{1,0:T(8,128)(2,1)}), bf16[1152,1024]{1,0:T(8,128)(2,1)}) %all-gather.15.cloned.1.call-update) | async-done | bytes 2359312 | tf_op jit(solution)/shard_map/all_gather | solution.py:641
  486.9 4.1 slice.138
  (208 shorter events, 73.3 us)
Async XLA Ops:
  7.2 58.0 %all-gather.9.cloned.1.call-start = ((), (), s32[]{:S(2)}) async-start(), calls=%async_computation.8 | async-start | bytes 4718592 | tf_op jit(solution)/shard_map/all_gather | solution.py:560
  19.6 105.9 %all-gather.11.cloned.1.call-start = ((), (), s32[]{:S(2)}) async-start(), calls=%async_computation.9 | async-start | bytes 4718592 | tf_op jit(solution)/shard_map/all_gather | solution.py:574
  21.9 43.3 %copy-start.1 = (bf16[1024,1024]{1,0:T(8,128)(2,1)S(1)}, bf16[1024,1024]{1,0:T(8,128)(2,1)}, u32[]{:S(2)}) copy-start(bf16[1024,1024]{1,0:T(8,128)(2,1)} %wq_ref.5) | copy-start | bytes 6291460
  21.9 43.3 %copy-start.25 = (f32[1024]{0:T(1024)S(1)}, f32[1024]{0:T(1024)}, u32[]{:S(2)}) copy-start(f32[1024]{0:T(1024)} %param.15) | copy-start | bytes 12292
  80.9 39.0 %copy-start.8 = (bf16[1024,1024]{1,0:T(8,128)(2,1)S(1)}, bf16[1024,1024]{1,0:T(8,128)(2,1)}, u32[]{:S(2)}) copy-start(bf16[1024,1024]{1,0:T(8,128)(2,1)} %wo_ref.3) | copy-start | bytes 6291460
  80.9 39.0 %copy-start.10 = (bf16[2,1,128,1024]{3,2,1,0:T(8,128)(2,1)S(1)}, bf16[2,1,128,1024]{3,2,1,0:T(8,128)(2,1)}, u32[]{:S(2)}) copy-start(bf16[2,1,128,1024]{3,2,1,0:T(8,128)(2,1)} %param.14) | copy-start | bytes 1572868
  80.9 39.0 %copy-start.26 = (f32[1024]{0:T(1024)S(1)}, f32[1024]{0:T(1024)}, u32[]{:S(2)}) copy-start(f32[1024]{0:T(1024)} %param.20) | copy-start | bytes 12292
  80.9 44.7 %copy-start = (bf16[2,1024,512]{2,1,0:T(8,128)(2,1)S(1)}, bf16[2,1024,512]{2,1,0:T(8,128)(2,1)}, u32[]{:S(2)}) copy-start(bf16[2,1024,512]{2,1,0:T(8,128)(2,1)} %wg_ref.7) | copy-start | bytes 6291460
  123.3 2.3 collective-permute-start.1
  123.6 16.4 %collective-permute-start = (bf16[256,1024]{1,0:T(8,128)(2,1)}, bf16[256,1024]{1,0:T(8,128)(2,1)}, u32[]{:S(2)}, u32[]{:S(2)}) collective-permute-start(bf16[256,1024]{1,0:T(8,128)(2,1)} %get-tuple-element.98.a_ref), channel_id=1, source_target_pairs={{0,2},{1,3},{2,4},{3,5},{4,6},{5,7},{6,0},{7,1},{8,10},{9,11},{10,... | collective-permute-start | bytes 1572872 | tf_op jit(solution)/shard_map/ppermute | solution.py:590
  140.0 2.3 collective-permute-start.3
  140.1 16.4 %collective-permute-start.2 = (bf16[256,1024]{1,0:T(8,128)(2,1)}, bf16[256,1024]{1,0:T(8,128)(2,1)}, u32[]{:S(2)}, u32[]{:S(2)}) collective-permute-start(bf16[256,1024]{1,0:T(8,128)(2,1)} %collective-permute-done.a_ref), channel_id=1, source_target_pairs={{0,2},{1,3},{2,4},{3,5},{4,6},{5,7},{6,0},{7,1},{8,10},{9,11},{10,... | collective-permute-start | bytes 1572872 | tf_op jit(solution)/shard_map/ppermute | solution.py:590
  156.6 2.0 collective-permute-start.4
  159.5 2.3 collective-permute-start.6
  159.7 16.9 %collective-permute-start.5 = (bf16[256,1024]{1,0:T(8,128)(2,1)}, bf16[256,1024]{1,0:T(8,128)(2,1)}, u32[]{:S(2)}, u32[]{:S(2)}) collective-permute-start(bf16[256,1024]{1,0:T(8,128)(2,1)} %collective-permute-done.2.a_ref), channel_id=1, source_target_pairs={{0,2},{1,3},{2,4},{3,5},{4,6},{5,7},{6,0},{7,1},{8,10},{9,11},{10,... | collective-permute-start | bytes 1572872 | tf_op jit(solution)/shard_map/ppermute | solution.py:590
  159.7 27.4 %collective-permute-start.8 = (bf16[256,1024]{1,0:T(8,128)(2,1)}, bf16[256,1024]{1,0:T(8,128)(2,1)S(1)}, u32[]{:S(2)}, u32[]{:S(2)}) collective-permute-start(bf16[256,1024]{1,0:T(8,128)(2,1)} %fusion.18), channel_id=1, source_target_pairs={{0,2},{1,3},{2,4},{3,5},{4,6},{5,7},{6,0},{7,1},{8,10},{9,11},{10,... | collective-permute-start | bytes 1572872 | tf_op jit(solution)/shard_map/ppermute | solution.py:608
  176.6 10.5 %collective-permute-start.7 = (bf16[256,1024]{1,0:T(8,128)(2,1)S(1)}, bf16[256,1024]{1,0:T(8,128)(2,1)S(1)}, u32[]{:S(2)}, u32[]{:S(2)}) collective-permute-start(bf16[256,1024]{1,0:T(8,128)(2,1)S(1)} %slice_bitcast_fusion.2), channel_id=1, source_target_pairs={{0,1},{1,0},{2,3},{3,2},{4,5},{5,4},{6,7},{7,6},{8,9},{9,8},{10,11... | collective-permute-start | bytes 1572872 | tf_op jit(solution)/shard_map/ppermute | solution.py:497
  188.2 2.3 collective-permute-start.9
  189.4 35.4 %collective-permute-start.10 = (bf16[256,1024]{1,0:T(8,128)(2,1)S(1)}, bf16[256,1024]{1,0:T(8,128)(2,1)S(1)}, u32[]{:S(2)}, u32[]{:S(2)}) collective-permute-start(bf16[256,1024]{1,0:T(8,128)(2,1)S(1)} %slice_bitcast_fusion.1), channel_id=1, source_target_pairs={{0,1},{1,0},{2,3},{3,2},{4,5},{5,4},{6,7},{7,6},{8,9},{9,8},{10,11... | collective-permute-start | bytes 1572872 | tf_op jit(solution)/shard_map/ppermute | solution.py:497
  190.0 27.7 %collective-permute-start.12 = (bf16[256,1024]{1,0:T(8,128)(2,1)}, bf16[256,1024]{1,0:T(8,128)(2,1)}, u32[]{:S(2)}, u32[]{:S(2)}) collective-permute-start(bf16[256,1024]{1,0:T(8,128)(2,1)} %fusion.17), channel_id=1, source_target_pairs={{0,2},{1,3},{2,4},{3,5},{4,6},{5,7},{6,0},{7,1},{8,10},{9,11},{10,... | collective-permute-start | bytes 1572872 | tf_op jit(solution)/shard_map/ppermute | solution.py:608
  203.2 14.5 %collective-permute-start.11 = (bf16[256,1024]{1,0:T(8,128)(2,1)S(1)}, bf16[256,1024]{1,0:T(8,128)(2,1)S(1)}, u32[]{:S(2)}, u32[]{:S(2)}) collective-permute-start(bf16[256,1024]{1,0:T(8,128)(2,1)S(1)} %slice_bitcast_fusion), channel_id=1, source_target_pairs={{0,1},{1,0},{2,3},{3,2},{4,5},{5,4},{6,7},{7,6},{8,9},{9,8},{10,11... | collective-permute-start | bytes 1572872 | tf_op jit(solution)/shard_map/ppermute | solution.py:497
  219.4 16.4 %collective-permute-start.13 = (bf16[256,1024]{1,0:T(8,128)(2,1)S(1)}, bf16[256,1024]{1,0:T(8,128)(2,1)S(1)}, u32[]{:S(2)}, u32[]{:S(2)}) collective-permute-start(bf16[256,1024]{1,0:T(8,128)(2,1)S(1)} %fusion.13), channel_id=1, source_target_pairs={{0,2},{1,3},{2,4},{3,5},{4,6},{5,7},{6,0},{7,1},{8,10},{9,11},{10,... | collective-permute-start | bytes 1572872 | tf_op jit(solution)/shard_map/ppermute | solution.py:608
  238.9 38.8 %collective-permute-start.15 = (bf16[1024,512]{0,1:T(8,128)(2,1)}, bf16[1024,512]{0,1:T(8,128)(2,1)}, u32[]{:S(2)}, u32[]{:S(2)}) collective-permute-start(bf16[1024,512]{0,1:T(8,128)(2,1)} %select_bitcast_fusion), channel_id=1, source_target_pairs={{0,16},{8,24},{16,0},{24,8},{1,17},{9,25},{17,1},{25,9},{2,18},{10... | collective-permute-start | bytes 3145736 | tf_op jit(solution)/shard_map/ppermute | solution.py:497
  241.5 15.3 %collective-permute-start.16 = (bf16[256,1024]{1,0:T(8,128)(2,1)}, bf16[256,1024]{1,0:T(8,128)(2,1)}, u32[]{:S(2)}, u32[]{:S(2)}) collective-permute-start(bf16[256,1024]{1,0:T(8,128)(2,1)} %get-tuple-element.216), channel_id=1, source_target_pairs={{0,8},{8,0},{16,24},{24,16},{1,9},{9,1},{17,25},{25,17},{2,10},{10... | collective-permute-start | bytes 1572872 | tf_op jit(solution)/shard_map/ppermute | solution.py:497
  243.0 32.1 %collective-permute-start.17 = (bf16[256,1024]{1,0:T(8,128)(2,1)}, bf16[256,1024]{1,0:T(8,128)(2,1)}, u32[]{:S(2)}, u32[]{:S(2)}) collective-permute-start(bf16[256,1024]{1,0:T(8,128)(2,1)} %get-tuple-element.215), channel_id=1, source_target_pairs={{0,16},{8,24},{16,0},{24,8},{1,17},{9,25},{17,1},{25,9},{2,18},{10... | collective-permute-start | bytes 1572872 | tf_op jit(solution)/shard_map/ppermute | solution.py:497
  244.6 34.8 %collective-permute-start.14 = (bf16[1024,512]{0,1:T(8,128)(2,1)}, bf16[1024,512]{0,1:T(8,128)(2,1)}, u32[]{:S(2)}, u32[]{:S(2)}) collective-permute-start(bf16[1024,512]{0,1:T(8,128)(2,1)} %select_bitcast_fusion.1), channel_id=1, source_target_pairs={{0,8},{8,0},{16,24},{24,16},{1,9},{9,1},{17,25},{25,17},{2,10},{10... | collective-permute-start | bytes 3145736 | tf_op jit(solution)/shard_map/ppermute | solution.py:497
  248.3 32.9 %all-to-all-start.2 = ((bf16[8,256,128]{2,1,0:T(8,128)(2,1)}), bf16[8,256,128]{2,1,0:T(8,128)(2,1)}, u32[]{:S(2)}, u32[]{:S(2)}) async-start(bf16[8,256,128]{2,1,0:T(8,128)(2,1)} %get-tuple-element.139), calls=%async_computation.2 | async-start | bytes 1048576 | tf_op jit(solution)/shard_map/all_to_all | solution.py:547
  252.5 65.9 %reduce-scatter.5.cloned.1.call-start = ((), (), s32[]{:S(2)}) async-start(), calls=%async_computation.7 | async-start | bytes 2654208 | tf_op jit(solution)/shard_map/reduce_scatter | solution.py:636
  281.2 126.5 %reduce-scatter.3.cloned.1.call-start = ((), (), s32[]{:S(2)}) async-start(), calls=%async_computation.6 | async-start | bytes 4718592 | tf_op jit(solution)/shard_map/reduce_scatter | solution.py:637
  281.8 173.4 %all-gather.13.cloned.1.call-start = ((), (), s32[]{:S(2)}) async-start(), calls=%async_computation.10 | async-start | bytes 4325376 | tf_op jit(solution)/shard_map/all_gather | solution.py:663
  282.2 18.8 %collective-permute-start.21 = (bf16[128,1024]{1,0:T(8,128)(2,1)S(1)}, bf16[128,1024]{1,0:T(8,128)(2,1)S(1)}, u32[]{:S(2)}, u32[]{:S(2)}) collective-permute-start(bf16[128,1024]{1,0:T(8,128)(2,1)S(1)} %broadcast_select_fusion.17), channel_id=1, source_target_pairs={{0,8},{8,0},{16,24},{24,16},{1,9},{9,1},{17,25},{25,17},{2,10},{10... | collective-permute-start | bytes 786440 | tf_op jit(solution)/shard_map/ppermute | solution.py:497
  283.9 17.3 %collective-permute-start.20 = (bf16[128,1024]{1,0:T(8,128)(2,1)S(1)}, bf16[128,1024]{1,0:T(8,128)(2,1)S(1)}, u32[]{:S(2)}, u32[]{:S(2)}) collective-permute-start(bf16[128,1024]{1,0:T(8,128)(2,1)S(1)} %broadcast_select_fusion.20), channel_id=1, source_target_pairs={{0,16},{8,24},{16,0},{24,8},{1,17},{9,25},{17,1},{25,9},{2,18},{10... | collective-permute-start | bytes 786440 | tf_op jit(solution)/shard_map/ppermute | solution.py:497
  285.4 16.6 %collective-permute-start.19 = (bf16[512,512]{0,1:T(8,128)(2,1)S(1)}, bf16[512,512]{0,1:T(8,128)(2,1)S(1)}, u32[]{:S(2)}, u32[]{:S(2)}) collective-permute-start(bf16[512,512]{0,1:T(8,128)(2,1)S(1)} %broadcast_select_fusion.10), channel_id=1, source_target_pairs={{0,8},{8,0},{16,24},{24,16},{1,9},{9,1},{17,25},{25,17},{2,10},{10... | collective-permute-start | bytes 1572872 | tf_op jit(solution)/shard_map/ppermute | solution.py:497
  286.1 16.1 %collective-permute-start.18 = (bf16[512,512]{0,1:T(8,128)(2,1)S(1)}, bf16[512,512]{0,1:T(8,128)(2,1)S(1)}, u32[]{:S(2)}, u32[]{:S(2)}) collective-permute-start(bf16[512,512]{0,1:T(8,128)(2,1)S(1)} %broadcast_select_fusion.13), channel_id=1, source_target_pairs={{0,16},{8,24},{16,0},{24,8},{1,17},{9,25},{17,1},{25,9},{2,18},{10... | collective-permute-start | bytes 1572872 | tf_op jit(solution)/shard_map/ppermute | solution.py:497
  306.0 6.4 %collective-permute-start.22 = (bf16[512,256]{1,0:T(8,128)(2,1)S(1)}, bf16[512,256]{1,0:T(8,128)(2,1)S(1)}, u32[]{:S(2)}, u32[]{:S(2)}) collective-permute-start(bf16[512,256]{1,0:T(8,128)(2,1)S(1)} %broadcast_select_fusion.14), channel_id=1, source_target_pairs={{0,16},{8,24},{16,0},{24,8},{1,17},{9,25},{17,1},{25,9},{2,18},{10... | collective-permute-start | bytes 786440 | tf_op jit(solution)/shard_map/ppermute | solution.py:497
  312.5 5.0 %collective-permute-start.23 = (bf16[256,256]{1,0:T(8,128)(2,1)S(1)}, bf16[256,256]{1,0:T(8,128)(2,1)S(1)}, u32[]{:S(2)}, u32[]{:S(2)}) collective-permute-start(bf16[256,256]{1,0:T(8,128)(2,1)S(1)} %broadcast_select_fusion.21), channel_id=1, source_target_pairs={{0,8},{8,0},{16,24},{24,16},{1,9},{9,1},{17,25},{25,17},{2,10},{10... | collective-permute-start | bytes 393224 | tf_op jit(solution)/shard_map/ppermute | solution.py:497
  318.3 168.6 %all-gather.15.cloned.1.call-start = ((), (), s32[]{:S(2)}) async-start(), calls=%async_computation.11 | async-start | bytes 2654208 | tf_op jit(solution)/shard_map/all_gather | solution.py:641
  318.4 7.0 %collective-permute-start.24 = (bf16[144,1024]{1,0:T(8,128)(2,1)}, bf16[144,1024]{1,0:T(8,128)(2,1)S(1)}, u32[]{:S(2)}, u32[]{:S(2)}) collective-permute-start(bf16[144,1024]{1,0:T(8,128)(2,1)} %bitcast.155), channel_id=1, source_target_pairs={{0,8},{8,0},{16,24},{24,16},{1,9},{9,1},{17,25},{25,17},{2,10},{10... | collective-permute-start | bytes 884744 | tf_op jit(solution)/shard_map/ppermute | solution.py:497
  326.4 8.1 %collective-permute-start.25 = (bf16[144,1024]{1,0:T(8,128)(2,1)S(1)}, bf16[144,1024]{1,0:T(8,128)(2,1)S(1)}, u32[]{:S(2)}, u32[]{:S(2)}) collective-permute-start(bf16[144,1024]{1,0:T(8,128)(2,1)S(1)} %add_convert_fusion.3), channel_id=1, source_target_pairs={{0,16},{8,24},{16,0},{24,8},{1,17},{9,25},{17,1},{25,9},{2,18},{10... | collective-permute-start | bytes 884744 | tf_op jit(solution)/shard_map/ppermute | solution.py:497
  328.1 17.2 %collective-permute-start.30 = (bf16[128,1024]{1,0:T(8,128)(2,1)S(1)}, bf16[128,1024]{1,0:T(8,128)(2,1)S(1)}, u32[]{:S(2)}, u32[]{:S(2)}) collective-permute-start(bf16[128,1024]{1,0:T(8,128)(2,1)S(1)} %copy-done.38), channel_id=1, source_target_pairs={{0,16},{8,24},{16,0},{24,8},{1,17},{9,25},{17,1},{25,9},{2,18},{10... | collective-permute-start | bytes 786440 | tf_op jit(solution)/shard_map/ppermute | solution.py:497
  335.3 11.5 %collective-permute-start.32 = (bf16[128,1024]{1,0:T(8,128)(2,1)S(1)}, bf16[128,1024]{1,0:T(8,128)(2,1)S(1)}, u32[]{:S(2)}, u32[]{:S(2)}) collective-permute-start(bf16[128,1024]{1,0:T(8,128)(2,1)S(1)} %add_convert_fusion.5), channel_id=1, source_target_pairs={{0,8},{8,0},{16,24},{24,16},{1,9},{9,1},{17,25},{25,17},{2,10},{10... | collective-permute-start | bytes 786440 | tf_op jit(solution)/shard_map/ppermute | solution.py:497
  336.9 10.7 %collective-permute-start.28 = (bf16[512,512]{0,1:T(8,128)(2,1)S(1)}, bf16[512,512]{0,1:T(8,128)(2,1)S(1)}, u32[]{:S(2)}, u32[]{:S(2)}) collective-permute-start(bf16[512,512]{0,1:T(8,128)(2,1)S(1)} %add_convert_fusion), channel_id=1, source_target_pairs={{0,8},{8,0},{16,24},{24,16},{1,9},{9,1},{17,25},{25,17},{2,10},{10... | collective-permute-start | bytes 1572872 | tf_op jit(solution)/shard_map/ppermute | solution.py:497
  337.4 12.0 %collective-permute-start.26 = (bf16[512,512]{0,1:T(8,128)(2,1)S(1)}, bf16[512,512]{0,1:T(8,128)(2,1)S(1)}, u32[]{:S(2)}, u32[]{:S(2)}) collective-permute-start(bf16[512,512]{0,1:T(8,128)(2,1)S(1)} %add_convert_fusion.1), channel_id=1, source_target_pairs={{0,16},{8,24},{16,0},{24,8},{1,17},{9,25},{17,1},{25,9},{2,18},{10... | collective-permute-start | bytes 1572872 | tf_op jit(solution)/shard_map/ppermute | solution.py:497
  339.0 61.5 %all-to-all-start.3 = ((bf16[8,256,256]{2,1,0:T(8,128)(2,1)}), bf16[8,256,256]{2,1,0:T(8,128)(2,1)}, u32[]{:S(2)}, u32[]{:S(2)}) async-start(bf16[8,256,256]{2,1,0:T(8,128)(2,1)} %bitcast.47), calls=%async_computation.4 | async-start | bytes 2097152 | tf_op jit(solution)/shard_map/all_to_all | solution.py:550
  345.4 14.8 %collective-permute-start.31 = (bf16[256,1024]{1,0:T(8,128)(2,1)S(1)}, bf16[256,1024]{1,0:T(8,128)(2,1)S(1)}, u32[]{:S(2)}, u32[]{:S(2)}) collective-permute-start(bf16[256,1024]{1,0:T(8,128)(2,1)S(1)} %pad_maximum_fusion.5), channel_id=1, source_target_pairs={{0,8},{8,0},{16,24},{24,16},{1,9},{9,1},{17,25},{25,17},{2,10},{10... | collective-permute-start | bytes 1572872 | tf_op jit(solution)/shard_map/ppermute | solution.py:497
  346.9 14.8 %collective-permute-start.33 = (bf16[256,1024]{1,0:T(8,128)(2,1)S(1)}, bf16[256,1024]{1,0:T(8,128)(2,1)S(1)}, u32[]{:S(2)}, u32[]{:S(2)}) collective-permute-start(bf16[256,1024]{1,0:T(8,128)(2,1)S(1)} %pad_maximum_fusion.6), channel_id=1, source_target_pairs={{0,16},{8,24},{16,0},{24,8},{1,17},{9,25},{17,1},{25,9},{2,18},{10... | collective-permute-start | bytes 1572872 | tf_op jit(solution)/shard_map/ppermute | solution.py:497
  347.8 35.7 %collective-permute-start.29 = (bf16[1024,512]{0,1:T(8,128)(2,1)S(1)}, bf16[1024,512]{0,1:T(8,128)(2,1)S(1)}, u32[]{:S(2)}, u32[]{:S(2)}) collective-permute-start(bf16[1024,512]{0,1:T(8,128)(2,1)S(1)} %pad_maximum_fusion.4), channel_id=1, source_target_pairs={{0,16},{8,24},{16,0},{24,8},{1,17},{9,25},{17,1},{25,9},{2,18},{10... | collective-permute-start | bytes 3145736 | tf_op jit(solution)/shard_map/ppermute | solution.py:497
  349.6 42.3 %collective-permute-start.27 = (bf16[1024,512]{0,1:T(8,128)(2,1)S(1)}, bf16[1024,512]{0,1:T(8,128)(2,1)S(1)}, u32[]{:S(2)}, u32[]{:S(2)}) collective-permute-start(bf16[1024,512]{0,1:T(8,128)(2,1)S(1)} %pad_maximum_fusion.3), channel_id=1, source_target_pairs={{0,8},{8,0},{16,24},{24,16},{1,9},{9,1},{17,25},{25,17},{2,10},{10... | collective-permute-start | bytes 3145736 | tf_op jit(solution)/shard_map/ppermute | solution.py:497
  (35 other events, 241.0 us)
Sparse Core Ops, SparseCore 0:
  19.8 45.3 all-gather.8
  66.8 56.9 all-gather.10
  281.3 35.7 reduce-scatter.4
  319.8 65.7 reduce-scatter.2
  389.1 66.0 all-gather.12
  456.7 30.1 all-gather.14

commit v4 on v3

--- a/solution.py
+++ b/solution.py
@@ -37,7 +37,7 @@
 
 def cost(flops, nbytes, trans=0):
     return pl.CostEstimate(
-        flops=int(flops), bytes_accessed=int(nbytes), transcendentals=int(trans)
+        flops=int(flops / 8), bytes_accessed=int(nbytes / 8), transcendentals=int(trans / 8)
     )
 
 
@@ -111,7 +111,7 @@
             jax.ShapeDtypeStruct((blocks, rows, 2 * pair), bf16),
             jax.ShapeDtypeStruct((blocks, rows, features), bf16),
         ],
-        compiler_params=params(32, "arbitrary"),
+        compiler_params=params(58, "arbitrary"),
         cost_estimate=cost(6 * blocks * rows * features * pair, 14e6),
         name="norm_qkv_rope",
     )(group, x_all, gain, cos_all, sin_all, wq, wk, wv)
@@ -254,8 +254,10 @@
 
 
 def expert_kernel(place_ref, a_ref, b_ref, cot_ref, w_ref, wg_ref, wu_ref, wd_ref, *refs):
-    dx_ref, moe_ref, x_ref, h_ref, dg_ref, du_ref, sg_ref = refs[-7:]
+    dx_ref, x_ref, ha_ref, hb_ref, dg_ref, du_ref, sa_ref, sb_ref = refs[-8:]
     step = pl.program_id(0)
+    first, second = place_ref[2], place_ref[3]
+    half = sa_ref.shape[2]
 
     @pl.when(step == 0)
     def _():
@@ -268,27 +270,27 @@
     x = x_ref[...]
     cot = residual_scale * cot_ref[0].astype(f32)
     weight = w_ref[...]
-    total, made = None, None
+    total = None
     for e in range(wg_ref.shape[0]):
         gate = dot(x, wg_ref[e])
         up = dot(x, wu_ref[e])
         slot_grad = (weight[:, e : e + 1] * cot).astype(bf16)
-        sg_ref[e] = slot_grad
+        to_a, to_b = jnp.bitwise_xor(first, e), jnp.bitwise_xor(second, e)
+        sa_ref[to_a] = slot_grad[:, :half]
+        sb_ref[to_b] = slot_grad[:, half:]
         hidden_grad = dot_nt(slot_grad, wd_ref[e])
         sig = 1.0 / (1.0 + jnp.exp(-gate))
         silu = gate * sig
         hidden = (silu * up).astype(bf16)
-        h_ref[e] = hidden
+        ha_ref[to_a] = hidden
+        hb_ref[to_b] = hidden
         gate_grad = (hidden_grad * up * (sig * (1.0 + gate * (1.0 - sig)))).astype(bf16)
         up_grad = (hidden_grad * silu).astype(bf16)
-        dg_ref[e] = gate_grad
-        du_ref[e] = up_grad
+        dg_ref[to_a] = gate_grad
+        du_ref[to_b] = up_grad
         term = dot_nt(gate_grad, wg_ref[e]) + dot_nt(up_grad, wu_ref[e])
-        out = weight[:, e : e + 1] * dot(hidden, wd_ref[e])
         total = term if total is None else total + term
-        made = out if made is None else made + out
     dx_ref[0] = total.astype(bf16)
-    moe_ref[0] = made.astype(bf16)
 
 
 def expert_call(at, place, own, other, cot_all, weight, wg, wu, wd, kept):
@@ -296,7 +298,9 @@
     count, _, hidden = wg.shape
     tokens = blocks * rows
     inner = jax.ShapeDtypeStruct((count, tokens, hidden), bf16)
+    outer = jax.ShapeDtypeStruct((count, tokens, features // 2), bf16)
     inner_spec = pl.BlockSpec((count, rows, hidden), lambda s, place: (0, 2 * at + s, 0))
+    outer_spec = pl.BlockSpec((count, rows, features // 2), lambda s, place: (0, 2 * at + s, 0))
     fixed = lambda shape: pl.BlockSpec(shape, lambda s, place: (0,) * len(shape))
     any_spec = pl.BlockSpec(memory_space=pl.ANY)
     first = 8
@@ -317,28 +321,100 @@
             + [any_spec] * len(kept),
             out_specs=[
                 pl.BlockSpec((1, rows, features), lambda s, place: (s, 0, 0)),
-                pl.BlockSpec((1, rows, features), lambda s, place: (place[s], 0, 0)),
                 pl.BlockSpec((rows, features), lambda s, place: (2 * at + s, 0)),
-                inner_spec,
-                inner_spec,
-                inner_spec,
-                pl.BlockSpec((count, rows, features), lambda s, place: (0, 2 * at + s, 0)),
-            ],
+            ]
+            + [inner_spec] * 4
+            + [outer_spec] * 2,
         ),
         out_shape=[
             jax.ShapeDtypeStruct((2, rows, features), bf16),
-            jax.ShapeDtypeStruct((blocks, rows, features), bf16),
             jax.ShapeDtypeStruct((tokens, features), bf16),
             inner,
             inner,
             inner,
-            jax.ShapeDtypeStruct((count, tokens, features), bf16),
+            inner,
+            outer,
+            outer,
         ],
         input_output_aliases={first + i: 1 + i for i in range(len(kept))},
         compiler_params=params(48, "arbitrary"),
-        cost_estimate=cost(24 * rows * wg.size, 2e7, 2 * rows * hidden * count),
+        cost_estimate=cost(20 * rows * wg.size, 2e7, 2 * rows * hidden * count),
         name="experts",
     )(place, own, other, cot_all, weight, wg, wu, wd, *kept)
+
+
+def expert_out_kernel(at_ref, a_ref, b_ref, gate_ref, up_ref, down_ref):
+    rows = gate_ref.shape[1]
+    half = down_ref.shape[2] // 2
+    gate_ref[0] = a_ref[:rows].astype(f32)
+    up_ref[0] = b_ref[:rows].astype(f32)
+    down_ref[0, :, :half] = a_ref[rows:].astype(f32)
+    down_ref[0, :, half:] = b_ref[rows:].astype(f32)
+
+
+def expert_out_call(at, a, b, gate_shape, down_shape):
+    parts, held, width = a.shape
+    count = gate_shape[0]
+    per = parts // count
+    gate_rows, down_rows = gate_shape[1] // per, down_shape[1] // per
+    taken = lambda which: pl.BlockSpec(
+        (None, held, width), lambda r, at: (jnp.bitwise_xor(r, at[which]), 0, 0)
+    )
+    place = lambda r, at: (lax.div(r, per), lax.rem(r, per), 0)
+    return pl.pallas_call(
+        expert_out_kernel,
+        grid_spec=pltpu.PrefetchScalarGridSpec(
+            num_scalar_prefetch=1,
+            grid=(parts,),
+            in_specs=[taken(0), taken(1)],
+            out_specs=[
+                pl.BlockSpec((1, gate_rows, gate_shape[2]), place),
+                pl.BlockSpec((1, gate_rows, gate_shape[2]), place),
+                pl.BlockSpec((1, down_rows, down_shape[2]), place),
+            ],
+        ),
+        out_shape=[
+            jax.ShapeDtypeStruct(gate_shape, f32),
+            jax.ShapeDtypeStruct(gate_shape, f32),
+            jax.ShapeDtypeStruct(down_shape, f32),
+        ],
+        compiler_params=params(40, "arbitrary"),
+        cost_estimate=cost(0, 2e7),
+        name="expert_weights_out",
+    )(at, a, b)
+
+
+def moe_kernel(place_ref, h_ref, w_ref, wd_ref, out_ref):
+    weight = w_ref[...]
+    total = None
+    first = place_ref[pl.num_programs(0)]
+    for e in range(wd_ref.shape[0]):
+        term = weight[:, e : e + 1] * dot(h_ref[jnp.bitwise_xor(first, e)], wd_ref[e])
+        total = term if total is None else total + term
+    out_ref[0] = total.astype(bf16)
+
+
+def moe_call(place, hidden, weight, wd, blocks):
+    count, tokens, inner = hidden.shape
+    features = wd.shape[2]
+    rows = tokens // blocks
+    return pl.pallas_call(
+        moe_kernel,
+        grid_spec=pltpu.PrefetchScalarGridSpec(
+            num_scalar_prefetch=1,
+            grid=(blocks,),
+            in_specs=[
+                pl.BlockSpec((count, rows, inner), lambda s, place: (0, s, 0)),
+                pl.BlockSpec((rows, count), lambda s, place: (place[s], 0)),
+                pl.BlockSpec(wd.shape, lambda s, place: (0, 0, 0)),
+            ],
+            out_specs=pl.BlockSpec((1, rows, features), lambda s, place: (place[s], 0, 0)),
+        ),
+        out_shape=jax.ShapeDtypeStruct((blocks, rows, features), bf16),
+        compiler_params=params(32, "arbitrary"),
+        cost_estimate=cost(2 * tokens * wd.size, 1.1e7),
+        name="expert_outputs",
+    )(place, hidden, weight, wd)
 
 
 def turn_kernel(sg_ref, middle_ref, gain_ref, cot_ref, wo_ref, mg_ref, proj_ref, dmid_ref, dgain_ref):
@@ -405,6 +481,85 @@
         cost_estimate=cost(2 * rows * width * features, 4e6),
         name="output_weight_part",
     )(mixed, proj, dgain)
+
+
+def dense_out_kernel(
+    at_ref, own_ref, other_ref, wq_ref, wk_ref, wv_ref, gain_ref, dq_ref, dk_ref, dv_ref, dg_ref, wo_ref
+):
+    chips, _, width = own_ref.shape
+    rows = dq_ref.shape[0]
+    pair = width // 2
+    chip, core = at_ref[2], at_ref[3]
+    total = jnp.zeros((rows, pair), f32)
+    for k in range(chips):
+        source = lax.rem(chip - k + chips, chips)
+        a = jnp.where(core == 0, own_ref[k], other_ref[k]).astype(f32)
+        b = jnp.where(core == 0, other_ref[k], own_ref[k]).astype(f32)
+        q = jnp.concatenate([a[:rows, :pair], b[:rows, :pair]], axis=1)
+        cols = pl.ds(pl.multiple_of(source * width, width), width)
+        dq_ref[:, cols] = q
+        made = q * wq_ref[:, cols].astype(f32)
+        total += made[:, :pair] + made[:, pair:]
+        a_kv, b_kv = a[:rows, pair:], b[:rows, pair:]
+        lane = lax.broadcasted_iota(jnp.int32, a_kv.shape, 1)
+        key = jnp.where(lane < HEAD_DIM, a_kv, pltpu.roll(b_kv, HEAD_DIM, 1))
+        val = jnp.where(lane < HEAD_DIM, pltpu.roll(a_kv, HEAD_DIM, 1), b_kv)
+        cols = pl.ds(pl.multiple_of(source * pair, pair), pair)
+        dk_ref[:, cols] = key
+        dv_ref[:, cols] = val
+        total += key * wk_ref[:, cols].astype(f32) + val * wv_ref[:, cols].astype(f32)
+        wo_ref[2 * source, 0] = a[rows:]
+        wo_ref[2 * source + 1, 0] = b[rows:]
+    dg_ref[...] = jnp.sum(jnp.transpose(total), axis=0, keepdims=True) / gain_ref[...]
+
+
+def dense_out_call(at, own, other, wq, wk, wv, gain, wo_shape):
+    streams, parts, chips, held, width = own.shape
+    features = wq.shape[0]
+    groups = 2 * chips
+    rows = features // (streams * parts)
+    block_cols = wo_shape[1] // width
+    per_block = streams * parts // block_cols
+    wo_rows = wo_shape[0] // groups // per_block
+    by_rows = lambda w: pl.BlockSpec((rows, w.shape[1]), lambda s, r, at: (s * parts + r, 0))
+    taken = pl.BlockSpec(
+        (None, None, chips, held, width), lambda s, r, at: (s, jnp.bitwise_xor(r, at[s]), 0, 0, 0)
+    )
+    gain_spec = pl.BlockSpec((1, rows), lambda s, r, at: (0, s * parts + r))
+    outs = pl.pallas_call(
+        dense_out_kernel,
+        grid_spec=pltpu.PrefetchScalarGridSpec(
+            num_scalar_prefetch=1,
+            grid=(streams, parts),
+            in_specs=[taken, taken, by_rows(wq), by_rows(wk), by_rows(wv), gain_spec],
+            out_specs=[
+                by_rows(wq),
+                by_rows(wk),
+                by_rows(wv),
+                gain_spec,
+                pl.BlockSpec(
+                    (groups, 1, wo_rows, width),
+                    lambda s, r, at: (
+                        0,
+                        lax.rem(s * parts + r, per_block),
+                        0,
+                        lax.div(s * parts + r, per_block),
+                    ),
+                ),
+            ],
+        ),
+        out_shape=[
+            jax.ShapeDtypeStruct(wq.shape, f32),
+            jax.ShapeDtypeStruct(wk.shape, f32),
+            jax.ShapeDtypeStruct(wv.shape, f32),
+            jax.ShapeDtypeStruct((1, features), f32),
+            jax.ShapeDtypeStruct((groups, per_block, wo_rows, wo_shape[1]), f32),
+        ],
+        compiler_params=params(48, "arbitrary", "arbitrary"),
+        cost_estimate=cost(2 * wq.size, 2.4e7),
+        name="dense_weights_out",
+    )(at, own, other, wq, wk, wv, gain)
+    return (*outs[:4], outs[4].reshape(wo_shape))
 
 
 def weights_out_kernel(wide_ref, wq_ref, wk_ref, wv_ref, gain_ref, dq_ref, dk_ref, dv_ref, dg_ref):
@@ -499,18 +654,17 @@
 
 def half_sum(values, axis, bit):
     half = values.shape[0] // 2
-    upper = (lax.axis_index(axis) & bit) > 0
-    low, high = values[:half], values[half:]
-    came = swap(jnp.where(upper, low, high), axis, bit)
-    return (jnp.where(upper, high, low).astype(f32) + came.astype(f32)).astype(bf16)
-
-
-def join_halves(values, axis, bit):
-    came = swap(values, axis, bit)
-    upper = (lax.axis_index(axis) & bit) > 0
-    return jnp.concatenate(
-        [jnp.where(upper, came, values), jnp.where(upper, values, came)], axis=0
-    )
+    upper = ((lax.axis_index(axis) & bit) > 0).astype(jnp.int32)
+    came = swap(lax.dynamic_slice_in_dim(values, (1 - upper) * half, half), axis, bit)
+    mine = lax.dynamic_slice_in_dim(values, upper * half, half)
+    return (mine.astype(f32) + came.astype(f32)).astype(bf16)
+
+
+def join_parts(stream, axis, bits):
+    shape = stream.shape
+    for bit in bits[::-1]:
+        stream = jnp.stack([stream, swap(stream, axis, bit)])
+    return stream.reshape(-1, *shape)
 
 
 def body(
@@ -556,8 +710,7 @@
     pos_all = lax.all_to_all(
         jnp.broadcast_to(positions.reshape(1, rows), (devices, rows)), "seq", 0, 0, tiled=True
     )
-    x_then, pos_all = lax.optimization_barrier((x, pos_all))
-    x_all = lax.all_gather(x_then, "seq", axis=0)
+    x_all = lax.all_gather(x, "seq", axis=0)
     cos_all, sin_all = rope_tables(pos_all.reshape(-1), pair)
     mine = seq_place * local_experts + jnp.arange(local_experts, dtype=jnp.int32)
     ids = expert_ids[:, 0]
@@ -585,12 +738,17 @@
     chips = devices // 2
     chip, core = seq_place // 2, seq_place % 2
     onward = [(i, (i + 2) % devices) for i in range(devices)]
-    held, kept, running = second_low, (), None
+    dp_place = lax.axis_index("dp")
+    first_bit = dp_place & 1
+    last_bit = dp_place >> (len(dp_bits) - 1)
+    held, kept, running, places = second_low, (), None, []
     for hop in range(chips):
         following = lax.ppermute(held, "seq", onward) if hop < chips - 1 else None
         other = swap(held, "seq", 1)
         source = 2 * ((chip - hop) % chips)
-        place = jnp.stack([source + core, source + 1 - core]).astype(jnp.int32)
+        place = jnp.stack([source + core, source + 1 - core, 1 - first_bit, 1 - last_bit])
+        place = place.astype(jnp.int32)
+        places.append(place[:2])
         dx, *kept = expert_call(
             hop, place, held, other, cot_all, routed, gate_weight, up_weight, down_weight, kept
         )
@@ -605,44 +763,56 @@
             part = part.astype(bf16)
             if following is not None:
                 part, following = lax.optimization_barrier((part, following))
+            else:
+                part, kept = lax.optimization_barrier((part, kept))
             running = lax.ppermute(part, "seq", onward)
         held = following
     second_grad = (own_part + running.astype(f32)).astype(bf16)
-    moe_all, tokens, hidden, gate_low, up_low, slot_grad = kept
-
-    gate_term = jnp.einsum("td,etf->edf", tokens, gate_low, preferred_element_type=f32)
-    up_term = jnp.einsum("td,etf->edf", tokens, up_low, preferred_element_type=f32)
-    down_term = jnp.einsum("etf,etd->efd", hidden, slot_grad, preferred_element_type=f32)
-    gate_term, up_term, down_low, second_grad = lax.optimization_barrier(
-        (gate_term.astype(bf16), up_term.astype(bf16), down_term.astype(bf16), second_grad)
-    )
-    cut = local_experts // 2
-    sums = [
-        (gate_term.reshape(-1, gate_term.shape[-1]), dp_bits),
-        (up_term.reshape(-1, up_term.shape[-1]), dp_bits[::-1]),
-        (down_low[:cut].reshape(-1, features), dp_bits),
-        (down_low[cut:].reshape(-1, features), dp_bits[::-1]),
-    ]
-    pieces = [half_sum(values, "dp", bits[0]) for values, bits in sums]
+    tokens, hidden_a, hidden_b, gate_low, up_low, slot_a, slot_b = kept
+
+    def weight_parts(at, tokens, hidden_a, hidden_b, gate_low, up_low, slot_a, slot_b):
+        pairs = (
+            (tokens, gate_low[at]),
+            (tokens, up_low[at]),
+            (hidden_a[at], slot_a[at]),
+            (hidden_b[at], slot_b[at]),
+        )
+        return [
+            lax.dot_general(a, b, TN, preferred_element_type=f32).astype(bf16) for a, b in pairs
+        ]
+
+    leaving = weight_parts(0, *kept)
+    leaving, second_grad = lax.optimization_barrier((leaving, second_grad))
+    part_bits = (dp_bits[0], dp_bits[-1], dp_bits[0], dp_bits[-1])
+    came = [swap(values, "dp", bit) for values, bit in zip(leaving, part_bits)]
 
     mg_send, proj, middle_grad, gain_two_part = turn_call(
         second_grad, middle, gain_two, cot, output_weight, groups
     )
     mg = spread(mg_send)
+    mixed, kept, proj, _ = lax.optimization_barrier((mixed, kept, proj, mg_send))
+    staying = weight_parts(1, *kept)
+    moe_place = jnp.concatenate(places + [(1 - first_bit).astype(jnp.int32).reshape(1)])
+    moe_all = moe_call(moe_place, kept[1], routed, down_weight, devices)
     dense = output_weight_call(mixed, proj, gain_two_part, devices)
-    mg, dense, moe_all, *pieces = lax.optimization_barrier((mg, dense, moe_all, *pieces))
+    mg, dense, moe_all, came, staying = lax.optimization_barrier(
+        (mg, dense, moe_all, came, staying)
+    )
+    summed = [
+        (a.astype(f32) + b.astype(f32)).astype(bf16).reshape(replicas // 2, -1, b.shape[-1])
+        for a, b in zip(came, staying)
+    ]
+    streams = [
+        jnp.concatenate([summed[0], summed[2]], axis=1),
+        jnp.concatenate([summed[1], summed[3]], axis=1),
+    ]
+    stream_bits = (dp_bits, dp_bits[::-1])
     for at in range(1, len(dp_bits)):
-        pieces = [half_sum(p, "dp", bits[at]) for p, (_, bits) in zip(pieces, sums)]
+        streams = [half_sum(v, "dp", bits[at]) for v, bits in zip(streams, stream_bits)]
     dense = lax.psum_scatter(dense, "seq", scatter_dimension=0)
+    moe_all, _ = lax.optimization_barrier((moe_all, mg))
     moe = lax.psum_scatter(moe_all, "seq", scatter_dimension=0)
     layer_output = (middle + residual_scale * moe.astype(f32)).astype(bf16)
-    for bit in dp_bits:
-        dense = (dense.astype(f32) + swap(dense, "dp", bit).astype(f32)).astype(bf16)
-    dense = lax.all_gather(dense, "seq", axis=0).astype(f32)
-    each = output_weight.shape[0] // devices
-    output_weight_grad = dense[:, :each].reshape(output_weight.shape)
-    second_gain_grad = dense[0, each]
-
     table_shape = (devices, micro, per_device, pair)
     dqkv = attend_back_call(
         qkv,
@@ -650,23 +820,85 @@
         cos_all.reshape(table_shape),
         sin_all.reshape(table_shape),
     )
-    dqkv, *pieces = lax.optimization_barrier((dqkv, *pieces))
-    for at in range(len(dp_bits))[::-1]:
-        pieces = [join_halves(p, "dp", bits[at]) for p, (_, bits) in zip(pieces, sums)]
-    gate_sum, up_sum = pieces[0].reshape(gate_term.shape), pieces[1].reshape(up_term.shape)
-    down_sum = jnp.concatenate(pieces[2:], axis=0).reshape(down_low.shape)
+    dqkv, streams = lax.optimization_barrier((dqkv, streams))
+    turned = sum(((dp_place >> i) & 1) << (len(dp_bits) - 1 - i) for i in range(len(dp_bits)))
+    part_at = jnp.stack([turned, dp_place]).astype(jnp.int32)
+    expert_parts = [
+        join_parts(v[0], "dp", bits[-1:]) for v, bits in zip(streams, stream_bits)
+    ]
     d_all = dqkv.reshape(devices * rows, 2 * pair)
     first_tokens = first_all.reshape(devices * rows, features)
     part = lax.dot_general(first_tokens, d_all, TN, preferred_element_type=f32).astype(bf16)
-    for bit in dp_bits[::-1]:
-        part = half_sum(part, "dp", bit)
-    wide = lax.all_gather(part, ("dp", "seq"), axis=0)
-    wide = wide.reshape(replicas, devices, features // replicas, 2 * pair)[:, ::copies]
-    query_weight_grad, key_weight_grad, value_weight_grad, first_gain_grad = weights_out_call(
-        wide, query_weight, key_weight, value_weight, gain_one
-    )
-
     back = unspread(dqkv.reshape(devices, rows, 2 * pair))
+    dense = dense.reshape(dense.shape[-2], features)
+    each = output_weight.shape[0] // devices
+    gain_row, dense = dense[each:], dense[:each]
+    for bit in dp_bits:
+        gain_row = (gain_row.astype(f32) + swap(gain_row, "dp", bit).astype(f32)).astype(bf16)
+    second_gain_grad = gain_row[0].astype(f32)
+    if copies == 1:
+        pieces_all = 2 * replicas
+        width = 2 * pair
+        per_block = pieces_all * width // features
+        dense = dense.reshape(per_block, each // per_block, features // width, width)
+        dense = jnp.transpose(dense, (2, 0, 1, 3)).reshape(pieces_all, each // per_block, width)
+        joint = jnp.concatenate([part.reshape(pieces_all, -1, width), dense], axis=1)
+        depth = joint.shape[1]
+        streams = []
+        for at, bits in enumerate(stream_bits):
+            stream = joint[at * replicas : (at + 1) * replicas].reshape(replicas * depth, width)
+            for bit in bits:
+                stream = half_sum(stream, "dp", bit)
+            streams.append(stream)
+        own = jnp.stack(streams)
+        backward = [(i, (i - 2) % devices) for i in range(devices)]
+        round_ring = {0: own}
+        for k in range(1, chips // 2 + 1):
+            round_ring[k] = lax.ppermute(round_ring[k - 1], "seq", onward)
+            if chips - k > k:
+                round_ring[chips - k] = lax.ppermute(
+                    round_ring[(chips - k + 1) % chips], "seq", backward
+                )
+        held = jnp.stack([round_ring[k] for k in range(chips)])
+        held, expert_parts = lax.optimization_barrier((held, expert_parts))
+        full = [join_parts(held[:, at], "dp", b[-1:]) for at, b in enumerate(stream_bits)]
+        full, expert_parts = lax.optimization_barrier((full, expert_parts))
+        full = [
+            join_parts(v, "dp", b[:-1]).reshape(-1, *held[:, 0].shape)
+            for v, b in zip(full, stream_bits)
+        ]
+        full, back = lax.optimization_barrier((jnp.stack(full), back))
+        other = swap(full, "seq", 1)
+        where_at = jnp.stack([turned, dp_place, chip, core]).astype(jnp.int32)
+        (
+            query_weight_grad,
+            key_weight_grad,
+            value_weight_grad,
+            first_gain_grad,
+            output_weight_grad,
+        ) = dense_out_call(
+            where_at, full, other, query_weight, key_weight, value_weight, gain_one, output_weight.shape
+        )
+    else:
+        for bit in dp_bits:
+            dense = (dense.astype(f32) + swap(dense, "dp", bit).astype(f32)).astype(bf16)
+        dense = lax.all_gather(dense, "seq", axis=0).astype(f32)
+        output_weight_grad = dense.reshape(output_weight.shape)
+        for bit in dp_bits[::-1]:
+            part = half_sum(part, "dp", bit)
+        wide = lax.all_gather(part, ("dp", "seq"), axis=0)
+        wide = wide.reshape(replicas, devices, features // replicas, 2 * pair)[:, ::copies]
+        query_weight_grad, key_weight_grad, value_weight_grad, first_gain_grad = weights_out_call(
+            wide, query_weight, key_weight, value_weight, gain_one
+        )
+
+    expert_parts = [
+        join_parts(v, "dp", bits[:-1]).reshape(-1, *v.shape[-2:])
+        for v, bits in zip(expert_parts, stream_bits)
+    ]
+    gate_sum, up_sum, down_sum = expert_out_call(
+        part_at, *expert_parts, gate_weight.shape, down_weight.shape
+    )
     input_grad = last_call(
         back, query_weight, key_weight, value_weight, x, gain_one, middle_grad
     )
@@ -679,9 +911,9 @@
         value_weight_grad,
         output_weight_grad,
         second_gain_grad,
-        gate_sum.astype(f32),
-        up_sum.astype(f32),
-        down_sum.astype(f32),
+        gate_sum,
+        up_sum,
+        down_sum,
     )
 
 

time: 509 us -> 488 us (0.959)
  waiting for transfers between devices: 208 us -> 184 us
  local copies, waits for them, and re-layouts: 39.7 us -> 21.6 us
  Pallas kernels: 95 us -> 112 us
  blocking collectives: 42.9 us -> 32.3 us
  matrix products: 21.7 us -> 31.6 us
  starting transfers between devices: 37.3 us -> 45.2 us
    all_gather x3 -> x1, waiting for transfers between devices: 106 us -> 31.6 us  [body(): x_all = lax.all_gather(x, 'seq', axis=0)]
    ppermute x28 -> x29, waiting for transfers between devices: 75.2 us -> 100 us  [swap(): lax.ppermute(values, axis, [(i, i ^ bit) for i in range(lax.axis_size(axi...]
    ppermute x0 -> x3, waiting for transfers between devices: none -> 23.9 us  [the longest x2 23.5 us: body(): round_ring[k] = lax.ppermute(round_ring[k - 1], 'seq', onward)]
    pallas_call x1 -> x3, Pallas kernels: 4.13 us -> 22.2 us  [the longest x1 10.3 us: dense_out_call(): pl.pallas_call(dense_out_kernel, grid_spec=pltpu.PrefetchScalarGridSpec(n...]
    unnamed x86 -> x90, local copies, waits for them, and re-layouts: 32.1 us -> 16.4 us
    all_to_all x1 -> x0, blocking collectives: 11.7 us -> none  [body(): lax.all_to_all(jnp.broadcast_to(positions.reshape(1, rows), (devices, row...]
    ppermute x3, waiting for transfers between devices: 21.5 us -> 11.3 us  [body(): running = lax.ppermute(part, 'seq', onward)]
    dot_general x3 -> x8, matrix products: 19.1 us -> 29 us  [weight_parts(): lax.dot_general(a, b, TN, preferred_element_type=f32).astype(bf16)]
  transfers between devices with their start and end apart: 42 -> 45, of which waited for: 21 -> 30; matrix products, arithmetic and copies ran while one was open for 14% -> 15% of each run, Pallas kernels for 19% -> 21%
where the time goes in v4:
time: 488 us; the launch traced here: 478 us
  waiting for transfers between devices  184 us (38%)
  Pallas kernels  112 us (23%)
  starting transfers between devices  45.2 us (9%)
  other arithmetic  37.3 us (8%)
  blocking collectives  32.3 us (7%)
  matrix products  31.6 us (6%)
  local copies, waits for them, and re-layouts  21.6 us (4%)
  between operations  14.6 us (3%)
    ppermute x29, waiting for transfers between devices, swap(): lax.ppermute(values, axis, [(i, i ^ bit) for i in range(lax.axis_size(axi...  100 us
    pallas_call x4, Pallas kernels, expert_call(): pl.pallas_call(expert_kernel, grid_spec=pltpu.PrefetchScalarGridSpec(num_...  46 us
    all_to_all x1, blocking collectives, unspread(): return lax.all_to_all(blocks, 'seq', 0, 0, tiled=True)[::copies]  32.3 us
    all_gather x1, waiting for transfers between devices, body(): x_all = lax.all_gather(x, 'seq', axis=0)  31.6 us
    dot_general x8, matrix products, weight_parts(): lax.dot_general(a, b, TN, preferred_element_type=f32).astype(bf16)  29 us
    ppermute x29, starting transfers between devices, swap(): lax.ppermute(values, axis, [(i, i ^ bit) for i in range(lax.axis_size(axi...  24.1 us
    ppermute x2, waiting for transfers between devices, body(): round_ring[k] = lax.ppermute(round_ring[k - 1], 'seq', onward)  23.5 us
    unnamed x90, local copies, waits for them, and re-layouts  16.4 us
  transfers between devices with their start and end apart: 45, of which 30 were waited for; matrix products, arithmetic and copies ran while one was open for 15% of the time, Pallas kernels for 21%

profile of v4, /device:TPU:0, one launch (start us, length us, event | category | flops | bytes accessed | tf_op | source)
XLA Modules:
  0.0 478.3 jit_solution(6146248381616290817)
XLA Ops:
  9.2 6.3 %all-to-all-start = ((s32[8,1,256]{2,1,0:T(1,128)}), s32[8,1,256]{2,1,0:T(1,128)S(1)}, u32[]{:S(2)}, u32[]{:S(2)}) async-start(s32[8,1,256]{2,1,0:T(1,128)} %broadcast_in_dim.24), calls=%async_computation | async-start | bytes 16384 | tf_op jit(solution)/shard_map/all_to_all | solution.py:710
  17.7 3.4 all-to-all-done
  21.1 3.7 fusion.77
  24.9 3.0 pad_maximum_fusion.7
  27.9 31.6 %all-gather.4.cloned.1.call-done.x_ref = bf16[8,256,1024]{2,1,0:T(8,128)(2,1)} async-done(((bf16[1,256,1024]{2,1,0:T(8,128)(2,1)}), bf16[8,256,1024]{2,1,0:T(8,128)(2,1)}) %all-gather.4.cloned.1.call-update) | async-done | bytes 4194320 | tf_op jit(solution)/shard_map/all_gather | solution.py:713
  59.5 9.9 %norm_qkv_rope.1 = (bf16[8,256,256]{2,1,0:T(8,128)(2,1)}, bf16[8,256,1024]{2,1,0:T(8,128)(2,1)}) custom-call(s32[1]{0:T(128)} %bitcast.place_ref, bf16[8,256,1024]{2,1,0:T(8,128)(2,1)} %all-gather.4.cloned.1.call-done.x_ref, f32[1,1024]{1,0:T(1,128)} %bitcast.208, f32[2048,128]{1,0:T(8,128)} %get-tuple-element.128.cos_ref, ...), custom_call_target="tpu_custom_call" | custom-call | flops 201326592 | bytes 1750000 | tf_op jit(solution)/shard_map/norm_qkv_rope/pallas_call | solution.py:91
  70.8 7.8 %attention_forward.1 = bf16[8,2,128,128]{3,2,1,0:T(8,128)(2,1)S(1)} custom-call(bf16[8,2,128,256]{3,2,1,0:T(8,128)(2,1)S(1)} %bitcast.204), custom_call_target="tpu_custom_call" | custom-call | flops 134217728 | bytes 196608 | tf_op jit(solution)/shard_map/attention_forward/pallas_call | solution.py:168
  78.6 32.3 %all_to_all.21.mix_ref = bf16[8,256,128]{2,1,0:T(8,128)(2,1)S(1)} all-to-all(bf16[8,256,128]{2,1,0:T(8,128)(2,1)S(1)} %bitcast.207), channel_id=1, replica_groups=mesh['dp'=4,'seq'=8] {'seq'}, dimensions={0} | all-to-all | bytes 1048576 | tf_op jit(solution)/shard_map/all_to_all | solution.py:704
  118.1 11.5 %experts.4 = (bf16[2,256,1024]{2,1,0:T(8,128)(2,1)S(1)}, bf16[2048,1024]{1,0:T(8,128)(2,1)}, bf16[2,2048,512]{2,1,0:T(8,128)(2,1)}, bf16[2,2048,512]{2,1,0:T(8,1...) custom-call(s32[4]{0:T(128)S(1)} %add_add_fusion.1.place_ref, ...), custom_call_target="tpu_custom_call" | custom-call | flops 671088640 | bytes 2500000 | tf_op jit(solution)/shard_map/experts/pallas_call | solution.py:307
  131.0 2.2 collective-permute-done.3.b_ref
  133.2 11.5 %experts.5 = (bf16[2,256,1024]{2,1,0:T(8,128)(2,1)S(1)}, bf16[2048,1024]{1,0:T(8,128)(2,1)}, bf16[2,2048,512]{2,1,0:T(8,128)(2,1)}, bf16[2,2048,512]{2,1,0:T(8,1...) custom-call(s32[4]{0:T(128)S(1)} %add_add_fusion.2.place_ref, ...), custom_call_target="tpu_custom_call", output_to_operand_aliasing={{1}: (8, {}), {2}: (9, {}), {3}: (10, {}), {4}: (11, {}), {... | custom-call | flops 671088640 | bytes 2500000 | tf_op jit(solution)/shard_map/experts/pallas_call | solution.py:307
  144.6 2.7 collective-permute-done.2.a_ref
  152.6 11.5 %experts.6 = (bf16[2,256,1024]{2,1,0:T(8,128)(2,1)S(1)}, bf16[2048,1024]{1,0:T(8,128)(2,1)}, bf16[2,2048,512]{2,1,0:T(8,128)(2,1)}, bf16[2,2048,512]{2,1,0:T(8,1...) custom-call(s32[4]{0:T(128)S(1)} %add_add_fusion.3.place_ref, ...), custom_call_target="tpu_custom_call", output_to_operand_aliasing={{1}: (8, {}), {2}: (9, {}), {3}: (10, {}), {4}: (11, {}), {... | custom-call | flops 671088640 | bytes 2500000 | tf_op jit(solution)/shard_map/experts/pallas_call | solution.py:307
  164.1 3.3 collective-permute-done.5.a_ref
  167.5 10.5 %collective-permute-done.8 = bf16[256,1024]{1,0:T(8,128)(2,1)S(1)} collective-permute-done((bf16[256,1024]{1,0:T(8,128)(2,1)}, bf16[256,1024]{1,0:T(8,128)(2,1)S(1)}, u32[]{:S(2)}, u32[]{:S(2)}) %collective-permute-start.8) | collective-permute-done | bytes 524320 | tf_op jit(solution)/shard_map/ppermute | solution.py:768
  181.3 11.5 %experts.7 = (bf16[2,256,1024]{2,1,0:T(8,128)(2,1)S(1)}, bf16[2048,1024]{1,0:T(8,128)(2,1)}, bf16[2,2048,512]{2,1,0:T(8,128)(2,1)}, bf16[2,2048,512]{2,1,0:T(8,1...) custom-call(s32[4]{0:T(128)S(1)} %add_add_fusion.place_ref, ...), custom_call_target="tpu_custom_call", output_to_operand_aliasing={{1}: (8, {}), {2}: (9, {}), {3}: (10, {}), {4}: (11, {}), {... | custom-call | flops 671088640 | bytes 2500000 | tf_op jit(solution)/shard_map/experts/pallas_call | solution.py:307
  197.3 6.3 %fusion.35 = bf16[1024,512]{1,0:T(8,128)(2,1)} fusion(bf16[2048,1024]{1,0:T(8,128)(2,1)} %get-tuple-element.197, bf16[2,2048,512]{2,1,0:T(8,128)(2,1)} %get-tuple-element.199), kind=kOutput, calls=%fused_computation.54 | convolution fusion | flops 2148007936 | bytes 7340032 | tf_op jit(solution)/shard_map/dot_general | solution.py:781
  203.7 3.4 fusion.32
  210.3 2.1 fusion.44
  217.8 5.3 %all-to-all-start.2 = ((bf16[8,256,128]{2,1,0:T(8,128)(2,1)}), bf16[8,256,128]{2,1,0:T(8,128)(2,1)}, u32[]{:S(2)}, u32[]{:S(2)}) async-start(bf16[8,256,128]{2,1,0:T(8,128)(2,1)} %get-tuple-element.186), calls=%async_computation.2 | async-start | bytes 1048576 | tf_op jit(solution)/shard_map/all_to_all | solution.py:701
  226.6 6.2 %fusion.41 = bf16[1024,512]{1,0:T(8,128)(2,1)} fusion(bf16[2048,1024]{1,0:T(8,128)(2,1)} %get-tuple-element.197, bf16[2,2048,512]{2,1,0:T(8,128)(2,1)} %get-tuple-element.199), kind=kOutput, calls=%fused_computation.56 | convolution fusion | flops 2148007936 | bytes 7340032 | tf_op jit(solution)/shard_map/dot_general | solution.py:781
  232.8 3.4 fusion.38
  237.9 2.1 fusion.54
  240.0 4.3 output_weight_part.1
  244.2 2.2 copy-done.2
  246.4 6.6 %expert_outputs.1 = bf16[8,256,1024]{2,1,0:T(8,128)(2,1)S(1)} custom-call(s32[9]{0:T(128)S(1)} %concatenate.25.place_ref, bf16[2,2048,512]{2,1,0:T(8,128)(2,1)S(1)} %copy-done.2, f32[2048,2]{1,0:T(8,128)S(1)} %bitcast.197, bf16[2,512,1024]{2,1,0:T(8,128)(2,1)S(1)} %copy-done.3), custom_call_target="tpu_custom_call" | custom-call | flops 536870912 | bytes 1375000 | tf_op jit(solution)/shard_map/expert_outputs/pallas_call | solution.py:401
  255.1 3.5 fusion.59
  258.6 2.1 collective-permute-done.16
  271.7 14.3 %attention_backward.1 = bf16[8,2,128,256]{3,2,1,0:T(8,128)(2,1)} custom-call(bf16[8,2,128,256]{3,2,1,0:T(8,128)(2,1)} %bitcast.203, bf16[8,2,128,128]{3,2,1,0:T(8,128)(2,1)} %bitcast.49.grad_ref, f32[8,2,128,128]{3,2,1,0:T(8,128)} %bitcast.217, f32[8,2,128,128]{3,2,1,0:T(8,128)} %bitcast.218), custom_call_target="tpu_custom_call" | custom-call | flops 335544320 | bytes 655360 | tf_op jit(solution)/shard_map/attention_backward/pallas_call | solution.py:217
  286.0 2.4 add_convert_fusion.2
  289.0 2.2 add_convert_fusion.3
  291.3 2.6 convolution_convert_fusion
  293.9 4.8 %reduce-scatter.5.cloned.1.call-done = bf16[1,144,1024]{2,1,0:T(8,128)(2,1)} async-done(((bf16[8,144,1024]{2,1,0:T(8,128)(2,1)}), bf16[1,144,1024]{2,1,0:T(8,128)(2,1)}) %reduce-scatter.5.cloned.1.call-update) | async-done | bytes 294928 | tf_op jit(solution)/shard_map/reduce_scatter | solution.py:812
  304.2 3.7 collective-permute-done.20
  309.4 14.3 %collective-permute-done.22 = bf16[384,256]{1,0:T(8,128)(2,1)S(1)} collective-permute-done((bf16[384,256]{1,0:T(8,128)(2,1)S(1)}, bf16[384,256]{1,0:T(8,128)(2,1)S(1)}, u32[]{:S(2)}, u32[]{:S(2)}) %collective-permute-start.22) | collective-permute-done | bytes 196640 | tf_op jit(solution)/shard_map/ppermute | solution.py:652
  325.3 3.2 collective-permute-done.23
  328.6 3.8 collective-permute-start.26
  332.4 10.2 %collective-permute-done.24 = bf16[2,192,256]{2,1,0:T(8,128)(2,1)S(1)} collective-permute-done((bf16[2,192,256]{2,1,0:T(8,128)(2,1)S(1)}, bf16[2,192,256]{2,1,0:T(8,128)(2,1)S(1)}, u32[]{:S(2)}, u32[]{:S(2)}) %collective-permute-start.24) | collective-permute-done | bytes 196640 | tf_op jit(solution)/shard_map/ppermute | solution.py:857
  345.5 13.4 %collective-permute-done.25 = bf16[2,192,256]{2,1,0:T(8,128)(2,1)S(1)} collective-permute-done((bf16[2,192,256]{2,1,0:T(8,128)(2,1)S(1)}, bf16[2,192,256]{2,1,0:T(8,128)(2,1)S(1)}, u32[]{:S(2)}, u32[]{:S(2)}) %collective-permute-start.25) | collective-permute-done | bytes 196640 | tf_op jit(solution)/shard_map/ppermute | solution.py:857
  360.6 4.5 all-to-all-start.3
  368.9 7.7 %collective-permute-done.29 = bf16[4,192,256]{2,1,0:T(8,128)(2,1)S(1)} collective-permute-done((bf16[4,192,256]{2,1,0:T(8,128)(2,1)S(1)}, bf16[4,192,256]{2,1,0:T(8,128)(2,1)S(1)}, u32[]{:S(2)}, u32[]{:S(2)}) %collective-permute-start.29) | collective-permute-done | bytes 393248 | tf_op jit(solution)/shard_map/ppermute | solution.py:652
  378.8 17.1 %collective-permute-done.31 = bf16[2,4,192,256]{3,2,1,0:T(8,128)(2,1)S(1)} collective-permute-done((bf16[2,4,192,256]{3,2,1,0:T(8,128)(2,1)S(1)}, bf16[2,4,192,256]{3,2,1,0:T(8,128)(2,1)S(1)}, u32[]{:S(2)}, u32[]{:S(2)}) %collective-permute-start.31) | collective-permute-done | bytes 786464 | tf_op jit(solution)/shard_map/ppermute | solution.py:652
  402.8 34.6 %collective-permute-done.34 = bf16[16,1024]{1,0:T(8,128)(2,1)S(1)} collective-permute-done((bf16[16,1024]{1,0:T(8,128)(2,1)S(1)}, bf16[16,1024]{1,0:T(8,128)(2,1)S(1)}, u32[]{:S(2)}, u32[]{:S(2)}) %collective-permute-start.34) | collective-permute-done | bytes 32800 | tf_op jit(solution)/shard_map/ppermute | solution.py:652
  438.8 3.2 collective-permute-done.35
  446.2 3.8 input_gradient.1
  453.6 5.3 %expert_weights_out.1 = (f32[2,1024,512]{2,1,0:T(8,128)}, f32[2,1024,512]{2,1,0:T(8,128)}, f32[2,512,1024]{2,1,0:T(8,128)}) custom-call(s32[2]{0:T(128)S(1)} %pad_add_fusion.1.at_ref, bf16[4,768,512]{2,1,0:T(8,128)(2,1)S(1)} %bitcast.199, bf16[4,768,512]{2,1,0:T(8,128)(2,1)S(1)} %bitcast.198), custom_call_target="tpu_custom_call" | custom-call | bytes 2500000 | tf_op jit(solution)/shard_map/expert_weights_out/pallas_call | solution.py:364
  458.9 2.4 fusion.71
  461.3 10.3 %dense_weights_out.1 = (f32[1024,1024]{1,0:T(8,128)}, f32[1024,512]{1,0:T(8,128)}, f32[1024,512]{1,0:T(8,128)}, f32[1,1024]{1,0:T(1,128)}, f32[8,2,64,1024]{3,2,1,0:T(8,128)}) custom-call(s32[4]{0:T(128)S(1)} %pad_add_fusion.at_ref, bf16[2,4,4,192,256]{4,3,2,1,0:T(8,128)(2,1)} %pad_maximum_fusion.own_ref, ...), custom_call_target="tpu_custom_call" | custom-call | flops 262144 | bytes 3000000 | tf_op jit(solution)/shard_map/dense_weights_out/pallas_call | solution.py:529
  (221 shorter events, 89.7 us)
Async XLA Ops:
  7.2 52.3 %all-gather.4.cloned.1.call-start = ((), (), s32[]{:S(2)}) async-start(), calls=%async_computation.6 | async-start | bytes 4718592 | tf_op jit(solution)/shard_map/all_gather | solution.py:713
  9.2 11.9 %all-to-all-start = ((s32[8,1,256]{2,1,0:T(1,128)}), s32[8,1,256]{2,1,0:T(1,128)S(1)}, u32[]{:S(2)}, u32[]{:S(2)}) async-start(s32[8,1,256]{2,1,0:T(1,128)} %broadcast_in_dim.24), calls=%async_computation | async-start | bytes 16384 | tf_op jit(solution)/shard_map/all_to_all | solution.py:710
  15.5 102.5 %all-gather.6.cloned.1.call-start = ((), (), s32[]{:S(2)}) async-start(), calls=%async_computation.9 | async-start | bytes 4718592 | tf_op jit(solution)/shard_map/all_gather | solution.py:727
  59.5 51.3 %copy-start.28 = (f32[1024]{0:T(1024)S(1)}, f32[1024]{0:T(1024)}, u32[]{:S(2)}) copy-start(f32[1024]{0:T(1024)} %param.20) | copy-start | bytes 12292
  114.3 2.3 collective-permute-start.1
  114.3 16.6 %collective-permute-start = (bf16[256,1024]{1,0:T(8,128)(2,1)}, bf16[256,1024]{1,0:T(8,128)(2,1)}, u32[]{:S(2)}, u32[]{:S(2)}) collective-permute-start(bf16[256,1024]{1,0:T(8,128)(2,1)} %get-tuple-element.132.a_ref), channel_id=1, source_target_pairs={{0,2},{1,3},{2,4},{3,5},{4,6},{5,7},{6,0},{7,1},{8,10},{9,11},{10,... | collective-permute-start | bytes 1572872 | tf_op jit(solution)/shard_map/ppermute | solution.py:746
  130.9 2.3 collective-permute-start.3
  130.9 16.4 %collective-permute-start.2 = (bf16[256,1024]{1,0:T(8,128)(2,1)}, bf16[256,1024]{1,0:T(8,128)(2,1)}, u32[]{:S(2)}, u32[]{:S(2)}) collective-permute-start(bf16[256,1024]{1,0:T(8,128)(2,1)} %collective-permute-done.a_ref), channel_id=1, source_target_pairs={{0,2},{1,3},{2,4},{3,5},{4,6},{5,7},{6,0},{7,1},{8,10},{9,11},{10,... | collective-permute-start | bytes 1572872 | tf_op jit(solution)/shard_map/ppermute | solution.py:746
  147.4 2.0 collective-permute-start.4
  150.4 2.3 collective-permute-start.6
  150.5 16.9 %collective-permute-start.5 = (bf16[256,1024]{1,0:T(8,128)(2,1)}, bf16[256,1024]{1,0:T(8,128)(2,1)}, u32[]{:S(2)}, u32[]{:S(2)}) collective-permute-start(bf16[256,1024]{1,0:T(8,128)(2,1)} %collective-permute-done.2.a_ref), channel_id=1, source_target_pairs={{0,2},{1,3},{2,4},{3,5},{4,6},{5,7},{6,0},{7,1},{8,10},{9,11},{10,... | collective-permute-start | bytes 1572872 | tf_op jit(solution)/shard_map/ppermute | solution.py:746
  150.6 27.4 %collective-permute-start.8 = (bf16[256,1024]{1,0:T(8,128)(2,1)}, bf16[256,1024]{1,0:T(8,128)(2,1)S(1)}, u32[]{:S(2)}, u32[]{:S(2)}) collective-permute-start(bf16[256,1024]{1,0:T(8,128)(2,1)} %fusion.70), channel_id=1, source_target_pairs={{0,2},{1,3},{2,4},{3,5},{4,6},{5,7},{6,0},{7,1},{8,10},{9,11},{10,... | collective-permute-start | bytes 1572872 | tf_op jit(solution)/shard_map/ppermute | solution.py:768
  167.4 10.5 %collective-permute-start.7 = (bf16[256,1024]{1,0:T(8,128)(2,1)S(1)}, bf16[256,1024]{1,0:T(8,128)(2,1)S(1)}, u32[]{:S(2)}, u32[]{:S(2)}) collective-permute-start(bf16[256,1024]{1,0:T(8,128)(2,1)S(1)} %slice_bitcast_fusion.2), channel_id=1, source_target_pairs={{0,1},{1,0},{2,3},{3,2},{4,5},{5,4},{6,7},{7,6},{8,9},{9,8},{10,11... | collective-permute-start | bytes 1572872 | tf_op jit(solution)/shard_map/ppermute | solution.py:652
  179.0 2.3 collective-permute-start.9
  179.1 16.7 %collective-permute-start.11 = (bf16[256,1024]{1,0:T(8,128)(2,1)}, bf16[256,1024]{1,0:T(8,128)(2,1)}, u32[]{:S(2)}, u32[]{:S(2)}) collective-permute-start(bf16[256,1024]{1,0:T(8,128)(2,1)} %fusion.69), channel_id=1, source_target_pairs={{0,2},{1,3},{2,4},{3,5},{4,6},{5,7},{6,0},{7,1},{8,10},{9,11},{10,... | collective-permute-start | bytes 1572872 | tf_op jit(solution)/shard_map/ppermute | solution.py:768
  193.8 2.0 collective-permute-start.10
  195.2 17.2 %collective-permute-start.12 = (bf16[256,1024]{1,0:T(8,128)(2,1)S(1)}, bf16[256,1024]{1,0:T(8,128)(2,1)S(1)}, u32[]{:S(2)}, u32[]{:S(2)}) collective-permute-start(bf16[256,1024]{1,0:T(8,128)(2,1)S(1)} %slice_bitcast_fusion), channel_id=1, source_target_pairs={{0,1},{1,0},{2,3},{3,2},{4,5},{5,4},{6,7},{7,6},{8,9},{9,8},{10,11... | collective-permute-start | bytes 1572872 | tf_op jit(solution)/shard_map/ppermute | solution.py:652
  197.3 15.8 %collective-permute-start.13 = (bf16[256,1024]{1,0:T(8,128)(2,1)S(1)}, bf16[256,1024]{1,0:T(8,128)(2,1)S(1)}, u32[]{:S(2)}, u32[]{:S(2)}) collective-permute-start(bf16[256,1024]{1,0:T(8,128)(2,1)S(1)} %fusion.67), channel_id=1, source_target_pairs={{0,2},{1,3},{2,4},{3,5},{4,6},{5,7},{6,0},{7,1},{8,10},{9,11},{10,... | collective-permute-start | bytes 1572872 | tf_op jit(solution)/shard_map/ppermute | solution.py:768
  217.8 44.2 %all-to-all-start.2 = ((bf16[8,256,128]{2,1,0:T(8,128)(2,1)}), bf16[8,256,128]{2,1,0:T(8,128)(2,1)}, u32[]{:S(2)}, u32[]{:S(2)}) async-start(bf16[8,256,128]{2,1,0:T(8,128)(2,1)} %get-tuple-element.186), calls=%async_computation.2 | async-start | bytes 1048576 | tf_op jit(solution)/shard_map/all_to_all | solution.py:701
  223.1 75.6 %reduce-scatter.5.cloned.1.call-start = ((), (), s32[]{:S(2)}) async-start(), calls=%async_computation.8 | async-start | bytes 2654208 | tf_op jit(solution)/shard_map/reduce_scatter | solution.py:812
  223.6 38.3 %collective-permute-start.14 = (bf16[1024,512]{1,0:T(8,128)(2,1)}, bf16[1024,512]{1,0:T(8,128)(2,1)}, u32[]{:S(2)}, u32[]{:S(2)}) collective-permute-start(bf16[1024,512]{1,0:T(8,128)(2,1)} %fusion.32), channel_id=1, source_target_pairs={{0,8},{8,0},{16,24},{24,16},{1,9},{9,1},{17,25},{25,17},{2,10},{10... | collective-permute-start | bytes 3145736 | tf_op jit(solution)/shard_map/ppermute | solution.py:652
  225.1 36.8 %collective-permute-start.15 = (bf16[1024,512]{1,0:T(8,128)(2,1)}, bf16[1024,512]{1,0:T(8,128)(2,1)}, u32[]{:S(2)}, u32[]{:S(2)}) collective-permute-start(bf16[1024,512]{1,0:T(8,128)(2,1)} %fusion.35), channel_id=1, source_target_pairs={{0,16},{8,24},{16,0},{24,8},{1,17},{9,25},{17,1},{25,9},{2,18},{10... | collective-permute-start | bytes 3145736 | tf_op jit(solution)/shard_map/ppermute | solution.py:652
  236.2 24.5 %collective-permute-start.16 = (bf16[512,512]{1,0:T(8,128)(2,1)}, bf16[512,512]{1,0:T(8,128)(2,1)}, u32[]{:S(2)}, u32[]{:S(2)}) collective-permute-start(bf16[512,512]{1,0:T(8,128)(2,1)} %fusion.44), channel_id=1, source_target_pairs={{0,8},{8,0},{16,24},{24,16},{1,9},{9,1},{17,25},{25,17},{2,10},{10... | collective-permute-start | bytes 1572872 | tf_op jit(solution)/shard_map/ppermute | solution.py:652
  237.1 24.8 %collective-permute-start.17 = (bf16[512,512]{1,0:T(8,128)(2,1)}, bf16[512,512]{1,0:T(8,128)(2,1)}, u32[]{:S(2)}, u32[]{:S(2)}) collective-permute-start(bf16[512,512]{1,0:T(8,128)(2,1)} %fusion.49), channel_id=1, source_target_pairs={{0,16},{8,24},{16,0},{24,8},{1,17},{9,25},{17,1},{25,9},{2,18},{10... | collective-permute-start | bytes 1572872 | tf_op jit(solution)/shard_map/ppermute | solution.py:652
  261.9 197.0 %reduce-scatter.3.cloned.1.call-start = ((), (), s32[]{:S(2)}) async-start(), calls=%async_computation.7 | async-start | bytes 4718592 | tf_op jit(solution)/shard_map/reduce_scatter | solution.py:814
  265.9 20.1 %collective-permute-start.19 = (bf16[1,768,512]{2,1,0:T(8,128)(2,1)}, bf16[1,768,512]{2,1,0:T(8,128)(2,1)}, u32[]{:S(2)}, u32[]{:S(2)}) collective-permute-start(bf16[1,768,512]{2,1,0:T(8,128)(2,1)} %fusion.72), channel_id=1, source_target_pairs={{0,8},{8,0},{16,24},{24,16},{1,9},{9,1},{17,25},{25,17},{2,10},{10... | collective-permute-start | bytes 2359304 | tf_op jit(solution)/shard_map/ppermute | solution.py:652
  270.2 18.9 %collective-permute-start.18 = (bf16[1,768,512]{2,1,0:T(8,128)(2,1)}, bf16[1,768,512]{2,1,0:T(8,128)(2,1)}, u32[]{:S(2)}, u32[]{:S(2)}) collective-permute-start(bf16[1,768,512]{2,1,0:T(8,128)(2,1)} %fusion.74), channel_id=1, source_target_pairs={{0,16},{8,24},{16,0},{24,8},{1,17},{9,25},{17,1},{25,9},{2,18},{10... | collective-permute-start | bytes 2359304 | tf_op jit(solution)/shard_map/ppermute | solution.py:652
  300.0 7.9 %collective-permute-start.20 = (bf16[384,256]{1,0:T(8,128)(2,1)S(1)}, bf16[384,256]{1,0:T(8,128)(2,1)S(1)}, u32[]{:S(2)}, u32[]{:S(2)}) collective-permute-start(bf16[384,256]{1,0:T(8,128)(2,1)S(1)} %constant_dynamic-slice_fusion.3), channel_id=1, source_target_pairs={{0,8},{8,0},{16,24},{24,16},{1,9},{9,1},{17,25},{25,17},{2,10},{10... | collective-permute-start | bytes 589832 | tf_op jit(solution)/shard_map/ppermute | solution.py:652
  301.3 41.3 %collective-permute-start.28 = (bf16[768,512]{1,0:T(8,128)(2,1)S(1)}, bf16[768,512]{1,0:T(8,128)(2,1)S(1)}, u32[]{:S(2)}, u32[]{:S(2)}) collective-permute-start(bf16[768,512]{1,0:T(8,128)(2,1)S(1)} %bitcast.233), channel_id=1, source_target_pairs={{0,8},{8,0},{16,24},{24,16},{1,9},{9,1},{17,25},{25,17},{2,10},{10... | collective-permute-start | bytes 2359304 | tf_op jit(solution)/shard_map/ppermute | solution.py:652
  302.1 41.8 %collective-permute-start.27 = (bf16[768,512]{1,0:T(8,128)(2,1)S(1)}, bf16[768,512]{1,0:T(8,128)(2,1)S(1)}, u32[]{:S(2)}, u32[]{:S(2)}) collective-permute-start(bf16[768,512]{1,0:T(8,128)(2,1)S(1)} %bitcast.234), channel_id=1, source_target_pairs={{0,16},{8,24},{16,0},{24,8},{1,17},{9,25},{17,1},{25,9},{2,18},{10... | collective-permute-start | bytes 2359304 | tf_op jit(solution)/shard_map/ppermute | solution.py:652
  303.5 20.2 %collective-permute-start.22 = (bf16[384,256]{1,0:T(8,128)(2,1)S(1)}, bf16[384,256]{1,0:T(8,128)(2,1)S(1)}, u32[]{:S(2)}, u32[]{:S(2)}) collective-permute-start(bf16[384,256]{1,0:T(8,128)(2,1)S(1)} %constant_dynamic-slice_fusion.1), channel_id=1, source_target_pairs={{0,16},{8,24},{16,0},{24,8},{1,17},{9,25},{17,1},{25,9},{2,18},{10... | collective-permute-start | bytes 589832 | tf_op jit(solution)/shard_map/ppermute | solution.py:652
  308.0 17.2 %collective-permute-start.21 = (bf16[192,256]{1,0:T(8,128)(2,1)S(1)}, bf16[192,256]{1,0:T(8,128)(2,1)S(1)}, u32[]{:S(2)}, u32[]{:S(2)}) collective-permute-start(bf16[192,256]{1,0:T(8,128)(2,1)S(1)} %constant_dynamic-slice_fusion.2), channel_id=1, source_target_pairs={{0,16},{8,24},{16,0},{24,8},{1,17},{9,25},{17,1},{25,9},{2,18},{10... | collective-permute-start | bytes 294920 | tf_op jit(solution)/shard_map/ppermute | solution.py:652
  323.8 4.7 collective-permute-start.23
  328.6 14.0 %collective-permute-start.24 = (bf16[2,192,256]{2,1,0:T(8,128)(2,1)S(1)}, bf16[2,192,256]{2,1,0:T(8,128)(2,1)S(1)}, u32[]{:S(2)}, u32[]{:S(2)}) collective-permute-start(bf16[2,192,256]{2,1,0:T(8,128)(2,1)S(1)} %get-tuple-element.299), channel_id=1, source_target_pairs={{0,2},{1,3},{2,4},{3,5},{4,6},{5,7},{6,0},{7,1},{8,10},{9,11},{10,... | collective-permute-start | bytes 589832 | tf_op jit(solution)/shard_map/ppermute | solution.py:857
  328.6 16.9 %collective-permute-start.26 = (bf16[2,192,256]{2,1,0:T(8,128)(2,1)S(1)}, bf16[2,192,256]{2,1,0:T(8,128)(2,1)S(1)}, u32[]{:S(2)}, u32[]{:S(2)}) collective-permute-start(bf16[2,192,256]{2,1,0:T(8,128)(2,1)S(1)} %get-tuple-element.299), channel_id=1, source_target_pairs={{0,6},{1,7},{2,0},{3,1},{4,2},{5,3},{6,4},{7,5},{8,14},{9,15},{10,... | collective-permute-start | bytes 589832 | tf_op jit(solution)/shard_map/ppermute | solution.py:859
  342.6 16.3 %collective-permute-start.25 = (bf16[2,192,256]{2,1,0:T(8,128)(2,1)S(1)}, bf16[2,192,256]{2,1,0:T(8,128)(2,1)S(1)}, u32[]{:S(2)}, u32[]{:S(2)}) collective-permute-start(bf16[2,192,256]{2,1,0:T(8,128)(2,1)S(1)} %collective-permute-done.24), channel_id=1, source_target_pairs={{0,2},{1,3},{2,4},{3,5},{4,6},{5,7},{6,0},{7,1},{8,10},{9,11},{10,... | collective-permute-start | bytes 589832 | tf_op jit(solution)/shard_map/ppermute | solution.py:857
  359.2 9.6 %collective-permute-start.30 = (bf16[4,192,256]{2,1,0:T(8,128)(2,1)S(1)}, bf16[4,192,256]{2,1,0:T(8,128)(2,1)S(1)}, u32[]{:S(2)}, u32[]{:S(2)}) collective-permute-start(bf16[4,192,256]{2,1,0:T(8,128)(2,1)S(1)} %get-tuple-element.294), channel_id=1, source_target_pairs={{0,8},{8,0},{16,24},{24,16},{1,9},{9,1},{17,25},{25,17},{2,10},{10... | collective-permute-start | bytes 1179656 | tf_op jit(solution)/shard_map/ppermute | solution.py:652
  360.6 37.9 %all-to-all-start.3 = ((bf16[8,256,256]{2,1,0:T(8,128)(2,1)}), bf16[8,256,256]{2,1,0:T(8,128)(2,1)}, u32[]{:S(2)}, u32[]{:S(2)}) async-start(bf16[8,256,256]{2,1,0:T(8,128)(2,1)} %bitcast.87), calls=%async_computation.5 | async-start | bytes 2097152 | tf_op jit(solution)/shard_map/all_to_all | solution.py:704
  365.0 11.5 %collective-permute-start.29 = (bf16[4,192,256]{2,1,0:T(8,128)(2,1)S(1)}, bf16[4,192,256]{2,1,0:T(8,128)(2,1)S(1)}, u32[]{:S(2)}, u32[]{:S(2)}) collective-permute-start(bf16[4,192,256]{2,1,0:T(8,128)(2,1)S(1)} %get-tuple-element.293), channel_id=1, source_target_pairs={{0,16},{8,24},{16,0},{24,8},{1,17},{9,25},{17,1},{25,9},{2,18},{10... | collective-permute-start | bytes 1179656 | tf_op jit(solution)/shard_map/ppermute | solution.py:652
  376.6 19.3 %collective-permute-start.31 = (bf16[2,4,192,256]{3,2,1,0:T(8,128)(2,1)S(1)}, bf16[2,4,192,256]{3,2,1,0:T(8,128)(2,1)S(1)}, u32[]{:S(2)}, u32[]{:S(2)}) collective-permute-start(bf16[2,4,192,256]{3,2,1,0:T(8,128)(2,1)S(1)} %pad_maximum_fusion.10), channel_id=1, source_target_pairs={{0,8},{8,0},{16,24},{24,16},{1,9},{9,1},{17,25},{25,17},{2,10},{10... | collective-permute-start | bytes 2359304 | tf_op jit(solution)/shard_map/ppermute | solution.py:652
  377.4 18.9 %collective-permute-start.32 = (bf16[2,4,192,256]{3,2,1,0:T(8,128)(2,1)S(1)}, bf16[2,4,192,256]{3,2,1,0:T(8,128)(2,1)S(1)}, u32[]{:S(2)}, u32[]{:S(2)}) collective-permute-start(bf16[2,4,192,256]{3,2,1,0:T(8,128)(2,1)S(1)} %pad_maximum_fusion.11), channel_id=1, source_target_pairs={{0,16},{8,24},{16,0},{24,8},{1,17},{9,25},{17,1},{25,9},{2,18},{10... | collective-permute-start | bytes 2359304 | tf_op jit(solution)/shard_map/ppermute | solution.py:652
  396.5 46.2 %copy-start.5 = (bf16[1024,1024]{1,0:T(8,128)(2,1)S(1)}, bf16[1024,1024]{1,0:T(8,128)(2,1)}, u32[]{:S(2)}) copy-start(bf16[1024,1024]{1,0:T(8,128)(2,1)} %wq_ref.5) | copy-start | bytes 6291460
  396.5 46.2 %copy-start.7 = (bf16[1024,512]{1,0:T(8,128)(2,1)S(1)}, bf16[1024,512]{1,0:T(8,128)(2,1)}, u32[]{:S(2)}) copy-start(bf16[1024,512]{1,0:T(8,128)(2,1)} %wk_ref.5) | copy-start | bytes 3145732
  398.5 62.8 %collective-permute-start.33 = (bf16[2,4,4,192,256]{4,3,2,1,0:T(8,128)(2,1)}, bf16[2,4,4,192,256]{4,3,2,1,0:T(8,128)(2,1)}, u32[]{:S(2)}, u32[]{:S(2)}) collective-permute-start(bf16[2,4,4,192,256]{4,3,2,1,0:T(8,128)(2,1)} %pad_maximum_fusion.own_ref), channel_id=1, source_target_pairs={{0,1},{1,0},{2,3},{3,2},{4,5},{5,4},{6,7},{7,6},{8,9},{9,8},{10,11... | collective-permute-start | bytes 9437192 | tf_op jit(solution)/shard_map/ppermute | solution.py:652
  398.5 51.6 %collective-permute-start.37 = (bf16[2,768,512]{2,1,0:T(8,128)(2,1)}, bf16[2,768,512]{2,1,0:T(8,128)(2,1)}, u32[]{:S(2)}, u32[]{:S(2)}) collective-permute-start(bf16[2,768,512]{2,1,0:T(8,128)(2,1)} %pad_maximum_fusion.4), channel_id=1, source_target_pairs={{0,16},{8,24},{16,0},{24,8},{1,17},{9,25},{17,1},{25,9},{2,18},{10... | collective-permute-start | bytes 4718600 | tf_op jit(solution)/shard_map/ppermute | solution.py:652
  399.9 52.0 %collective-permute-start.36 = (bf16[2,768,512]{2,1,0:T(8,128)(2,1)}, bf16[2,768,512]{2,1,0:T(8,128)(2,1)}, u32[]{:S(2)}, u32[]{:S(2)}) collective-permute-start(bf16[2,768,512]{2,1,0:T(8,128)(2,1)} %pad_maximum_fusion.3), channel_id=1, source_target_pairs={{0,8},{8,0},{16,24},{24,16},{1,9},{9,1},{17,25},{25,17},{2,10},{10... | collective-permute-start | bytes 4718600 | tf_op jit(solution)/shard_map/ppermute | solution.py:652
  402.2 35.1 %collective-permute-start.34 = (bf16[16,1024]{1,0:T(8,128)(2,1)S(1)}, bf16[16,1024]{1,0:T(8,128)(2,1)S(1)}, u32[]{:S(2)}, u32[]{:S(2)}) collective-permute-start(bf16[16,1024]{1,0:T(8,128)(2,1)S(1)} %slice_bitcast_fusion.8), channel_id=1, source_target_pairs={{0,8},{8,0},{16,24},{24,16},{1,9},{9,1},{17,25},{25,17},{2,10},{10... | collective-permute-start | bytes 98312 | tf_op jit(solution)/shard_map/ppermute | solution.py:652
  438.1 4.0 collective-permute-start.35
  (42 other events, 301.8 us)
Sparse Core Ops, SparseCore 0:
  9.6 49.8 all-gather.3
  61.1 56.9 all-gather.5
  262.1 36.5 reduce-scatter.4
  301.4 61.8 reduce-scatter.2
